TPU v7x, 1024 devices: a whole 8x8x8 slice. The times are simulated.
1024 devices in a mesh: replica: 32 (over y, x_hi, core), tensor: 32 (over z, x_lo).
Axes of the slice: x: 8 (x_hi: 2, x_lo: 4; x = x_hi * 4 + x_lo), y: 8, z: 8, core: 2. Of those that a mesh axis runs over, the one named last changes fastest.
Arguments:
- attn_out: bfloat16 [32, 768, 4096], P('replica', None, 'tensor'), may hold values from -6 to 6
- proj: bfloat16 [32, 4096, 2048], P('replica', 'tensor'), may hold values from -6 to 6
- momentum: bfloat16 [32, 4096, 2048], P('replica', 'tensor'), may hold values from -6 to 6
- target: bfloat16 [32, 768, 2048], P('replica'), may hold values from -6 to 6
- segment_ids: int32 [32, 768], P('replica'), may hold values from 0 to 95, never falling along the last dimension, each value on 1 to 192 neighbouring positions
- step: int32 [1], replicated, may hold values from 0 to 999
Outputs:
- projected: bfloat16 [32, 768, 2048], P('replica', 'tensor')
- attn_grad: bfloat16 [32, 768, 4096], P('replica', None, 'tensor')
- new_proj: bfloat16 [32, 4096, 2048], P('replica', 'tensor')
- new_moment: bfloat16 [32, 4096, 2048], P('replica', 'tensor')
All inputs are finite; a program needn't handle non-finite values.
Results may differ from a plain program's by a relative error of at most 0.0055.
Values may be sent and summed in bfloat16 or wider, within the bound.
No kernel may reach another device: no remote copies, remote signals or barrier semaphores. Data moves between devices by JAX's collectives and lax.ppermute only.
A program may use at most 64 MiB of HBM per device.

v0:
```python
from functools import partial

import jax
import jax.numpy as jnp
from jax import lax
from jax.sharding import PartitionSpec as P

SEGS = 96


BETA_MOM = 0.9
STEP_RATE = 0.1


def as_sent(x):
    return jax.tree.map(lambda a: a.astype(jnp.bfloat16) if a.dtype == jnp.float32 else a, x)


def passed_along(x, axis, by):
    size = lax.axis_size(axis)
    return lax.ppermute(x, axis, [(i, (i + by) % size) for i in range(size)])


def send_partner(stacked, offset):
    return jax.tree.map(
        lambda part, own: part.astype(own.dtype),
        passed_along(as_sent(stacked), "replica", offset),
        stacked,
    )


def on_device(attn_out, proj, momentum, target, segment_ids, step):
    heads_in = attn_out[0]
    weight = proj[0]
    moment_in = momentum[0]
    target_rows = target[0]
    seg_rows = segment_ids[0]
    tokens_here = heads_in.shape[0]
    head_rows = weight.shape[0]
    tensor_size = lax.axis_size("tensor")
    rows_each = tokens_here // tensor_size
    scaling = (head_rows * tensor_size) ** (-0.5)
    same_doc = (seg_rows[:, None] == seg_rows[None, :]).astype(jnp.float32)
    doc_sizes = jnp.sum(same_doc, axis=1)
    weights = tokens_here / (SEGS * doc_sizes)
    first_row = lax.axis_index("tensor") * rows_each
    own_sums = lax.psum_scatter(
        jnp.dot(heads_in, weight, preferred_element_type=jnp.float32) * scaling,
        "tensor",
        scatter_dimension=0,
        tiled=True,
    )
    own_weights = lax.dynamic_slice_in_dim(weights, first_row, rows_each, 0)
    own_targets = lax.dynamic_slice_in_dim(target_rows, first_row, rows_each, 0)
    grad_shard = ((own_sums - own_targets.astype(jnp.float32)) * own_weights[:, None]).astype(
        jnp.bfloat16
    )
    grad_block = lax.all_gather(grad_shard, "tensor", axis=0, tiled=True)
    weight_sum = jnp.dot(heads_in.T, grad_block, preferred_element_type=jnp.float32)
    back_block = jnp.dot(grad_block, weight.T, preferred_element_type=jnp.float32)
    attn_grad = back_block
    projected = own_sums.astype(jnp.bfloat16)
    attn_grad = (attn_grad * scaling).astype(jnp.bfloat16)
    moment = (BETA_MOM * moment_in.astype(jnp.float32) + weight_sum * scaling).astype(jnp.bfloat16)
    updated = (weight.astype(jnp.float32) - STEP_RATE * moment.astype(jnp.float32)).astype(
        jnp.bfloat16
    )
    stacked = jnp.stack((updated, moment))
    levels = lax.axis_size("replica").bit_length() - 1
    chosen = step[0] % levels
    branches = [partial(send_partner, offset=1 << bit_pos) for bit_pos in range(levels)]
    partner = lax.switch(chosen, branches, stacked)
    mixed = ((stacked.astype(jnp.float32) + partner.astype(jnp.float32)) * 0.5).astype(jnp.bfloat16)
    return (projected[None], attn_grad[None], mixed[0][None], mixed[1][None])


def solution(mesh):
    return jax.shard_map(
        on_device,
        mesh=mesh,
        in_specs=(
            P("replica", None, "tensor"),
            P("replica", "tensor", None),
            P("replica", "tensor", None),
            P("replica", None, None),
            P("replica", None),
            P(),
        ),
        out_specs=(
            P("replica", "tensor", None),
            P("replica", None, "tensor"),
            P("replica", "tensor", None),
            P("replica", "tensor", None),
        ),
        check_vma=False,
    )
```

profile of v0, /device:TPU:14, one launch (start us, length us, event | category | flops | bytes accessed | tf_op | source)
XLA Modules:
  0.0 426.5 jit_solution(3441167970009986341)
XLA Ops:
  7.2 0.0 copy-start
  7.2 0.0 reduce-scatter.2.cloned.1.call-start
  7.2 0.9 copy-done
  8.1 4.7 %convolution_multiply_fusion = f32[768,2048]{1,0:T(8,128)} fusion(bf16[1,128,2048]{2,1,0:T(8,128)(2,1)} %param.12, bf16[1,768,128]{2,1,0:T(8,128)(2,1)S(1)} %copy-done), kind=kOutput, calls=%fused_computation | convolution fusion | flops 404226048 | bytes 7012352 | tf_op jit(solution)/shard_map/dot_general | solution.py:48
  12.8 0.0 copy-start.3
  12.8 0.0 copy-start.1
  12.8 0.0 copy-start.2
  12.8 0.0 reduce-scatter.2.cloned.1.call-update
  12.8 0.0 all-gather.2.cloned.1.call-start
  12.9 0.6 copy-done.3
  13.5 0.4 convert_reduce_fusion
  13.9 0.1 dynamic_slice.7
  13.9 189.5 %reduce-scatter.2.cloned.1.call-done = f32[24,2048]{1,0:T(8,128)} async-done(((f32[768,2048]{1,0:T(8,128)}), f32[24,2048]{1,0:T(8,128)}) %reduce-scatter.2.cloned.1.call-update) | async-done | bytes 196624 | tf_op jit(solution)/shard_map/reduce_scatter | solution.py:47
  203.5 1.8 fusion.9
  205.3 0.0 all-gather.2.cloned.1.call-update
  206.0 0.0 copy-done.1
  206.0 0.3 copy.20
  206.2 0.0 copy-done.2
  206.3 0.3 copy.21
  206.5 168.8 %all-gather.2.cloned.1.call-done = bf16[768,2048]{1,0:T(8,128)(2,1)} async-done(((bf16[24,2048]{1,0:T(8,128)(2,1)}), bf16[768,2048]{1,0:T(8,128)(2,1)}) %all-gather.2.cloned.1.call-update) | async-done | bytes 3145744 | tf_op jit(solution)/shard_map/all_gather | solution.py:58
  375.3 2.9 fusion.2
  378.2 0.2 fusion.5
  378.4 0.1 pad_maximum_fusion
  378.5 1.3 copy.22
  379.8 32.2 %conditional.4 = (bf16[2,128,2048]{2,1,0:T(8,128)(2,1)}) conditional(s32[]{:T(128)} %clamp.3, bf16[2,128,2048]{2,1,0:T(8,128)(2,1)} %copy.22, bf16[2,128,2048]{2,1,0:T(8,128)(2,1)} %copy.22, bf16[2,128,2048]{2,1,0:T(8,128)(2,1)} %copy.22, bf16[2,128,2048]{2,1,0:T(8,128)(2,1)} %copy.22, ...), branch_computations={%region_2.3_spmd, %region_3.4_spmd, %region_4.5_spmd, %region_5.6_... | conditional | bytes 4194352
  379.8 4.6 %collective-permute-start.3 = (bf16[2,128,2048]{2,1,0:T(8,128)(2,1)}, bf16[2,128,2048]{2,1,0:T(8,128)(2,1)}, u32[]{:S(2)}, u32[]{:S(2)}) collective-permute-start(bf16[2,128,2048]{2,1,0:T(8,128)(2,1)} %param.3), channel_id=1, source_target_pairs={{0,256},{32,288},{64,320},{96,352},{128,384},{160,416},{192,448},{... | collective-permute-start | bytes 3145736 | tf_op jit(solution)/shard_map/cond/branch_3_fun/ppermute | solution.py:21
  384.4 27.6 %collective-permute-done.3 = bf16[2,128,2048]{2,1,0:T(8,128)(2,1)} collective-permute-done((bf16[2,128,2048]{2,1,0:T(8,128)(2,1)}, bf16[2,128,2048]{2,1,0:T(8,128)(2,1)}, u32[]{:S(2)}, u32[]{:S(2)}) %collective-permute-start.3) | collective-permute-done | bytes 1048608 | tf_op jit(solution)/shard_map/cond/branch_3_fun/ppermute | solution.py:21
  412.0 1.6 copy.27
  413.6 0.3 multiply_convert_fusion
  414.0 0.1 fusion.12
  414.0 1.0 copy.28
  415.1 1.0 copy.29
  416.1 3.6 fusion.4
  (2 shorter events, 0.0 us)
Async XLA Ops:
  7.2 0.9 copy-start
  7.2 196.3 %reduce-scatter.2.cloned.1.call-start = ((), (), s32[]{:S(2)}) async-start(), calls=%async_computation.1 | async-start | bytes 6488064 | tf_op jit(solution)/shard_map/reduce_scatter | solution.py:47
  12.8 0.7 copy-start.3
  12.8 193.2 %copy-start.1 = (bf16[1,128,2048]{2,1,0:T(8,128)(2,1)S(1)}, bf16[1,128,2048]{2,1,0:T(8,128)(2,1)}, u32[]{:S(2)}) copy-start(bf16[1,128,2048]{2,1,0:T(8,128)(2,1)} %param.12) | copy-start | bytes 1572868
  12.8 193.5 %copy-start.2 = (bf16[1,128,2048]{2,1,0:T(8,128)(2,1)S(1)}, bf16[1,128,2048]{2,1,0:T(8,128)(2,1)}, u32[]{:S(2)}) copy-start(bf16[1,128,2048]{2,1,0:T(8,128)(2,1)} %param.13) | copy-start | bytes 1572868
  12.8 362.5 %all-gather.2.cloned.1.call-start = ((), (), s32[]{:S(2)}) async-start(), calls=%async_computation.2 | async-start | bytes 3244032 | tf_op jit(solution)/shard_map/all_gather | solution.py:58
  379.8 32.2 %collective-permute-start.3 = (bf16[2,128,2048]{2,1,0:T(8,128)(2,1)}, bf16[2,128,2048]{2,1,0:T(8,128)(2,1)}, u32[]{:S(2)}, u32[]{:S(2)}) collective-permute-start(bf16[2,128,2048]{2,1,0:T(8,128)(2,1)} %param.3), channel_id=1, source_target_pairs={{0,256},{32,288},{64,320},{96,352},{128,384},{160,416},{192,448},{... | collective-permute-start | bytes 3145736 | tf_op jit(solution)/shard_map/cond/branch_3_fun/ppermute | solution.py:21
Sparse Core Ops, SparseCore 0:
  12.9 190.4 reduce-scatter.1
  206.7 168.5 all-gather.1
where the time goes:
time: 432 us; the launch traced here: 426 us
  waiting for transfers between devices  386 us (89%)
  between operations  14.8 us (3%)
  matrix products  11.2 us (3%)
  local copies, waits for them, and re-layouts  7.11 us (2%)
  starting transfers between devices  4.69 us (1%)
    reduce_scatter x1, waiting for transfers between devices, on_device(): lax.psum_scatter(jnp.dot(heads_in, weight, preferred_element_type=jnp.flo...  190 us
    all_gather x1, waiting for transfers between devices, on_device(): grad_block = lax.all_gather(grad_shard, 'tensor', axis=0, tiled=True)  169 us
    ppermute x1, waiting for transfers between devices, passed_along(): return lax.ppermute(x, axis, [(i, (i + by) % size) for i in range(size)])  27.6 us
  transfers between devices with their start and end apart: 3, of which 3 were waited for; matrix products, arithmetic and copies ran while one was open for 0% of the time, Pallas kernels for 0%

commit v1 on v0

v1 whole, which is shorter than its diff:
```python
from functools import partial

import jax
import jax.numpy as jnp
from jax import lax
from jax.experimental import pallas as pl
from jax.experimental.pallas import tpu as pltpu
from jax.sharding import PartitionSpec as P

SEGS = 96
BETA_MOM = 0.9
STEP_RATE = 0.1
NX = 4
COLS = 2


def vmem(count):
    return [pl.BlockSpec(memory_space=pltpu.VMEM)] * count


def shift_z(x, by):
    size = lax.axis_size("tensor")
    return lax.ppermute(x, "tensor", [(i, (i + by * NX) % size) for i in range(size)])


def swap_x(x, k):
    size = lax.axis_size("tensor")
    return lax.ppermute(x, "tensor", [(i, i ^ k) for i in range(size)])


def pass_replica(x, by):
    size = lax.axis_size("replica")
    return lax.ppermute(x, "replica", [(i, (i + by) % size) for i in range(size)])


def place_of(j, k, z, x, nz):
    return lax.rem(z + j, nz) * NX + (x ^ k)


def order_kernel(nz, place_ref, rows_ref, out_ref):
    for j in range(nz):
        for k in range(NX):
            out_ref[j * NX + k] = rows_ref[place_of(j, k, place_ref[0], place_ref[1], nz)]


def moment_kernel(scaling, nz, *refs):
    heads_ref, blocks, mom_ref, out_ref, held = refs[0], refs[1 : 1 + nz], refs[-3], refs[-2], refs[-1]
    rows = blocks[0].shape[0]
    for j in range(nz):
        held[j * rows : (j + 1) * rows, :] = blocks[j][...]
    total = lax.dot_general(
        heads_ref[...], held[...], (((0,), (0,)), ((), ())), preferred_element_type=jnp.float32
    )
    out_ref[...] = (BETA_MOM * mom_ref[...].astype(jnp.float32) + total * scaling).astype(jnp.bfloat16)


def moment_of(heads, blocks, mom, scaling):
    nz, (rows, cols) = len(blocks), blocks[0].shape
    tile = min(512, cols)
    deep = heads.shape[1]
    column = lambda n: pl.BlockSpec((n, tile), lambda i: (0, i))
    return pl.pallas_call(
        partial(moment_kernel, scaling, nz),
        grid=(cols // tile,),
        out_shape=jax.ShapeDtypeStruct((deep, cols), jnp.bfloat16),
        in_specs=[pl.BlockSpec(heads.shape, lambda i: (0, 0))] + [column(rows)] * nz + [column(deep)],
        out_specs=column(deep),
        scratch_shapes=[pltpu.VMEM((nz * rows, tile), jnp.bfloat16)],
        cost_estimate=pl.CostEstimate(
            flops=2 * heads.size * cols, bytes_accessed=2 * (nz * rows * cols + 2 * deep * cols), transcendentals=0
        ),
        name="moment",
    )(heads, *blocks, mom)


def back_kernel(scaling, nz, parts, place_ref, *refs):
    w_ref, out_ref = refs[-2], refs[-1]
    cols = w_ref.shape[1] // parts
    for j in range(nz):
        total = None
        for c in range(parts):
            term = lax.dot_general(
                refs[c * nz + j][...],
                w_ref[:, c * cols : (c + 1) * cols],
                (((1,), (1,)), ((), ())),
                preferred_element_type=jnp.float32,
            )
            total = term if total is None else total + term
        rows = out_ref.shape[1]
        for k in range(NX):
            out_ref[place_of(j, k, place_ref[0], place_ref[1], nz)] = (
                total[k * rows : (k + 1) * rows] * scaling
            ).astype(jnp.bfloat16)


def on_device(hop, heads_in, weight, moment_in, target_rows, seg_rows):
    tokens, deep = heads_in.shape
    width = weight.shape[1]
    size = lax.axis_size("tensor")
    nz, rows = size // NX, tokens // size
    scaling = (deep * size) ** (-0.5)
    own = lax.axis_index("tensor")
    place = jnp.stack([own // NX, own % NX]).astype(jnp.int32)
    smem = pl.BlockSpec(memory_space=pltpu.SMEM)

    with jax.named_scope("early_partner"):
        partner_w = pass_replica(weight, hop)
    with jax.named_scope("order"):
        heads = pl.pallas_call(
            partial(order_kernel, nz),
            out_shape=jax.ShapeDtypeStruct((size, rows, deep), jnp.bfloat16),
            in_specs=[smem] + vmem(1),
            out_specs=vmem(1)[0],
            name="order",
        )(place, heads_in.reshape(size, rows, deep)).reshape(tokens, deep)
    first_row = own * rows
    own_seg = lax.dynamic_slice_in_dim(seg_rows, first_row, rows, 0)
    doc_sizes = jnp.sum((own_seg[:, None] == seg_rows[None, :]).astype(jnp.float32), axis=1)
    own_weights = (tokens / (SEGS * doc_sizes))[:, None]
    own_targets = lax.dynamic_slice_in_dim(target_rows, first_row, rows, 0).astype(jnp.float32)

    cols = width // COLS
    chunk = rows * NX
    sums, grads, blocks = [], [], []
    for c in range(COLS):
        part = slice(c * cols, (c + 1) * cols)
        up_steps, down_steps = (nz // 2, nz // 2 - 1) if c % 2 == 0 else (nz // 2 - 1, nz // 2)

        def share(j):
            j = j % nz
            return scaling * jnp.dot(
                heads[j * chunk : (j + 1) * chunk], weight[:, part], preferred_element_type=jnp.float32
            )

        with jax.named_scope("sum_z"):
            total = share(0)
            flows = [[1, up_steps, None], [-1, down_steps, None]]
            for s in range(nz // 2):
                for flow in flows:
                    way, steps, cur = flow
                    if s < steps:
                        term = share(way * (steps - s))
                        if cur is not None:
                            term = term + cur.astype(jnp.float32)
                        flow[2] = shift_z(term.astype(jnp.bfloat16), way)
            total = total + flows[0][2].astype(jnp.float32) + flows[1][2].astype(jnp.float32)
        with jax.named_scope("sum_x"):
            mine = total[:rows]
            for k in range(1, NX):
                sent = swap_x(total[k * rows : (k + 1) * rows].astype(jnp.bfloat16), k)
                mine = mine + sent.astype(jnp.float32)
        sums.append(mine.astype(jnp.bfloat16))
        grad = ((mine - own_targets[:, part]) * own_weights).astype(jnp.bfloat16)
        with jax.named_scope("gather_x"):
            block = jnp.concatenate([grad] + [swap_x(grad, k) for k in range(1, NX)], axis=0)
        with jax.named_scope("gather_z"):
            held = [block] + [None] * (nz - 1)
            flows = [[1, up_steps, block], [-1, down_steps, block]]
            for s in range(nz // 2):
                for flow in flows:
                    way, steps, cur = flow
                    if s < steps:
                        flow[2] = shift_z(cur, way)
                        held[(-way * (s + 1)) % nz] = flow[2]
        blocks.append(held)

    new_w, new_m = [], []
    for c in range(COLS):
        part = slice(c * cols, (c + 1) * cols)
        moment = moment_of(heads, blocks[c], moment_in[:, part], scaling)
        with jax.named_scope("partner"):
            partner_m = pass_replica(moment, hop).astype(jnp.float32)
        moment = moment.astype(jnp.float32)
        updated = (weight[:, part].astype(jnp.float32) - STEP_RATE * moment).astype(jnp.bfloat16)
        partner_u = (partner_w[:, part].astype(jnp.float32) - STEP_RATE * partner_m).astype(jnp.bfloat16)
        new_w.append(((updated.astype(jnp.float32) + partner_u.astype(jnp.float32)) * 0.5).astype(jnp.bfloat16))
        new_m.append(((moment + partner_m) * 0.5).astype(jnp.bfloat16))
    with jax.named_scope("back"):
        attn_grad = pl.pallas_call(
            partial(back_kernel, scaling, nz, COLS),
            out_shape=jax.ShapeDtypeStruct((size, rows, deep), jnp.bfloat16),
            in_specs=[smem] + vmem(nz * COLS + 1),
            out_specs=vmem(1)[0],
            cost_estimate=pl.CostEstimate(
                flops=2 * tokens * width * deep, bytes_accessed=2 * tokens * width, transcendentals=0
            ),
            name="back",
        )(place, *[b for held in blocks for b in held], weight).reshape(tokens, deep)
    join = lambda pieces: jnp.concatenate(pieces, axis=1)
    return join(sums), attn_grad, join(new_w), join(new_m)


def program(attn_out, proj, momentum, target, segment_ids, step):
    levels = lax.axis_size("replica").bit_length() - 1
    branches = [partial(on_device, 1 << bit) for bit in range(levels)]
    outs = lax.switch(
        step[0] % levels, branches, attn_out[0], proj[0], momentum[0], target[0], segment_ids[0]
    )
    return tuple(out[None] for out in outs)


def solution(mesh):
    return jax.shard_map(
        program,
        mesh=mesh,
        in_specs=(
            P("replica", None, "tensor"),
            P("replica", "tensor", None),
            P("replica", "tensor", None),
            P("replica", None, None),
            P("replica", None),
            P(),
        ),
        out_specs=(
            P("replica", "tensor", None),
            P("replica", None, "tensor"),
            P("replica", "tensor", None),
            P("replica", "tensor", None),
        ),
        check_vma=False,
    )
```

time: 432 us -> 216 us (0.50)
  the two profiles are of different devices: /device:TPU:14 before, /device:TPU:2 now
where the time goes in v1:
time: 216 us; the launch traced here: 214 us
  starting transfers between devices  162 us (75%)
  matrix products  15.2 us (7%)
  waiting for transfers between devices  12.8 us (6%)
  Pallas kernels  11.4 us (5%)
  other arithmetic  7 us (3%)
  local copies, waits for them, and re-layouts  3.14 us (1%)
    ppermute x28, starting transfers between devices, shift_z(): lax.ppermute(x, 'tensor', [(i, (i + by * NX) % size) for i in range(size)])  105 us
    ppermute x12, starting transfers between devices, swap_x(): return lax.ppermute(x, 'tensor', [(i, i ^ k) for i in range(size)])  40.9 us
    ppermute x3, starting transfers between devices, pass_replica(): lax.ppermute(x, 'replica', [(i, (i + by) % size) for i in range(size)])  16.1 us
    dot_general x16, matrix products, share(): jnp.dot(heads[j * chunk:(j + 1) * chunk], weight[:, part], preferred_elem...  15.2 us
    ppermute x3, waiting for transfers between devices, pass_replica(): lax.ppermute(x, 'replica', [(i, (i + by) % size) for i in range(size)])  6.6 us
    pallas_call x2, Pallas kernels, moment_of(): pl.pallas_call(partial(moment_kernel, scaling, nz), grid=(cols // tile,),...  5.63 us
  transfers between devices with their start and end apart: 43, of which 5 were waited for; matrix products, arithmetic and copies ran while one was open for 8% of the time, Pallas kernels for 5%

profile of v1, /device:TPU:2, one launch (start us, length us, event | category | flops | bytes accessed | tf_op | source)
XLA Modules:
  0.0 214.1 jit_solution(4357983009684324097)
XLA Ops:
  1.3 212.8 %conditional.1 = (bf16[1,24,2048]{2,1,0:T(8,128)(2,1)}, bf16[1,768,128]{2,1,0:T(8,128)(2,1)}, bf16[1,128,2048]{2,1,0:T(8,128)(2,1)}, bf16[1,128,2048]{2,1,0:T(8,128)(2,1)}) conditional(s32[]{:T(128)} %clamp.3, (bf16[1,768,128]{2,1,0:T(8,128)(2,1)}, bf16[1,128,2048]{2,1,0:T(8,128)(2,1)}, ...), branch_computations={%region_0.2_spmd, %region_2.4_spmd, %region_4.6_spmd, %region_6.8_... | conditional | flops 1223038976 | bytes 82600168 | solution.py:196
  1.9 1.7 order.6
  4.5 1.8 fusion.44
  6.4 5.2 %collective-permute-start.53 = (bf16[96,1024]{1,0:T(8,128)(2,1)}, bf16[96,1024]{1,0:T(8,128)(2,1)}, u32[]{:S(2)}, u32[]{:S(2)}) collective-permute-start(bf16[96,1024]{1,0:T(8,128)(2,1)} %fusion.44), channel_id=1, source_target_pairs={{0,4},{1,5},{2,6},{3,7},{4,8},{5,9},{6,10},{7,11},{8,12},{9,13},{1... | collective-permute-start | bytes 589832 | tf_op jit(solution)/shard_map/cond/branch_1_fun/sum_z/ppermute | solution.py:23
  11.5 1.8 fusion.42
  13.4 5.2 %collective-permute-start.43 = (bf16[96,1024]{1,0:T(8,128)(2,1)}, bf16[96,1024]{1,0:T(8,128)(2,1)}, u32[]{:S(2)}, u32[]{:S(2)}) collective-permute-start(bf16[96,1024]{1,0:T(8,128)(2,1)} %fusion.42), channel_id=1, source_target_pairs={{0,4},{1,5},{2,6},{3,7},{4,8},{5,9},{6,10},{7,11},{8,12},{9,13},{1... | collective-permute-start | bytes 589832 | tf_op jit(solution)/shard_map/cond/branch_1_fun/sum_z/ppermute | solution.py:23
  18.6 1.8 fusion.45
  20.4 10.8 %collective-permute-start.56 = (bf16[96,1024]{1,0:T(8,128)(2,1)}, bf16[96,1024]{1,0:T(8,128)(2,1)}, u32[]{:S(2)}, u32[]{:S(2)}) collective-permute-start(bf16[96,1024]{1,0:T(8,128)(2,1)} %fusion.45), channel_id=1, source_target_pairs={{0,28},{1,29},{2,30},{3,31},{4,0},{5,1},{6,2},{7,3},{8,4},{9,5},{1... | collective-permute-start | bytes 589832 | tf_op jit(solution)/shard_map/cond/branch_1_fun/sum_z/ppermute | solution.py:23
  31.2 1.8 fusion.43
  33.0 3.9 %collective-permute-start.47 = (bf16[96,1024]{1,0:T(8,128)(2,1)}, bf16[96,1024]{1,0:T(8,128)(2,1)}, u32[]{:S(2)}, u32[]{:S(2)}) collective-permute-start(bf16[96,1024]{1,0:T(8,128)(2,1)} %fusion.43), channel_id=1, source_target_pairs={{0,28},{1,29},{2,30},{3,31},{4,0},{5,1},{6,2},{7,3},{8,4},{9,5},{1... | collective-permute-start | bytes 589832 | tf_op jit(solution)/shard_map/cond/branch_1_fun/sum_z/ppermute | solution.py:23
  36.9 1.1 convolution_multiply_fusion.19
  41.5 1.1 add_convert_fusion.14
  42.7 1.9 collective-permute-start.54
  44.6 1.1 add_convert_fusion.19
  45.7 2.1 collective-permute-start.44
  47.8 1.1 add_convert_fusion.12
  48.9 5.1 %collective-permute-start.57 = (bf16[96,1024]{1,0:T(8,128)(2,1)S(1)}, bf16[96,1024]{1,0:T(8,128)(2,1)S(1)}, u32[]{:S(2)}, u32[]{:S(2)}) collective-permute-start(bf16[96,1024]{1,0:T(8,128)(2,1)S(1)} %add_convert_fusion.12), channel_id=1, source_target_pairs={{0,28},{1,29},{2,30},{3,31},{4,0},{5,1},{6,2},{7,3},{8,4},{9,5},{1... | collective-permute-start | bytes 589832 | tf_op jit(solution)/shard_map/cond/branch_1_fun/sum_z/ppermute | solution.py:23
  54.1 1.1 add_convert_fusion.16
  55.2 3.9 %collective-permute-start.48 = (bf16[96,1024]{1,0:T(8,128)(2,1)S(1)}, bf16[96,1024]{1,0:T(8,128)(2,1)S(1)}, u32[]{:S(2)}, u32[]{:S(2)}) collective-permute-start(bf16[96,1024]{1,0:T(8,128)(2,1)S(1)} %add_convert_fusion.16), channel_id=1, source_target_pairs={{0,28},{1,29},{2,30},{3,31},{4,0},{5,1},{6,2},{7,3},{8,4},{9,5},{1... | collective-permute-start | bytes 589832 | tf_op jit(solution)/shard_map/cond/branch_1_fun/sum_z/ppermute | solution.py:23
  59.2 3.7 %collective-permute-start.58 = (bf16[96,1024]{1,0:T(8,128)(2,1)S(1)}, bf16[96,1024]{1,0:T(8,128)(2,1)S(1)}, u32[]{:S(2)}, u32[]{:S(2)}) collective-permute-start(bf16[96,1024]{1,0:T(8,128)(2,1)S(1)} %add_convert_fusion.11), channel_id=1, source_target_pairs={{0,28},{1,29},{2,30},{3,31},{4,0},{5,1},{6,2},{7,3},{8,4},{9,5},{1... | collective-permute-start | bytes 589832 | tf_op jit(solution)/shard_map/cond/branch_1_fun/sum_z/ppermute | solution.py:23
  63.0 2.2 %collective-permute-start.45 = (bf16[96,1024]{1,0:T(8,128)(2,1)S(1)}, bf16[96,1024]{1,0:T(8,128)(2,1)S(1)}, u32[]{:S(2)}, u32[]{:S(2)}) collective-permute-start(bf16[96,1024]{1,0:T(8,128)(2,1)S(1)} %add_convert_fusion.18), channel_id=1, source_target_pairs={{0,4},{1,5},{2,6},{3,7},{4,8},{5,9},{6,10},{7,11},{8,12},{9,13},{1... | collective-permute-start | bytes 589832 | tf_op jit(solution)/shard_map/cond/branch_1_fun/sum_z/ppermute | solution.py:23
  65.2 4.9 %collective-permute-start.49 = (bf16[96,1024]{1,0:T(8,128)(2,1)S(1)}, bf16[96,1024]{1,0:T(8,128)(2,1)S(1)}, u32[]{:S(2)}, u32[]{:S(2)}) collective-permute-start(bf16[96,1024]{1,0:T(8,128)(2,1)S(1)} %add_convert_fusion.15), channel_id=1, source_target_pairs={{0,28},{1,29},{2,30},{3,31},{4,0},{5,1},{6,2},{7,3},{8,4},{9,5},{1... | collective-permute-start | bytes 589832 | tf_op jit(solution)/shard_map/cond/branch_1_fun/sum_z/ppermute | solution.py:23
  70.2 2.1 collective-permute-start.55
  72.3 5.1 %collective-permute-start.59 = (bf16[96,1024]{1,0:T(8,128)(2,1)S(1)}, bf16[96,1024]{1,0:T(8,128)(2,1)S(1)}, u32[]{:S(2)}, u32[]{:S(2)}) collective-permute-start(bf16[96,1024]{1,0:T(8,128)(2,1)S(1)} %add_convert_fusion.10), channel_id=1, source_target_pairs={{0,28},{1,29},{2,30},{3,31},{4,0},{5,1},{6,2},{7,3},{8,4},{9,5},{1... | collective-permute-start | bytes 589832 | tf_op jit(solution)/shard_map/cond/branch_1_fun/sum_z/ppermute | solution.py:23
  77.5 1.9 collective-permute-start.46
  79.5 1.2 collective-permute-done.59
  80.7 3.3 %collective-permute-start.60 = (bf16[24,1024]{1,0:T(8,128)(2,1)S(1)}, bf16[24,1024]{1,0:T(8,128)(2,1)S(1)}, u32[]{:S(2)}, u32[]{:S(2)}) collective-permute-start(bf16[24,1024]{1,0:T(8,128)(2,1)S(1)} %get-tuple-element.225), channel_id=1, source_target_pairs={{0,1},{1,0},{2,3},{3,2},{4,5},{5,4},{6,7},{7,6},{8,9},{9,8},{10,11... | collective-permute-start | bytes 147464 | tf_op jit(solution)/shard_map/cond/branch_1_fun/sum_x/ppermute | solution.py:28
  84.1 3.6 %collective-permute-start.62 = (bf16[24,1024]{1,0:T(8,128)(2,1)S(1)}, bf16[24,1024]{1,0:T(8,128)(2,1)S(1)}, u32[]{:S(2)}, u32[]{:S(2)}) collective-permute-start(bf16[24,1024]{1,0:T(8,128)(2,1)S(1)} %get-tuple-element.226), channel_id=1, source_target_pairs={{0,3},{1,2},{2,1},{3,0},{4,7},{5,6},{6,5},{7,4},{8,11},{9,10},{10,... | collective-permute-start | bytes 147464 | tf_op jit(solution)/shard_map/cond/branch_1_fun/sum_x/ppermute | solution.py:28
  87.7 3.3 %collective-permute-start.61 = (bf16[24,1024]{1,0:T(8,128)(2,1)S(1)}, bf16[24,1024]{1,0:T(8,128)(2,1)S(1)}, u32[]{:S(2)}, u32[]{:S(2)}) collective-permute-start(bf16[24,1024]{1,0:T(8,128)(2,1)S(1)} %get-tuple-element.227), channel_id=1, source_target_pairs={{0,2},{1,3},{2,0},{3,1},{4,6},{5,7},{6,4},{7,5},{8,10},{9,11},{10,... | collective-permute-start | bytes 147464 | tf_op jit(solution)/shard_map/cond/branch_1_fun/sum_x/ppermute | solution.py:28
  91.2 2.3 %collective-permute-start.50 = (bf16[24,1024]{1,0:T(8,128)(2,1)S(1)}, bf16[24,1024]{1,0:T(8,128)(2,1)S(1)}, u32[]{:S(2)}, u32[]{:S(2)}) collective-permute-start(bf16[24,1024]{1,0:T(8,128)(2,1)S(1)} %get-tuple-element.222), channel_id=1, source_target_pairs={{0,1},{1,0},{2,3},{3,2},{4,5},{5,4},{6,7},{7,6},{8,9},{9,8},{10,11... | collective-permute-start | bytes 147464 | tf_op jit(solution)/shard_map/cond/branch_1_fun/sum_x/ppermute | solution.py:28
  93.4 3.6 %collective-permute-start.52 = (bf16[24,1024]{1,0:T(8,128)(2,1)S(1)}, bf16[24,1024]{1,0:T(8,128)(2,1)S(1)}, u32[]{:S(2)}, u32[]{:S(2)}) collective-permute-start(bf16[24,1024]{1,0:T(8,128)(2,1)S(1)} %get-tuple-element.223), channel_id=1, source_target_pairs={{0,3},{1,2},{2,1},{3,0},{4,7},{5,6},{6,5},{7,4},{8,11},{9,10},{10,... | collective-permute-start | bytes 147464 | tf_op jit(solution)/shard_map/cond/branch_1_fun/sum_x/ppermute | solution.py:28
  97.1 4.2 %collective-permute-start.51 = (bf16[24,1024]{1,0:T(8,128)(2,1)S(1)}, bf16[24,1024]{1,0:T(8,128)(2,1)S(1)}, u32[]{:S(2)}, u32[]{:S(2)}) collective-permute-start(bf16[24,1024]{1,0:T(8,128)(2,1)S(1)} %get-tuple-element.224), channel_id=1, source_target_pairs={{0,2},{1,3},{2,0},{3,1},{4,6},{5,7},{6,4},{7,5},{8,10},{9,11},{10,... | collective-permute-start | bytes 147464 | tf_op jit(solution)/shard_map/cond/branch_1_fun/sum_x/ppermute | solution.py:28
  101.4 2.6 %collective-permute-done.51 = bf16[24,1024]{1,0:T(8,128)(2,1)S(1)} collective-permute-done((bf16[24,1024]{1,0:T(8,128)(2,1)S(1)}, bf16[24,1024]{1,0:T(8,128)(2,1)S(1)}, u32[]{:S(2)}, u32[]{:S(2)}) %collective-permute-start.51) | collective-permute-done | bytes 49184 | tf_op jit(solution)/shard_map/cond/branch_1_fun/sum_x/ppermute | solution.py:28
  104.7 2.8 %collective-permute-start.65 = (bf16[24,1024]{1,0:T(8,128)(2,1)S(1)}, bf16[24,1024]{1,0:T(8,128)(2,1)S(1)}, u32[]{:S(2)}, u32[]{:S(2)}) collective-permute-start(bf16[24,1024]{1,0:T(8,128)(2,1)S(1)} %get-tuple-element.221), channel_id=1, source_target_pairs={{0,3},{1,2},{2,1},{3,0},{4,7},{5,6},{6,5},{7,4},{8,11},{9,10},{10,... | collective-permute-start | bytes 147464 | tf_op jit(solution)/shard_map/cond/branch_1_fun/gather_x/ppermute | solution.py:28
  107.5 5.7 %collective-permute-start.64 = (bf16[24,1024]{1,0:T(8,128)(2,1)S(1)}, bf16[24,1024]{1,0:T(8,128)(2,1)S(1)}, u32[]{:S(2)}, u32[]{:S(2)}) collective-permute-start(bf16[24,1024]{1,0:T(8,128)(2,1)S(1)} %get-tuple-element.221), channel_id=1, source_target_pairs={{0,2},{1,3},{2,0},{3,1},{4,6},{5,7},{6,4},{7,5},{8,10},{9,11},{10,... | collective-permute-start | bytes 147464 | tf_op jit(solution)/shard_map/cond/branch_1_fun/gather_x/ppermute | solution.py:28
  113.2 1.9 collective-permute-start.63
  115.1 2.5 %collective-permute-start.75 = (bf16[24,1024]{1,0:T(8,128)(2,1)S(1)}, bf16[24,1024]{1,0:T(8,128)(2,1)S(1)}, u32[]{:S(2)}, u32[]{:S(2)}) collective-permute-start(bf16[24,1024]{1,0:T(8,128)(2,1)S(1)} %get-tuple-element.212), channel_id=1, source_target_pairs={{0,3},{1,2},{2,1},{3,0},{4,7},{5,6},{6,5},{7,4},{8,11},{9,10},{10,... | collective-permute-start | bytes 147464 | tf_op jit(solution)/shard_map/cond/branch_1_fun/gather_x/ppermute | solution.py:28
  117.6 5.7 %collective-permute-start.74 = (bf16[24,1024]{1,0:T(8,128)(2,1)S(1)}, bf16[24,1024]{1,0:T(8,128)(2,1)S(1)}, u32[]{:S(2)}, u32[]{:S(2)}) collective-permute-start(bf16[24,1024]{1,0:T(8,128)(2,1)S(1)} %get-tuple-element.212), channel_id=1, source_target_pairs={{0,2},{1,3},{2,0},{3,1},{4,6},{5,7},{6,4},{7,5},{8,10},{9,11},{10,... | collective-permute-start | bytes 147464 | tf_op jit(solution)/shard_map/cond/branch_1_fun/gather_x/ppermute | solution.py:28
  123.3 1.9 collective-permute-start.73
  125.3 2.5 %collective-permute-start.69 = (bf16[96,1024]{1,0:T(8,128)(2,1)S(1)}, bf16[96,1024]{1,0:T(8,128)(2,1)S(1)}, u32[]{:S(2)}, u32[]{:S(2)}) collective-permute-start(bf16[96,1024]{1,0:T(8,128)(2,1)S(1)} %pad_maximum_fusion.2.refs_0_.refs_1_), channel_id=1, source_target_pairs={{0,4},{1,5},{2,6},{3,7},{4,8},{5,9},{6,10},{7,11},{8,12},{9,13},{1... | collective-permute-start | bytes 589832 | tf_op jit(solution)/shard_map/cond/branch_1_fun/gather_z/ppermute | solution.py:23
  127.8 1.5 collective-permute-done.73
  129.3 6.1 %collective-permute-start.76 = (bf16[96,1024]{1,0:T(8,128)(2,1)S(1)}, bf16[96,1024]{1,0:T(8,128)(2,1)S(1)}, u32[]{:S(2)}, u32[]{:S(2)}) collective-permute-start(bf16[96,1024]{1,0:T(8,128)(2,1)S(1)} %pad_maximum_fusion.3.refs_8_.refs_1_), channel_id=1, source_target_pairs={{0,28},{1,29},{2,30},{3,31},{4,0},{5,1},{6,2},{7,3},{8,4},{9,5},{1... | collective-permute-start | bytes 589832 | tf_op jit(solution)/shard_map/cond/branch_1_fun/gather_z/ppermute | solution.py:23
  135.5 1.9 collective-permute-start.66
  137.4 3.9 %collective-permute-start.80 = (bf16[96,1024]{1,0:T(8,128)(2,1)S(1)}, bf16[96,1024]{1,0:T(8,128)(2,1)S(1)}, u32[]{:S(2)}, u32[]{:S(2)}) collective-permute-start(bf16[96,1024]{1,0:T(8,128)(2,1)S(1)} %pad_maximum_fusion.3.refs_8_.refs_1_), channel_id=1, source_target_pairs={{0,4},{1,5},{2,6},{3,7},{4,8},{5,9},{6,10},{7,11},{8,12},{9,13},{1... | collective-permute-start | bytes 589832 | tf_op jit(solution)/shard_map/cond/branch_1_fun/gather_z/ppermute | solution.py:23
  141.4 1.9 collective-permute-start.70
  143.3 5.1 %collective-permute-start.77 = (bf16[96,1024]{1,0:T(8,128)(2,1)S(1)}, bf16[96,1024]{1,0:T(8,128)(2,1)S(1)}, u32[]{:S(2)}, u32[]{:S(2)}) collective-permute-start(bf16[96,1024]{1,0:T(8,128)(2,1)S(1)} %collective-permute-done.76.refs_9_.refs_2_), channel_id=1, source_target_pairs={{0,28},{1,29},{2,30},{3,31},{4,0},{5,1},{6,2},{7,3},{8,4},{9,5},{1... | collective-permute-start | bytes 589832 | tf_op jit(solution)/shard_map/cond/branch_1_fun/gather_z/ppermute | solution.py:23
  148.5 1.9 collective-permute-start.67
  150.4 3.9 %collective-permute-start.81 = (bf16[96,1024]{1,0:T(8,128)(2,1)S(1)}, bf16[96,1024]{1,0:T(8,128)(2,1)S(1)}, u32[]{:S(2)}, u32[]{:S(2)}) collective-permute-start(bf16[96,1024]{1,0:T(8,128)(2,1)S(1)} %collective-permute-done.80.refs_15_.refs_8_), channel_id=1, source_target_pairs={{0,4},{1,5},{2,6},{3,7},{4,8},{5,9},{6,10},{7,11},{8,12},{9,13},{1... | collective-permute-start | bytes 589832 | tf_op jit(solution)/shard_map/cond/branch_1_fun/gather_z/ppermute | solution.py:23
  154.4 1.9 collective-permute-start.71
  156.3 5.1 %collective-permute-start.78 = (bf16[96,1024]{1,0:T(8,128)(2,1)S(1)}, bf16[96,1024]{1,0:T(8,128)(2,1)S(1)}, u32[]{:S(2)}, u32[]{:S(2)}) collective-permute-start(bf16[96,1024]{1,0:T(8,128)(2,1)S(1)} %collective-permute-done.77.refs_10_.refs_3_), channel_id=1, source_target_pairs={{0,28},{1,29},{2,30},{3,31},{4,0},{5,1},{6,2},{7,3},{8,4},{9,5},{1... | collective-permute-start | bytes 589832 | tf_op jit(solution)/shard_map/cond/branch_1_fun/gather_z/ppermute | solution.py:23
  161.5 5.1 %collective-permute-start.83 = (bf16[128,2048]{1,0:T(8,128)(2,1)S(1)}, bf16[128,2048]{1,0:T(8,128)(2,1)}, u32[]{:S(2)}, u32[]{:S(2)}) collective-permute-start(bf16[128,2048]{1,0:T(8,128)(2,1)S(1)} %bitcast.246), channel_id=1, source_target_pairs={{0,64},{32,96},{64,128},{96,160},{128,192},{160,224},{192,256},{22... | collective-permute-start | bytes 1572872 | tf_op jit(solution)/shard_map/cond/branch_1_fun/early_partner/ppermute | solution.py:33
  166.6 2.4 %collective-permute-start.68 = (bf16[96,1024]{1,0:T(8,128)(2,1)S(1)}, bf16[96,1024]{1,0:T(8,128)(2,1)S(1)}, u32[]{:S(2)}, u32[]{:S(2)}) collective-permute-start(bf16[96,1024]{1,0:T(8,128)(2,1)S(1)} %collective-permute-done.67.refs_2_.refs_3_), channel_id=1, source_target_pairs={{0,28},{1,29},{2,30},{3,31},{4,0},{5,1},{6,2},{7,3},{8,4},{9,5},{1... | collective-permute-start | bytes 589832 | tf_op jit(solution)/shard_map/cond/branch_1_fun/gather_z/ppermute | solution.py:23
  169.0 3.5 %collective-permute-start.82 = (bf16[96,1024]{1,0:T(8,128)(2,1)S(1)}, bf16[96,1024]{1,0:T(8,128)(2,1)S(1)}, u32[]{:S(2)}, u32[]{:S(2)}) collective-permute-start(bf16[96,1024]{1,0:T(8,128)(2,1)S(1)} %collective-permute-done.81.refs_14_.refs_7_), channel_id=1, source_target_pairs={{0,4},{1,5},{2,6},{3,7},{4,8},{5,9},{6,10},{7,11},{8,12},{9,13},{1... | collective-permute-start | bytes 589832 | tf_op jit(solution)/shard_map/cond/branch_1_fun/gather_z/ppermute | solution.py:23
  172.5 1.9 collective-permute-start.72
  174.4 5.1 %collective-permute-start.79 = (bf16[96,1024]{1,0:T(8,128)(2,1)S(1)}, bf16[96,1024]{1,0:T(8,128)(2,1)}, u32[]{:S(2)}, u32[]{:S(2)}) collective-permute-start(bf16[96,1024]{1,0:T(8,128)(2,1)S(1)} %collective-permute-done.78.refs_11_.refs_4_), channel_id=1, source_target_pairs={{0,28},{1,29},{2,30},{3,31},{4,0},{5,1},{6,2},{7,3},{8,4},{9,5},{1... | collective-permute-start | bytes 589832 | tf_op jit(solution)/shard_map/cond/branch_1_fun/gather_z/ppermute | solution.py:23
  181.9 2.8 %moment.12 = bf16[128,1024]{1,0:T(8,128)(2,1)} custom-call(bf16[768,128]{1,0:T(8,128)(2,1)} %bitcast.318, bf16[96,1024]{1,0:T(8,128)(2,1)} %copy-done.11, bf16[96,1024]{1,0:T(8,128)(2,1)} %copy-done.46, bf16[96,1024]{1,0:T(8,128)(2,1)} %copy-done.66, bf16[96,1024]{1,0:T(8,128)(2,1)} %copy-done.86, bf16[96,1024]{1,0:T(8,128)(2,1)} %copy-done.96, ...), custom_call_target="tpu_custom_call" | custom-call | flops 201326592 | bytes 2097152 | tf_op jit(solution)/shard_map/cond/branch_1_fun/moment/pallas_call | solution.py:62
  184.7 5.8 %collective-permute-start.84 = (bf16[128,1024]{1,0:T(8,128)(2,1)}, bf16[128,1024]{1,0:T(8,128)(2,1)}, u32[]{:S(2)}, u32[]{:S(2)}) collective-permute-start(bf16[128,1024]{1,0:T(8,128)(2,1)} %moment.12), channel_id=1, source_target_pairs={{0,64},{32,96},{64,128},{96,160},{128,192},{160,224},{192,256},{22... | collective-permute-start | bytes 786440 | tf_op jit(solution)/shard_map/cond/branch_1_fun/partner/ppermute | solution.py:33
  191.2 2.8 %moment.13 = bf16[128,1024]{1,0:T(8,128)(2,1)} custom-call(bf16[768,128]{1,0:T(8,128)(2,1)} %bitcast.319, bf16[96,1024]{1,0:T(8,128)(2,1)} %copy-done.16, bf16[96,1024]{1,0:T(8,128)(2,1)} %copy-done.41, bf16[96,1024]{1,0:T(8,128)(2,1)} %copy-done.61, bf16[96,1024]{1,0:T(8,128)(2,1)} %copy-done.81, bf16[96,1024]{1,0:T(8,128)(2,1)} %collective-permute-done.79.refs_12_.refs_5_, ...), custom_call_target="tpu_custom_call" | custom-call | flops 201326592 | bytes 2097152 | tf_op jit(solution)/shard_map/cond/branch_1_fun/moment/pallas_call | solution.py:62
  194.0 5.2 %collective-permute-start.85 = (bf16[128,1024]{1,0:T(8,128)(2,1)}, bf16[128,1024]{1,0:T(8,128)(2,1)S(1)}, u32[]{:S(2)}, u32[]{:S(2)}) collective-permute-start(bf16[128,1024]{1,0:T(8,128)(2,1)} %moment.13), channel_id=1, source_target_pairs={{0,64},{32,96},{64,128},{96,160},{128,192},{160,224},{192,256},{22... | collective-permute-start | bytes 786440 | tf_op jit(solution)/shard_map/cond/branch_1_fun/partner/ppermute | solution.py:33
  199.3 1.5 maximum_bitcast_fusion.5
  200.7 4.1 %back.6 = bf16[32,24,128]{2,1,0:T(8,128)(2,1)} custom-call(s32[2]{0:T(128)} %pad_add_fusion.1.place_ref, bf16[96,1024]{1,0:T(8,128)(2,1)} %copy-done.11, bf16[96,1024]{1,0:T(8,128)(2,1)} %copy-done.46, bf16[96,1024]{1,0:T(8,128)(2,1)} %copy-done.66, bf16[96,1024]{1,0:T(8,128)(2,1)} %copy-done.86, bf16[96,1024]{1,0:T(8,128)(2,1)} %copy-done.96, ...), custom_call_target="tpu_custom_call" | custom-call | flops 402653184 | bytes 3145728 | tf_op jit(solution)/shard_map/cond/branch_1_fun/back/back/pallas_call | solution.py:179
  204.8 6.6 %collective-permute-done.85 = bf16[128,1024]{1,0:T(8,128)(2,1)S(1)} collective-permute-done((bf16[128,1024]{1,0:T(8,128)(2,1)}, bf16[128,1024]{1,0:T(8,128)(2,1)S(1)}, u32[]{:S(2)}, u32[]{:S(2)}) %collective-permute-start.85) | collective-permute-done | bytes 262176 | tf_op jit(solution)/shard_map/cond/branch_1_fun/partner/ppermute | solution.py:33
  211.4 1.6 multiply_convert_fusion.3
  213.0 1.1 maximum_bitcast_fusion.3
  (109 shorter events, 9.1 us)
Async XLA Ops:
  1.3 36.8 %copy-start.1 = (bf16[1,128,2048]{2,1,0:T(8,128)(2,1)S(1)}, bf16[1,128,2048]{2,1,0:T(8,128)(2,1)}, u32[]{:S(2)}) copy-start(bf16[1,128,2048]{2,1,0:T(8,128)(2,1)} %get-tuple-element.148) | copy-start | bytes 1572868 | tf_op jit(solution)/shard_map/cond
  3.6 36.3 %copy-start.101 = (s32[1,768]{1,0:T(1,128)S(1)}, s32[1,768]{1,0:T(1,128)}, u32[]{:S(2)}) copy-start(s32[1,768]{1,0:T(1,128)} %get-tuple-element.74) | copy-start | bytes 9220 | tf_op jit(solution)/shard_map/cond
  6.4 35.1 %collective-permute-start.53 = (bf16[96,1024]{1,0:T(8,128)(2,1)}, bf16[96,1024]{1,0:T(8,128)(2,1)}, u32[]{:S(2)}, u32[]{:S(2)}) collective-permute-start(bf16[96,1024]{1,0:T(8,128)(2,1)} %fusion.44), channel_id=1, source_target_pairs={{0,4},{1,5},{2,6},{3,7},{4,8},{5,9},{6,10},{7,11},{8,12},{9,13},{1... | collective-permute-start | bytes 589832 | tf_op jit(solution)/shard_map/cond/branch_1_fun/sum_z/ppermute | solution.py:23
  13.4 31.2 %collective-permute-start.43 = (bf16[96,1024]{1,0:T(8,128)(2,1)}, bf16[96,1024]{1,0:T(8,128)(2,1)}, u32[]{:S(2)}, u32[]{:S(2)}) collective-permute-start(bf16[96,1024]{1,0:T(8,128)(2,1)} %fusion.42), channel_id=1, source_target_pairs={{0,4},{1,5},{2,6},{3,7},{4,8},{5,9},{6,10},{7,11},{8,12},{9,13},{1... | collective-permute-start | bytes 589832 | tf_op jit(solution)/shard_map/cond/branch_1_fun/sum_z/ppermute | solution.py:23
  20.4 27.4 %collective-permute-start.56 = (bf16[96,1024]{1,0:T(8,128)(2,1)}, bf16[96,1024]{1,0:T(8,128)(2,1)}, u32[]{:S(2)}, u32[]{:S(2)}) collective-permute-start(bf16[96,1024]{1,0:T(8,128)(2,1)} %fusion.45), channel_id=1, source_target_pairs={{0,28},{1,29},{2,30},{3,31},{4,0},{5,1},{6,2},{7,3},{8,4},{9,5},{1... | collective-permute-start | bytes 589832 | tf_op jit(solution)/shard_map/cond/branch_1_fun/sum_z/ppermute | solution.py:23
  33.0 21.1 %collective-permute-start.47 = (bf16[96,1024]{1,0:T(8,128)(2,1)}, bf16[96,1024]{1,0:T(8,128)(2,1)}, u32[]{:S(2)}, u32[]{:S(2)}) collective-permute-start(bf16[96,1024]{1,0:T(8,128)(2,1)} %fusion.43), channel_id=1, source_target_pairs={{0,28},{1,29},{2,30},{3,31},{4,0},{5,1},{6,2},{7,3},{8,4},{9,5},{1... | collective-permute-start | bytes 589832 | tf_op jit(solution)/shard_map/cond/branch_1_fun/sum_z/ppermute | solution.py:23
  42.7 27.5 %collective-permute-start.54 = (bf16[96,1024]{1,0:T(8,128)(2,1)S(1)}, bf16[96,1024]{1,0:T(8,128)(2,1)S(1)}, u32[]{:S(2)}, u32[]{:S(2)}) collective-permute-start(bf16[96,1024]{1,0:T(8,128)(2,1)S(1)} %add_convert_fusion.14), channel_id=1, source_target_pairs={{0,4},{1,5},{2,6},{3,7},{4,8},{5,9},{6,10},{7,11},{8,12},{9,13},{1... | collective-permute-start | bytes 589832 | tf_op jit(solution)/shard_map/cond/branch_1_fun/sum_z/ppermute | solution.py:23
  45.7 34.9 %copy-start.21 = (f32[96,1024]{1,0:T(8,128)S(1)}, f32[96,1024]{1,0:T(8,128)}, u32[]{:S(2)}) copy-start(f32[96,1024]{1,0:T(8,128)} %convolution_multiply_fusion.23) | copy-start | bytes 1179652 | tf_op jit(solution)/shard_map/cond
  45.7 17.2 %collective-permute-start.44 = (bf16[96,1024]{1,0:T(8,128)(2,1)S(1)}, bf16[96,1024]{1,0:T(8,128)(2,1)S(1)}, u32[]{:S(2)}, u32[]{:S(2)}) collective-permute-start(bf16[96,1024]{1,0:T(8,128)(2,1)S(1)} %add_convert_fusion.19), channel_id=1, source_target_pairs={{0,4},{1,5},{2,6},{3,7},{4,8},{5,9},{6,10},{7,11},{8,12},{9,13},{1... | collective-permute-start | bytes 589832 | tf_op jit(solution)/shard_map/cond/branch_1_fun/sum_z/ppermute | solution.py:23
  48.9 10.2 %collective-permute-start.57 = (bf16[96,1024]{1,0:T(8,128)(2,1)S(1)}, bf16[96,1024]{1,0:T(8,128)(2,1)S(1)}, u32[]{:S(2)}, u32[]{:S(2)}) collective-permute-start(bf16[96,1024]{1,0:T(8,128)(2,1)S(1)} %add_convert_fusion.12), channel_id=1, source_target_pairs={{0,28},{1,29},{2,30},{3,31},{4,0},{5,1},{6,2},{7,3},{8,4},{9,5},{1... | collective-permute-start | bytes 589832 | tf_op jit(solution)/shard_map/cond/branch_1_fun/sum_z/ppermute | solution.py:23
  55.2 9.9 %collective-permute-start.48 = (bf16[96,1024]{1,0:T(8,128)(2,1)S(1)}, bf16[96,1024]{1,0:T(8,128)(2,1)S(1)}, u32[]{:S(2)}, u32[]{:S(2)}) collective-permute-start(bf16[96,1024]{1,0:T(8,128)(2,1)S(1)} %add_convert_fusion.16), channel_id=1, source_target_pairs={{0,28},{1,29},{2,30},{3,31},{4,0},{5,1},{6,2},{7,3},{8,4},{9,5},{1... | collective-permute-start | bytes 589832 | tf_op jit(solution)/shard_map/cond/branch_1_fun/sum_z/ppermute | solution.py:23
  59.2 13.0 %collective-permute-start.58 = (bf16[96,1024]{1,0:T(8,128)(2,1)S(1)}, bf16[96,1024]{1,0:T(8,128)(2,1)S(1)}, u32[]{:S(2)}, u32[]{:S(2)}) collective-permute-start(bf16[96,1024]{1,0:T(8,128)(2,1)S(1)} %add_convert_fusion.11), channel_id=1, source_target_pairs={{0,28},{1,29},{2,30},{3,31},{4,0},{5,1},{6,2},{7,3},{8,4},{9,5},{1... | collective-permute-start | bytes 589832 | tf_op jit(solution)/shard_map/cond/branch_1_fun/sum_z/ppermute | solution.py:23
  63.0 14.5 %collective-permute-start.45 = (bf16[96,1024]{1,0:T(8,128)(2,1)S(1)}, bf16[96,1024]{1,0:T(8,128)(2,1)S(1)}, u32[]{:S(2)}, u32[]{:S(2)}) collective-permute-start(bf16[96,1024]{1,0:T(8,128)(2,1)S(1)} %add_convert_fusion.18), channel_id=1, source_target_pairs={{0,4},{1,5},{2,6},{3,7},{4,8},{5,9},{6,10},{7,11},{8,12},{9,13},{1... | collective-permute-start | bytes 589832 | tf_op jit(solution)/shard_map/cond/branch_1_fun/sum_z/ppermute | solution.py:23
  65.2 25.8 %collective-permute-start.49 = (bf16[96,1024]{1,0:T(8,128)(2,1)S(1)}, bf16[96,1024]{1,0:T(8,128)(2,1)S(1)}, u32[]{:S(2)}, u32[]{:S(2)}) collective-permute-start(bf16[96,1024]{1,0:T(8,128)(2,1)S(1)} %add_convert_fusion.15), channel_id=1, source_target_pairs={{0,28},{1,29},{2,30},{3,31},{4,0},{5,1},{6,2},{7,3},{8,4},{9,5},{1... | collective-permute-start | bytes 589832 | tf_op jit(solution)/shard_map/cond/branch_1_fun/sum_z/ppermute | solution.py:23
  70.2 109.4 %copy-start.6 = (bf16[1,128,2048]{2,1,0:T(8,128)(2,1)S(1)}, bf16[1,128,2048]{2,1,0:T(8,128)(2,1)}, u32[]{:S(2)}) copy-start(bf16[1,128,2048]{2,1,0:T(8,128)(2,1)} %get-tuple-element.158) | copy-start | bytes 1572868 | tf_op jit(solution)/shard_map/cond
  70.2 9.3 %collective-permute-start.55 = (bf16[96,1024]{1,0:T(8,128)(2,1)S(1)}, bf16[96,1024]{1,0:T(8,128)(2,1)S(1)}, u32[]{:S(2)}, u32[]{:S(2)}) collective-permute-start(bf16[96,1024]{1,0:T(8,128)(2,1)S(1)} %add_convert_fusion.13), channel_id=1, source_target_pairs={{0,4},{1,5},{2,6},{3,7},{4,8},{5,9},{6,10},{7,11},{8,12},{9,13},{1... | collective-permute-start | bytes 589832 | tf_op jit(solution)/shard_map/cond/branch_1_fun/sum_z/ppermute | solution.py:23
  72.3 8.3 %collective-permute-start.59 = (bf16[96,1024]{1,0:T(8,128)(2,1)S(1)}, bf16[96,1024]{1,0:T(8,128)(2,1)S(1)}, u32[]{:S(2)}, u32[]{:S(2)}) collective-permute-start(bf16[96,1024]{1,0:T(8,128)(2,1)S(1)} %add_convert_fusion.10), channel_id=1, source_target_pairs={{0,28},{1,29},{2,30},{3,31},{4,0},{5,1},{6,2},{7,3},{8,4},{9,5},{1... | collective-permute-start | bytes 589832 | tf_op jit(solution)/shard_map/cond/branch_1_fun/sum_z/ppermute | solution.py:23
  77.5 13.5 %collective-permute-start.46 = (bf16[96,1024]{1,0:T(8,128)(2,1)S(1)}, bf16[96,1024]{1,0:T(8,128)(2,1)S(1)}, u32[]{:S(2)}, u32[]{:S(2)}) collective-permute-start(bf16[96,1024]{1,0:T(8,128)(2,1)S(1)} %add_convert_fusion.17), channel_id=1, source_target_pairs={{0,4},{1,5},{2,6},{3,7},{4,8},{5,9},{6,10},{7,11},{8,12},{9,13},{1... | collective-permute-start | bytes 589832 | tf_op jit(solution)/shard_map/cond/branch_1_fun/sum_z/ppermute | solution.py:23
  80.7 16.4 %collective-permute-start.60 = (bf16[24,1024]{1,0:T(8,128)(2,1)S(1)}, bf16[24,1024]{1,0:T(8,128)(2,1)S(1)}, u32[]{:S(2)}, u32[]{:S(2)}) collective-permute-start(bf16[24,1024]{1,0:T(8,128)(2,1)S(1)} %get-tuple-element.225), channel_id=1, source_target_pairs={{0,1},{1,0},{2,3},{3,2},{4,5},{5,4},{6,7},{7,6},{8,9},{9,8},{10,11... | collective-permute-start | bytes 147464 | tf_op jit(solution)/shard_map/cond/branch_1_fun/sum_x/ppermute | solution.py:28
  84.1 17.3 %collective-permute-start.62 = (bf16[24,1024]{1,0:T(8,128)(2,1)S(1)}, bf16[24,1024]{1,0:T(8,128)(2,1)S(1)}, u32[]{:S(2)}, u32[]{:S(2)}) collective-permute-start(bf16[24,1024]{1,0:T(8,128)(2,1)S(1)} %get-tuple-element.226), channel_id=1, source_target_pairs={{0,3},{1,2},{2,1},{3,0},{4,7},{5,6},{6,5},{7,4},{8,11},{9,10},{10,... | collective-permute-start | bytes 147464 | tf_op jit(solution)/shard_map/cond/branch_1_fun/sum_x/ppermute | solution.py:28
  87.7 13.6 %collective-permute-start.61 = (bf16[24,1024]{1,0:T(8,128)(2,1)S(1)}, bf16[24,1024]{1,0:T(8,128)(2,1)S(1)}, u32[]{:S(2)}, u32[]{:S(2)}) collective-permute-start(bf16[24,1024]{1,0:T(8,128)(2,1)S(1)} %get-tuple-element.227), channel_id=1, source_target_pairs={{0,2},{1,3},{2,0},{3,1},{4,6},{5,7},{6,4},{7,5},{8,10},{9,11},{10,... | collective-permute-start | bytes 147464 | tf_op jit(solution)/shard_map/cond/branch_1_fun/sum_x/ppermute | solution.py:28
  91.2 10.2 %collective-permute-start.50 = (bf16[24,1024]{1,0:T(8,128)(2,1)S(1)}, bf16[24,1024]{1,0:T(8,128)(2,1)S(1)}, u32[]{:S(2)}, u32[]{:S(2)}) collective-permute-start(bf16[24,1024]{1,0:T(8,128)(2,1)S(1)} %get-tuple-element.222), channel_id=1, source_target_pairs={{0,1},{1,0},{2,3},{3,2},{4,5},{5,4},{6,7},{7,6},{8,9},{9,8},{10,11... | collective-permute-start | bytes 147464 | tf_op jit(solution)/shard_map/cond/branch_1_fun/sum_x/ppermute | solution.py:28
  93.4 7.9 %collective-permute-start.52 = (bf16[24,1024]{1,0:T(8,128)(2,1)S(1)}, bf16[24,1024]{1,0:T(8,128)(2,1)S(1)}, u32[]{:S(2)}, u32[]{:S(2)}) collective-permute-start(bf16[24,1024]{1,0:T(8,128)(2,1)S(1)} %get-tuple-element.223), channel_id=1, source_target_pairs={{0,3},{1,2},{2,1},{3,0},{4,7},{5,6},{6,5},{7,4},{8,11},{9,10},{10,... | collective-permute-start | bytes 147464 | tf_op jit(solution)/shard_map/cond/branch_1_fun/sum_x/ppermute | solution.py:28
  97.1 6.9 %collective-permute-start.51 = (bf16[24,1024]{1,0:T(8,128)(2,1)S(1)}, bf16[24,1024]{1,0:T(8,128)(2,1)S(1)}, u32[]{:S(2)}, u32[]{:S(2)}) collective-permute-start(bf16[24,1024]{1,0:T(8,128)(2,1)S(1)} %get-tuple-element.224), channel_id=1, source_target_pairs={{0,2},{1,3},{2,0},{3,1},{4,6},{5,7},{6,4},{7,5},{8,10},{9,11},{10,... | collective-permute-start | bytes 147464 | tf_op jit(solution)/shard_map/cond/branch_1_fun/sum_x/ppermute | solution.py:28
  104.7 18.7 %collective-permute-start.65 = (bf16[24,1024]{1,0:T(8,128)(2,1)S(1)}, bf16[24,1024]{1,0:T(8,128)(2,1)S(1)}, u32[]{:S(2)}, u32[]{:S(2)}) collective-permute-start(bf16[24,1024]{1,0:T(8,128)(2,1)S(1)} %get-tuple-element.221), channel_id=1, source_target_pairs={{0,3},{1,2},{2,1},{3,0},{4,7},{5,6},{6,5},{7,4},{8,11},{9,10},{10,... | collective-permute-start | bytes 147464 | tf_op jit(solution)/shard_map/cond/branch_1_fun/gather_x/ppermute | solution.py:28
  107.5 17.8 %collective-permute-start.64 = (bf16[24,1024]{1,0:T(8,128)(2,1)S(1)}, bf16[24,1024]{1,0:T(8,128)(2,1)S(1)}, u32[]{:S(2)}, u32[]{:S(2)}) collective-permute-start(bf16[24,1024]{1,0:T(8,128)(2,1)S(1)} %get-tuple-element.221), channel_id=1, source_target_pairs={{0,2},{1,3},{2,0},{3,1},{4,6},{5,7},{6,4},{7,5},{8,10},{9,11},{10,... | collective-permute-start | bytes 147464 | tf_op jit(solution)/shard_map/cond/branch_1_fun/gather_x/ppermute | solution.py:28
  113.2 12.1 %collective-permute-start.63 = (bf16[24,1024]{1,0:T(8,128)(2,1)S(1)}, bf16[24,1024]{1,0:T(8,128)(2,1)S(1)}, u32[]{:S(2)}, u32[]{:S(2)}) collective-permute-start(bf16[24,1024]{1,0:T(8,128)(2,1)S(1)} %get-tuple-element.221), channel_id=1, source_target_pairs={{0,1},{1,0},{2,3},{3,2},{4,5},{5,4},{6,7},{7,6},{8,9},{9,8},{10,11... | collective-permute-start | bytes 147464 | tf_op jit(solution)/shard_map/cond/branch_1_fun/gather_x/ppermute | solution.py:28
  115.1 12.7 %collective-permute-start.75 = (bf16[24,1024]{1,0:T(8,128)(2,1)S(1)}, bf16[24,1024]{1,0:T(8,128)(2,1)S(1)}, u32[]{:S(2)}, u32[]{:S(2)}) collective-permute-start(bf16[24,1024]{1,0:T(8,128)(2,1)S(1)} %get-tuple-element.212), channel_id=1, source_target_pairs={{0,3},{1,2},{2,1},{3,0},{4,7},{5,6},{6,5},{7,4},{8,11},{9,10},{10,... | collective-permute-start | bytes 147464 | tf_op jit(solution)/shard_map/cond/branch_1_fun/gather_x/ppermute | solution.py:28
  117.6 10.2 %collective-permute-start.74 = (bf16[24,1024]{1,0:T(8,128)(2,1)S(1)}, bf16[24,1024]{1,0:T(8,128)(2,1)S(1)}, u32[]{:S(2)}, u32[]{:S(2)}) collective-permute-start(bf16[24,1024]{1,0:T(8,128)(2,1)S(1)} %get-tuple-element.212), channel_id=1, source_target_pairs={{0,2},{1,3},{2,0},{3,1},{4,6},{5,7},{6,4},{7,5},{8,10},{9,11},{10,... | collective-permute-start | bytes 147464 | tf_op jit(solution)/shard_map/cond/branch_1_fun/gather_x/ppermute | solution.py:28
  123.3 6.0 %collective-permute-start.73 = (bf16[24,1024]{1,0:T(8,128)(2,1)S(1)}, bf16[24,1024]{1,0:T(8,128)(2,1)S(1)}, u32[]{:S(2)}, u32[]{:S(2)}) collective-permute-start(bf16[24,1024]{1,0:T(8,128)(2,1)S(1)} %get-tuple-element.212), channel_id=1, source_target_pairs={{0,1},{1,0},{2,3},{3,2},{4,5},{5,4},{6,7},{7,6},{8,9},{9,8},{10,11... | collective-permute-start | bytes 147464 | tf_op jit(solution)/shard_map/cond/branch_1_fun/gather_x/ppermute | solution.py:28
  125.3 55.9 %copy-start.11 = (bf16[96,1024]{1,0:T(8,128)(2,1)}, bf16[96,1024]{1,0:T(8,128)(2,1)S(1)}, u32[]{:S(2)}) copy-start(bf16[96,1024]{1,0:T(8,128)(2,1)S(1)} %pad_maximum_fusion.2.refs_0_.refs_1_) | copy-start | bytes 589828 | tf_op jit(solution)/shard_map/cond
  125.3 16.0 %collective-permute-start.69 = (bf16[96,1024]{1,0:T(8,128)(2,1)S(1)}, bf16[96,1024]{1,0:T(8,128)(2,1)S(1)}, u32[]{:S(2)}, u32[]{:S(2)}) collective-permute-start(bf16[96,1024]{1,0:T(8,128)(2,1)S(1)} %pad_maximum_fusion.2.refs_0_.refs_1_), channel_id=1, source_target_pairs={{0,4},{1,5},{2,6},{3,7},{4,8},{5,9},{6,10},{7,11},{8,12},{9,13},{1... | collective-permute-start | bytes 589832 | tf_op jit(solution)/shard_map/cond/branch_1_fun/gather_z/ppermute | solution.py:23
  129.3 61.2 %copy-start.16 = (bf16[96,1024]{1,0:T(8,128)(2,1)}, bf16[96,1024]{1,0:T(8,128)(2,1)S(1)}, u32[]{:S(2)}) copy-start(bf16[96,1024]{1,0:T(8,128)(2,1)S(1)} %pad_maximum_fusion.3.refs_8_.refs_1_) | copy-start | bytes 589828 | tf_op jit(solution)/shard_map/cond
  129.3 13.9 %collective-permute-start.76 = (bf16[96,1024]{1,0:T(8,128)(2,1)S(1)}, bf16[96,1024]{1,0:T(8,128)(2,1)S(1)}, u32[]{:S(2)}, u32[]{:S(2)}) collective-permute-start(bf16[96,1024]{1,0:T(8,128)(2,1)S(1)} %pad_maximum_fusion.3.refs_8_.refs_1_), channel_id=1, source_target_pairs={{0,28},{1,29},{2,30},{3,31},{4,0},{5,1},{6,2},{7,3},{8,4},{9,5},{1... | collective-permute-start | bytes 589832 | tf_op jit(solution)/shard_map/cond/branch_1_fun/gather_z/ppermute | solution.py:23
  135.5 13.0 %collective-permute-start.66 = (bf16[96,1024]{1,0:T(8,128)(2,1)S(1)}, bf16[96,1024]{1,0:T(8,128)(2,1)S(1)}, u32[]{:S(2)}, u32[]{:S(2)}) collective-permute-start(bf16[96,1024]{1,0:T(8,128)(2,1)S(1)} %pad_maximum_fusion.2.refs_0_.refs_1_), channel_id=1, source_target_pairs={{0,28},{1,29},{2,30},{3,31},{4,0},{5,1},{6,2},{7,3},{8,4},{9,5},{1... | collective-permute-start | bytes 589832 | tf_op jit(solution)/shard_map/cond/branch_1_fun/gather_z/ppermute | solution.py:23
  137.4 13.0 %collective-permute-start.80 = (bf16[96,1024]{1,0:T(8,128)(2,1)S(1)}, bf16[96,1024]{1,0:T(8,128)(2,1)S(1)}, u32[]{:S(2)}, u32[]{:S(2)}) collective-permute-start(bf16[96,1024]{1,0:T(8,128)(2,1)S(1)} %pad_maximum_fusion.3.refs_8_.refs_1_), channel_id=1, source_target_pairs={{0,4},{1,5},{2,6},{3,7},{4,8},{5,9},{6,10},{7,11},{8,12},{9,13},{1... | collective-permute-start | bytes 589832 | tf_op jit(solution)/shard_map/cond/branch_1_fun/gather_z/ppermute | solution.py:23
  141.3 39.9 %copy-start.36 = (bf16[96,1024]{1,0:T(8,128)(2,1)}, bf16[96,1024]{1,0:T(8,128)(2,1)S(1)}, u32[]{:S(2)}) copy-start(bf16[96,1024]{1,0:T(8,128)(2,1)S(1)} %collective-permute-done.69.refs_7_.refs_8_) | copy-start | bytes 589828 | tf_op jit(solution)/shard_map/cond
  141.4 13.0 %collective-permute-start.70 = (bf16[96,1024]{1,0:T(8,128)(2,1)S(1)}, bf16[96,1024]{1,0:T(8,128)(2,1)S(1)}, u32[]{:S(2)}, u32[]{:S(2)}) collective-permute-start(bf16[96,1024]{1,0:T(8,128)(2,1)S(1)} %collective-permute-done.69.refs_7_.refs_8_), channel_id=1, source_target_pairs={{0,4},{1,5},{2,6},{3,7},{4,8},{5,9},{6,10},{7,11},{8,12},{9,13},{1... | collective-permute-start | bytes 589832 | tf_op jit(solution)/shard_map/cond/branch_1_fun/gather_z/ppermute | solution.py:23
  143.3 47.3 %copy-start.41 = (bf16[96,1024]{1,0:T(8,128)(2,1)}, bf16[96,1024]{1,0:T(8,128)(2,1)S(1)}, u32[]{:S(2)}) copy-start(bf16[96,1024]{1,0:T(8,128)(2,1)S(1)} %collective-permute-done.76.refs_9_.refs_2_) | copy-start | bytes 589828 | tf_op jit(solution)/shard_map/cond
  143.3 13.0 %collective-permute-start.77 = (bf16[96,1024]{1,0:T(8,128)(2,1)S(1)}, bf16[96,1024]{1,0:T(8,128)(2,1)S(1)}, u32[]{:S(2)}, u32[]{:S(2)}) collective-permute-start(bf16[96,1024]{1,0:T(8,128)(2,1)S(1)} %collective-permute-done.76.refs_9_.refs_2_), channel_id=1, source_target_pairs={{0,28},{1,29},{2,30},{3,31},{4,0},{5,1},{6,2},{7,3},{8,4},{9,5},{1... | collective-permute-start | bytes 589832 | tf_op jit(solution)/shard_map/cond/branch_1_fun/gather_z/ppermute | solution.py:23
  148.5 32.8 %copy-start.46 = (bf16[96,1024]{1,0:T(8,128)(2,1)}, bf16[96,1024]{1,0:T(8,128)(2,1)S(1)}, u32[]{:S(2)}) copy-start(bf16[96,1024]{1,0:T(8,128)(2,1)S(1)} %collective-permute-done.66.refs_1_.refs_2_) | copy-start | bytes 589828 | tf_op jit(solution)/shard_map/cond
  148.5 18.1 %collective-permute-start.67 = (bf16[96,1024]{1,0:T(8,128)(2,1)S(1)}, bf16[96,1024]{1,0:T(8,128)(2,1)S(1)}, u32[]{:S(2)}, u32[]{:S(2)}) collective-permute-start(bf16[96,1024]{1,0:T(8,128)(2,1)S(1)} %collective-permute-done.66.refs_1_.refs_2_), channel_id=1, source_target_pairs={{0,28},{1,29},{2,30},{3,31},{4,0},{5,1},{6,2},{7,3},{8,4},{9,5},{1... | collective-permute-start | bytes 589832 | tf_op jit(solution)/shard_map/cond/branch_1_fun/gather_z/ppermute | solution.py:23
  150.4 40.2 %copy-start.51 = (bf16[96,1024]{1,0:T(8,128)(2,1)}, bf16[96,1024]{1,0:T(8,128)(2,1)S(1)}, u32[]{:S(2)}) copy-start(bf16[96,1024]{1,0:T(8,128)(2,1)S(1)} %collective-permute-done.80.refs_15_.refs_8_) | copy-start | bytes 589828 | tf_op jit(solution)/shard_map/cond
  150.4 18.5 %collective-permute-start.81 = (bf16[96,1024]{1,0:T(8,128)(2,1)S(1)}, bf16[96,1024]{1,0:T(8,128)(2,1)S(1)}, u32[]{:S(2)}, u32[]{:S(2)}) collective-permute-start(bf16[96,1024]{1,0:T(8,128)(2,1)S(1)} %collective-permute-done.80.refs_15_.refs_8_), channel_id=1, source_target_pairs={{0,4},{1,5},{2,6},{3,7},{4,8},{5,9},{6,10},{7,11},{8,12},{9,13},{1... | collective-permute-start | bytes 589832 | tf_op jit(solution)/shard_map/cond/branch_1_fun/gather_z/ppermute | solution.py:23
  154.4 26.9 %copy-start.56 = (bf16[96,1024]{1,0:T(8,128)(2,1)}, bf16[96,1024]{1,0:T(8,128)(2,1)S(1)}, u32[]{:S(2)}) copy-start(bf16[96,1024]{1,0:T(8,128)(2,1)S(1)} %collective-permute-done.70.refs_6_.refs_7_) | copy-start | bytes 589828 | tf_op jit(solution)/shard_map/cond
  154.4 18.1 %collective-permute-start.71 = (bf16[96,1024]{1,0:T(8,128)(2,1)S(1)}, bf16[96,1024]{1,0:T(8,128)(2,1)S(1)}, u32[]{:S(2)}, u32[]{:S(2)}) collective-permute-start(bf16[96,1024]{1,0:T(8,128)(2,1)S(1)} %collective-permute-done.70.refs_6_.refs_7_), channel_id=1, source_target_pairs={{0,4},{1,5},{2,6},{3,7},{4,8},{5,9},{6,10},{7,11},{8,12},{9,13},{1... | collective-permute-start | bytes 589832 | tf_op jit(solution)/shard_map/cond/branch_1_fun/gather_z/ppermute | solution.py:23
  156.3 34.3 %copy-start.61 = (bf16[96,1024]{1,0:T(8,128)(2,1)}, bf16[96,1024]{1,0:T(8,128)(2,1)S(1)}, u32[]{:S(2)}) copy-start(bf16[96,1024]{1,0:T(8,128)(2,1)S(1)} %collective-permute-done.77.refs_10_.refs_3_) | copy-start | bytes 589828 | tf_op jit(solution)/shard_map/cond
  156.3 18.1 %collective-permute-start.78 = (bf16[96,1024]{1,0:T(8,128)(2,1)S(1)}, bf16[96,1024]{1,0:T(8,128)(2,1)S(1)}, u32[]{:S(2)}, u32[]{:S(2)}) collective-permute-start(bf16[96,1024]{1,0:T(8,128)(2,1)S(1)} %collective-permute-done.77.refs_10_.refs_3_), channel_id=1, source_target_pairs={{0,28},{1,29},{2,30},{3,31},{4,0},{5,1},{6,2},{7,3},{8,4},{9,5},{1... | collective-permute-start | bytes 589832 | tf_op jit(solution)/shard_map/cond/branch_1_fun/gather_z/ppermute | solution.py:23
  161.5 43.4 %collective-permute-start.83 = (bf16[128,2048]{1,0:T(8,128)(2,1)S(1)}, bf16[128,2048]{1,0:T(8,128)(2,1)}, u32[]{:S(2)}, u32[]{:S(2)}) collective-permute-start(bf16[128,2048]{1,0:T(8,128)(2,1)S(1)} %bitcast.246), channel_id=1, source_target_pairs={{0,64},{32,96},{64,128},{96,160},{128,192},{160,224},{192,256},{22... | collective-permute-start | bytes 1572872 | tf_op jit(solution)/shard_map/cond/branch_1_fun/early_partner/ppermute | solution.py:33
  166.6 14.7 %copy-start.66 = (bf16[96,1024]{1,0:T(8,128)(2,1)}, bf16[96,1024]{1,0:T(8,128)(2,1)S(1)}, u32[]{:S(2)}) copy-start(bf16[96,1024]{1,0:T(8,128)(2,1)S(1)} %collective-permute-done.67.refs_2_.refs_3_) | copy-start | bytes 589828 | tf_op jit(solution)/shard_map/cond
  166.6 13.8 %collective-permute-start.68 = (bf16[96,1024]{1,0:T(8,128)(2,1)S(1)}, bf16[96,1024]{1,0:T(8,128)(2,1)S(1)}, u32[]{:S(2)}, u32[]{:S(2)}) collective-permute-start(bf16[96,1024]{1,0:T(8,128)(2,1)S(1)} %collective-permute-done.67.refs_2_.refs_3_), channel_id=1, source_target_pairs={{0,28},{1,29},{2,30},{3,31},{4,0},{5,1},{6,2},{7,3},{8,4},{9,5},{1... | collective-permute-start | bytes 589832 | tf_op jit(solution)/shard_map/cond/branch_1_fun/gather_z/ppermute | solution.py:23
  169.0 21.6 %copy-start.71 = (bf16[96,1024]{1,0:T(8,128)(2,1)}, bf16[96,1024]{1,0:T(8,128)(2,1)S(1)}, u32[]{:S(2)}) copy-start(bf16[96,1024]{1,0:T(8,128)(2,1)S(1)} %collective-permute-done.81.refs_14_.refs_7_) | copy-start | bytes 589828 | tf_op jit(solution)/shard_map/cond
  169.0 21.6 %collective-permute-start.82 = (bf16[96,1024]{1,0:T(8,128)(2,1)S(1)}, bf16[96,1024]{1,0:T(8,128)(2,1)S(1)}, u32[]{:S(2)}, u32[]{:S(2)}) collective-permute-start(bf16[96,1024]{1,0:T(8,128)(2,1)S(1)} %collective-permute-done.81.refs_14_.refs_7_), channel_id=1, source_target_pairs={{0,4},{1,5},{2,6},{3,7},{4,8},{5,9},{6,10},{7,11},{8,12},{9,13},{1... | collective-permute-start | bytes 589832 | tf_op jit(solution)/shard_map/cond/branch_1_fun/gather_z/ppermute | solution.py:23
  172.5 8.8 %copy-start.76 = (bf16[96,1024]{1,0:T(8,128)(2,1)}, bf16[96,1024]{1,0:T(8,128)(2,1)S(1)}, u32[]{:S(2)}) copy-start(bf16[96,1024]{1,0:T(8,128)(2,1)S(1)} %collective-permute-done.71.refs_5_.refs_6_) | copy-start | bytes 589828 | tf_op jit(solution)/shard_map/cond
  172.5 8.8 %collective-permute-start.72 = (bf16[96,1024]{1,0:T(8,128)(2,1)S(1)}, bf16[96,1024]{1,0:T(8,128)(2,1)S(1)}, u32[]{:S(2)}, u32[]{:S(2)}) collective-permute-start(bf16[96,1024]{1,0:T(8,128)(2,1)S(1)} %collective-permute-done.71.refs_5_.refs_6_), channel_id=1, source_target_pairs={{0,4},{1,5},{2,6},{3,7},{4,8},{5,9},{6,10},{7,11},{8,12},{9,13},{1... | collective-permute-start | bytes 589832 | tf_op jit(solution)/shard_map/cond/branch_1_fun/gather_z/ppermute | solution.py:23
  174.4 16.2 %copy-start.81 = (bf16[96,1024]{1,0:T(8,128)(2,1)}, bf16[96,1024]{1,0:T(8,128)(2,1)S(1)}, u32[]{:S(2)}) copy-start(bf16[96,1024]{1,0:T(8,128)(2,1)S(1)} %collective-permute-done.78.refs_11_.refs_4_) | copy-start | bytes 589828 | tf_op jit(solution)/shard_map/cond
  174.4 16.1 %collective-permute-start.79 = (bf16[96,1024]{1,0:T(8,128)(2,1)S(1)}, bf16[96,1024]{1,0:T(8,128)(2,1)}, u32[]{:S(2)}, u32[]{:S(2)}) collective-permute-start(bf16[96,1024]{1,0:T(8,128)(2,1)S(1)} %collective-permute-done.78.refs_11_.refs_4_), channel_id=1, source_target_pairs={{0,28},{1,29},{2,30},{3,31},{4,0},{5,1},{6,2},{7,3},{8,4},{9,5},{1... | collective-permute-start | bytes 589832 | tf_op jit(solution)/shard_map/cond/branch_1_fun/gather_z/ppermute | solution.py:23
  180.4 0.9 copy-start.86
  181.2 0.7 copy-start.96
  184.7 20.1 %collective-permute-start.84 = (bf16[128,1024]{1,0:T(8,128)(2,1)}, bf16[128,1024]{1,0:T(8,128)(2,1)}, u32[]{:S(2)}, u32[]{:S(2)}) collective-permute-start(bf16[128,1024]{1,0:T(8,128)(2,1)} %moment.12), channel_id=1, source_target_pairs={{0,64},{32,96},{64,128},{96,160},{128,192},{160,224},{192,256},{22... | collective-permute-start | bytes 786440 | tf_op jit(solution)/shard_map/cond/branch_1_fun/partner/ppermute | solution.py:33
  190.5 0.7 copy-start.91
  191.2 20.2 %copy-start.26 = (bf16[128,1024]{1,0:T(8,128)(2,1)S(1)}, bf16[128,1024]{1,0:T(8,128)(2,1)}, u32[]{:S(2)}) copy-start(bf16[128,1024]{1,0:T(8,128)(2,1)} %moment.12) | copy-start | bytes 786436 | tf_op jit(solution)/shard_map/cond
  194.0 17.4 %copy-start.31 = (bf16[128,1024]{1,0:T(8,128)(2,1)S(1)}, bf16[128,1024]{1,0:T(8,128)(2,1)}, u32[]{:S(2)}) copy-start(bf16[128,1024]{1,0:T(8,128)(2,1)} %moment.13) | copy-start | bytes 786436 | tf_op jit(solution)/shard_map/cond
  194.0 17.4 %collective-permute-start.85 = (bf16[128,1024]{1,0:T(8,128)(2,1)}, bf16[128,1024]{1,0:T(8,128)(2,1)S(1)}, u32[]{:S(2)}, u32[]{:S(2)}) collective-permute-start(bf16[128,1024]{1,0:T(8,128)(2,1)} %moment.13), channel_id=1, source_target_pairs={{0,64},{32,96},{64,128},{96,160},{128,192},{160,224},{192,256},{22... | collective-permute-start | bytes 786440 | tf_op jit(solution)/shard_map/cond/branch_1_fun/partner/ppermute | solution.py:33

commit v2 on v1

v2 whole, which is shorter than its diff:
```python
from functools import partial

import jax
import jax.numpy as jnp
from jax import lax
from jax.experimental import pallas as pl
from jax.experimental.pallas import tpu as pltpu
from jax.sharding import PartitionSpec as P

SEGS = 96
BETA_MOM = 0.9
STEP_RATE = 0.1
NX = 4
PARTS = 2
SCALARS = pl.BlockSpec(memory_space=pltpu.SMEM)


def vmem(count):
    return [pl.BlockSpec(memory_space=pltpu.VMEM)] * count


def shift_z(x, by):
    size = lax.axis_size("tensor")
    return lax.ppermute(x, "tensor", [(i, (i + by * NX) % size) for i in range(size)])


def swap_x(x, k):
    size = lax.axis_size("tensor")
    return lax.ppermute(x, "tensor", [(i, i ^ k) for i in range(size)])


def pass_replica(x, by):
    size = lax.axis_size("replica")
    return lax.ppermute(x, "replica", [(i, (i + by) % size) for i in range(size)])


def place_of(j, k, z, x, nz):
    return lax.rem(z + j, nz) * NX + (x ^ k)


def order_kernel(nz, place_ref, rows_ref, out_ref):
    for j in range(nz):
        for k in range(NX):
            out_ref[j * NX + k] = rows_ref[place_of(j, k, place_ref[0], place_ref[1], nz)]


def moment_kernel(scaling, nz, *refs):
    heads_ref, blocks, mom_ref, out_ref, held = refs[0], refs[1 : 1 + nz], refs[-3], refs[-2], refs[-1]
    rows = blocks[0].shape[0]
    for j in range(nz):
        held[j * rows : (j + 1) * rows, :] = blocks[j][...]
    total = lax.dot_general(
        heads_ref[...], held[...], (((0,), (0,)), ((), ())), preferred_element_type=jnp.float32
    )
    out_ref[...] = (BETA_MOM * mom_ref[...].astype(jnp.float32) + total * scaling).astype(jnp.bfloat16)


def moment_of(heads, blocks, mom, scaling, part):
    nz, (rows, width) = len(blocks), blocks[0].shape
    deep, cols = heads.shape[1], width // PARTS
    tile = min(512, cols)
    first = part * cols // tile
    column = lambda n: pl.BlockSpec((n, tile), lambda i: (0, first + i))
    return pl.pallas_call(
        partial(moment_kernel, scaling, nz),
        grid=(cols // tile,),
        out_shape=jax.ShapeDtypeStruct((deep, cols), jnp.bfloat16),
        in_specs=[pl.BlockSpec(heads.shape, lambda i: (0, 0))] + [column(rows)] * nz + [column(deep)],
        out_specs=pl.BlockSpec((deep, tile), lambda i: (0, i)),
        scratch_shapes=[pltpu.VMEM((nz * rows, tile), jnp.bfloat16)],
        cost_estimate=pl.CostEstimate(
            flops=2 * heads.size * cols, bytes_accessed=2 * (nz * rows * cols + 2 * deep * cols), transcendentals=0
        ),
        name="moment",
    )(heads, *blocks, mom)


def back_kernel(scaling, nz, place_ref, *refs):
    w_ref, out_ref = refs[-2], refs[-1]
    rows = out_ref.shape[1]
    for j in range(nz):
        total = lax.dot_general(
            refs[j][...], w_ref[...], (((1,), (1,)), ((), ())), preferred_element_type=jnp.float32
        )
        for k in range(NX):
            out_ref[place_of(j, k, place_ref[0], place_ref[1], nz)] = (
                total[k * rows : (k + 1) * rows] * scaling
            ).astype(jnp.bfloat16)


def sum_stage(heads_in, weight, target_rows, seg_rows):
    tokens, deep = heads_in.shape
    size = lax.axis_size("tensor")
    nz, rows = size // NX, tokens // size
    chunk = rows * NX
    scaling = (deep * size) ** (-0.5)
    own = lax.axis_index("tensor")
    place = jnp.stack([own // NX, own % NX]).astype(jnp.int32)
    with jax.named_scope("order"):
        heads = pl.pallas_call(
            partial(order_kernel, nz),
            out_shape=jax.ShapeDtypeStruct((size, rows, deep), jnp.bfloat16),
            in_specs=[SCALARS] + vmem(1),
            out_specs=vmem(1)[0],
            name="order",
        )(place, heads_in.reshape(size, rows, deep)).reshape(tokens, deep)
    first_row = own * rows
    own_seg = lax.dynamic_slice_in_dim(seg_rows, first_row, rows, 0)
    doc_sizes = jnp.sum((own_seg[:, None] == seg_rows[None, :]).astype(jnp.float32), axis=1)
    own_weights = (tokens / (SEGS * doc_sizes))[:, None]
    own_targets = lax.dynamic_slice_in_dim(target_rows, first_row, rows, 0).astype(jnp.float32)

    def share(j):
        j = j % nz
        return scaling * jnp.dot(
            heads[j * chunk : (j + 1) * chunk], weight, preferred_element_type=jnp.float32
        )

    with jax.named_scope("sum_z"):
        total = share(0)
        flows = [[1, nz // 2, None], [-1, nz // 2 - 1, None]]
        for s in range(nz // 2):
            for flow in flows:
                way, steps, cur = flow
                if s < steps:
                    term = share(way * (steps - s))
                    if cur is not None:
                        term = term + cur.astype(jnp.float32)
                    flow[2] = shift_z(term.astype(jnp.bfloat16), way)
        total = total + flows[0][2].astype(jnp.float32) + flows[1][2].astype(jnp.float32)
    with jax.named_scope("sum_x"):
        mine = total[:rows]
        for k in range(1, NX):
            sent = swap_x(total[k * rows : (k + 1) * rows].astype(jnp.bfloat16), k)
            mine = mine + sent.astype(jnp.float32)
    grad = ((mine - own_targets) * own_weights).astype(jnp.bfloat16)
    return mine.astype(jnp.bfloat16), grad, heads, place


def update_stage(hop, grad, heads, place, weight, moment_in):
    tokens, deep = heads.shape
    rows, width = grad.shape
    size = lax.axis_size("tensor")
    nz = size // NX
    scaling = (deep * size) ** (-0.5)
    with jax.named_scope("early_partner"):
        partner_w = pass_replica(weight, hop)
    with jax.named_scope("gather_x"):
        block = jnp.concatenate([grad] + [swap_x(grad, k) for k in range(1, NX)], axis=0)
    with jax.named_scope("gather_z"):
        held = [block] + [None] * (nz - 1)
        flows = [[1, nz // 2, block], [-1, nz // 2 - 1, block]]
        for s in range(nz // 2):
            for flow in flows:
                way, steps, cur = flow
                if s < steps:
                    if s == nz // 2 - 2 and way == 1:
                        cur, partner_w = lax.optimization_barrier((cur, partner_w))
                    flow[2] = shift_z(cur, way)
                    held[(-way * (s + 1)) % nz] = flow[2]
    new_w, new_m = [], []
    cols = width // PARTS
    for c in range(PARTS):
        part = slice(c * cols, (c + 1) * cols)
        moment = moment_of(heads, held, moment_in, scaling, c)
        with jax.named_scope("partner"):
            partner_m = pass_replica(moment, hop).astype(jnp.float32)
        moment = moment.astype(jnp.float32)
        updated = (weight[:, part].astype(jnp.float32) - STEP_RATE * moment).astype(jnp.bfloat16)
        partner_u = (partner_w[:, part].astype(jnp.float32) - STEP_RATE * partner_m).astype(jnp.bfloat16)
        new_w.append(((updated.astype(jnp.float32) + partner_u.astype(jnp.float32)) * 0.5).astype(jnp.bfloat16))
        new_m.append(((moment + partner_m) * 0.5).astype(jnp.bfloat16))
    with jax.named_scope("back"):
        attn_grad = pl.pallas_call(
            partial(back_kernel, scaling, nz),
            out_shape=jax.ShapeDtypeStruct((size, rows, deep), jnp.bfloat16),
            in_specs=[SCALARS] + vmem(nz + 1),
            out_specs=vmem(1)[0],
            cost_estimate=pl.CostEstimate(
                flops=2 * tokens * width * deep, bytes_accessed=2 * tokens * width, transcendentals=0
            ),
            name="back",
        )(place, *held, weight).reshape(tokens, deep)
    join = lambda pieces: jnp.concatenate(pieces, axis=1)
    return attn_grad, join(new_w), join(new_m)


def program(attn_out, proj, momentum, target, segment_ids, step):
    levels = lax.axis_size("replica").bit_length() - 1
    projected, grad, heads, place = sum_stage(attn_out[0], proj[0], target[0], segment_ids[0])
    branches = [partial(update_stage, 1 << bit) for bit in range(levels)]
    outs = lax.switch(step[0] % levels, branches, grad, heads, place, proj[0], momentum[0])
    return tuple(out[None] for out in (projected, *outs))


def solution(mesh):
    return jax.shard_map(
        program,
        mesh=mesh,
        in_specs=(
            P("replica", None, "tensor"),
            P("replica", "tensor", None),
            P("replica", "tensor", None),
            P("replica", None, None),
            P("replica", None),
            P(),
        ),
        out_specs=(
            P("replica", "tensor", None),
            P("replica", None, "tensor"),
            P("replica", "tensor", None),
            P("replica", "tensor", None),
        ),
        check_vma=False,
    )
```

time: 216 us -> 186 us (0.86)
  the two profiles are of different devices: /device:TPU:2 before, /device:TPU:66 now
where the time goes in v2:
time: 186 us; the launch traced here: 185 us
  starting transfers between devices  94.4 us (51%)
  waiting for transfers between devices  68.6 us (37%)
  Pallas kernels  9.44 us (5%)
  matrix products  5.2 us (3%)
  other arithmetic  2.77 us (1%)
  local copies, waits for them, and re-layouts  2.76 us (1%)
    ppermute x14, starting transfers between devices, shift_z(): lax.ppermute(x, 'tensor', [(i, (i + by * NX) % size) for i in range(size)])  59.8 us
    ppermute x14, waiting for transfers between devices, shift_z(): lax.ppermute(x, 'tensor', [(i, (i + by * NX) % size) for i in range(size)])  41 us
    ppermute x6, starting transfers between devices, swap_x(): return lax.ppermute(x, 'tensor', [(i, i ^ k) for i in range(size)])  20.6 us
    ppermute x3, waiting for transfers between devices, pass_replica(): lax.ppermute(x, 'replica', [(i, (i + by) % size) for i in range(size)])  19.5 us
    ppermute x3, starting transfers between devices, pass_replica(): lax.ppermute(x, 'replica', [(i, (i + by) % size) for i in range(size)])  14 us
    ppermute x6, waiting for transfers between devices, swap_x(): return lax.ppermute(x, 'tensor', [(i, i ^ k) for i in range(size)])  8.1 us
    dot_general x8, matrix products, share(): jnp.dot(heads[j * chunk:(j + 1) * chunk], weight, preferred_element_type=...  5.2 us
    pallas_call x2, Pallas kernels, moment_of(): pl.pallas_call(partial(moment_kernel, scaling, nz), grid=(cols // tile,),...  5.11 us
  transfers between devices with their start and end apart: 23, of which 14 were waited for; matrix products, arithmetic and copies ran while one was open for 2% of the time, Pallas kernels for 3%

profile of v2, /device:TPU:66, one launch (start us, length us, event | category | flops | bytes accessed | tf_op | source)
XLA Modules:
  0.0 185.3 jit_solution(13130995413511426643)
XLA Ops:
  0.7 0.1 pad_add_fusion.place_ref
  0.7 1.0 order.1
  1.8 1.3 fusion.60
  3.1 5.2 %collective-permute-start.65 = (bf16[96,2048]{1,0:T(8,128)(2,1)S(1)}, bf16[96,2048]{1,0:T(8,128)(2,1)S(1)}, u32[]{:S(2)}, u32[]{:S(2)}) collective-permute-start(bf16[96,2048]{1,0:T(8,128)(2,1)S(1)} %fusion.60), channel_id=1, source_target_pairs={{0,4},{1,5},{2,6},{3,7},{4,8},{5,9},{6,10},{7,11},{8,12},{9,13},{1... | collective-permute-start | bytes 1179656 | tf_op jit(solution)/shard_map/sum_z/ppermute | solution.py:24
  8.3 1.3 fusion.61
  9.6 14.0 %collective-permute-start.69 = (bf16[96,2048]{1,0:T(8,128)(2,1)S(1)}, bf16[96,2048]{1,0:T(8,128)(2,1)S(1)}, u32[]{:S(2)}, u32[]{:S(2)}) collective-permute-start(bf16[96,2048]{1,0:T(8,128)(2,1)S(1)} %fusion.61), channel_id=1, source_target_pairs={{0,28},{1,29},{2,30},{3,31},{4,0},{5,1},{6,2},{7,3},{8,4},{9,5},{1... | collective-permute-start | bytes 1179656 | tf_op jit(solution)/shard_map/sum_z/ppermute | solution.py:24
  23.7 1.3 convolution_multiply_fusion.2
  25.0 0.3 convolution_multiply_fusion.5
  25.3 4.3 %collective-permute-done.65 = bf16[96,2048]{1,0:T(8,128)(2,1)S(1)} collective-permute-done((bf16[96,2048]{1,0:T(8,128)(2,1)S(1)}, bf16[96,2048]{1,0:T(8,128)(2,1)S(1)}, u32[]{:S(2)}, u32[]{:S(2)}) %collective-permute-start.65) | collective-permute-done | bytes 393248 | tf_op jit(solution)/shard_map/sum_z/ppermute | solution.py:24
  29.5 0.3 add_convert_fusion.4
  29.8 1.9 %collective-permute-start.66 = (bf16[96,2048]{1,0:T(8,128)(2,1)S(1)}, bf16[96,2048]{1,0:T(8,128)(2,1)S(1)}, u32[]{:S(2)}, u32[]{:S(2)}) collective-permute-start(bf16[96,2048]{1,0:T(8,128)(2,1)S(1)} %add_convert_fusion.4), channel_id=1, source_target_pairs={{0,4},{1,5},{2,6},{3,7},{4,8},{5,9},{6,10},{7,11},{8,12},{9,13},{1... | collective-permute-start | bytes 1179656 | tf_op jit(solution)/shard_map/sum_z/ppermute | solution.py:24
  31.7 0.3 convolution_multiply_fusion.6
  32.0 0.3 add_convert_fusion.1
  32.3 5.6 %collective-permute-start.70 = (bf16[96,2048]{1,0:T(8,128)(2,1)S(1)}, bf16[96,2048]{1,0:T(8,128)(2,1)S(1)}, u32[]{:S(2)}, u32[]{:S(2)}) collective-permute-start(bf16[96,2048]{1,0:T(8,128)(2,1)S(1)} %add_convert_fusion.1), channel_id=1, source_target_pairs={{0,28},{1,29},{2,30},{3,31},{4,0},{5,1},{6,2},{7,3},{8,4},{9,5},{1... | collective-permute-start | bytes 1179656 | tf_op jit(solution)/shard_map/sum_z/ppermute | solution.py:24
  37.9 5.3 %collective-permute-done.66 = bf16[96,2048]{1,0:T(8,128)(2,1)S(1)} collective-permute-done((bf16[96,2048]{1,0:T(8,128)(2,1)S(1)}, bf16[96,2048]{1,0:T(8,128)(2,1)S(1)}, u32[]{:S(2)}, u32[]{:S(2)}) %collective-permute-start.66) | collective-permute-done | bytes 393248 | tf_op jit(solution)/shard_map/sum_z/ppermute | solution.py:24
  43.2 0.1 add_convert_fusion.3
  43.3 1.9 %collective-permute-start.67 = (bf16[96,2048]{1,0:T(8,128)(2,1)S(1)}, bf16[96,2048]{1,0:T(8,128)(2,1)S(1)}, u32[]{:S(2)}, u32[]{:S(2)}) collective-permute-start(bf16[96,2048]{1,0:T(8,128)(2,1)S(1)} %add_convert_fusion.3), channel_id=1, source_target_pairs={{0,4},{1,5},{2,6},{3,7},{4,8},{5,9},{6,10},{7,11},{8,12},{9,13},{1... | collective-permute-start | bytes 1179656 | tf_op jit(solution)/shard_map/sum_z/ppermute | solution.py:24
  45.2 0.2 collective-permute-done.70
  45.4 0.1 add_convert_fusion
  45.5 5.6 %collective-permute-start.71 = (bf16[96,2048]{1,0:T(8,128)(2,1)S(1)}, bf16[96,2048]{1,0:T(8,128)(2,1)S(1)}, u32[]{:S(2)}, u32[]{:S(2)}) collective-permute-start(bf16[96,2048]{1,0:T(8,128)(2,1)S(1)} %add_convert_fusion), channel_id=1, source_target_pairs={{0,28},{1,29},{2,30},{3,31},{4,0},{5,1},{6,2},{7,3},{8,4},{9,5},{1... | collective-permute-start | bytes 1179656 | tf_op jit(solution)/shard_map/sum_z/ppermute | solution.py:24
  51.1 4.7 %collective-permute-done.67 = bf16[96,2048]{1,0:T(8,128)(2,1)S(1)} collective-permute-done((bf16[96,2048]{1,0:T(8,128)(2,1)S(1)}, bf16[96,2048]{1,0:T(8,128)(2,1)S(1)}, u32[]{:S(2)}, u32[]{:S(2)}) %collective-permute-start.67) | collective-permute-done | bytes 393248 | tf_op jit(solution)/shard_map/sum_z/ppermute | solution.py:24
  55.8 0.1 add_convert_fusion.2
  55.9 2.1 %collective-permute-start.68 = (bf16[96,2048]{1,0:T(8,128)(2,1)S(1)}, bf16[96,2048]{1,0:T(8,128)(2,1)S(1)}, u32[]{:S(2)}, u32[]{:S(2)}) collective-permute-start(bf16[96,2048]{1,0:T(8,128)(2,1)S(1)} %add_convert_fusion.2), channel_id=1, source_target_pairs={{0,4},{1,5},{2,6},{3,7},{4,8},{5,9},{6,10},{7,11},{8,12},{9,13},{1... | collective-permute-start | bytes 1179656 | tf_op jit(solution)/shard_map/sum_z/ppermute | solution.py:24
  57.9 0.1 dynamic-slice_bitcast_fusion
  58.0 0.2 convert_reduce_fusion
  58.2 0.3 convolution_multiply_fusion.7
  58.5 9.1 %collective-permute-done.68 = bf16[96,2048]{1,0:T(8,128)(2,1)S(1)} collective-permute-done((bf16[96,2048]{1,0:T(8,128)(2,1)S(1)}, bf16[96,2048]{1,0:T(8,128)(2,1)S(1)}, u32[]{:S(2)}, u32[]{:S(2)}) %collective-permute-start.68) | collective-permute-done | bytes 393248 | tf_op jit(solution)/shard_map/sum_z/ppermute | solution.py:24
  67.5 0.1 fusion.74
  67.7 2.5 %collective-permute-start.72 = (bf16[24,2048]{1,0:T(8,128)(2,1)S(1)}, bf16[24,2048]{1,0:T(8,128)(2,1)S(1)}, u32[]{:S(2)}, u32[]{:S(2)}) collective-permute-start(bf16[24,2048]{1,0:T(8,128)(2,1)S(1)} %get-tuple-element.142), channel_id=1, source_target_pairs={{0,1},{1,0},{2,3},{3,2},{4,5},{5,4},{6,7},{7,6},{8,9},{9,8},{10,11... | collective-permute-start | bytes 294920 | tf_op jit(solution)/shard_map/sum_x/ppermute | solution.py:29
  70.2 4.4 %collective-permute-start.74 = (bf16[24,2048]{1,0:T(8,128)(2,1)S(1)}, bf16[24,2048]{1,0:T(8,128)(2,1)S(1)}, u32[]{:S(2)}, u32[]{:S(2)}) collective-permute-start(bf16[24,2048]{1,0:T(8,128)(2,1)S(1)} %get-tuple-element.143), channel_id=1, source_target_pairs={{0,3},{1,2},{2,1},{3,0},{4,7},{5,6},{6,5},{7,4},{8,11},{9,10},{10,... | collective-permute-start | bytes 294920 | tf_op jit(solution)/shard_map/sum_x/ppermute | solution.py:29
  74.6 3.3 %collective-permute-start.73 = (bf16[24,2048]{1,0:T(8,128)(2,1)S(1)}, bf16[24,2048]{1,0:T(8,128)(2,1)S(1)}, u32[]{:S(2)}, u32[]{:S(2)}) collective-permute-start(bf16[24,2048]{1,0:T(8,128)(2,1)S(1)} %get-tuple-element.144), channel_id=1, source_target_pairs={{0,2},{1,3},{2,0},{3,1},{4,6},{5,7},{6,4},{7,5},{8,10},{9,11},{10,... | collective-permute-start | bytes 294920 | tf_op jit(solution)/shard_map/sum_x/ppermute | solution.py:29
  78.5 1.5 collective-permute-done.74
  80.1 2.0 %collective-permute-done.73 = bf16[24,2048]{1,0:T(8,128)(2,1)S(1)} collective-permute-done((bf16[24,2048]{1,0:T(8,128)(2,1)S(1)}, bf16[24,2048]{1,0:T(8,128)(2,1)S(1)}, u32[]{:S(2)}, u32[]{:S(2)}) %collective-permute-start.73) | collective-permute-done | bytes 98336 | tf_op jit(solution)/shard_map/sum_x/ppermute | solution.py:29
  82.1 1.6 fusion.65
  83.7 100.6 %conditional.1 = (bf16[1,768,128]{2,1,0:T(8,128)(2,1)S(1)}, bf16[1,128,2048]{2,1,0:T(8,128)(2,1)S(1)}, bf16[1,128,2048]{2,1,0:T(8,128)(2,1)S(1)}) conditional(s32[]{:T(128)} %clamp.3, (bf16[24,2048]{1,0:T(8,128)(2,1)S(1)}, bf16[128,2048]{1,0:T(8,128)(2,1)S(1)}, s32[2]{0:T(128)S(1)}, ...), branch_computations={%region_1.2_spmd, %region_2.3_spmd, %region_3.4_spmd, %region_4.5_... | conditional | flops 812122112 | bytes 48628592 | solution.py:192
  83.7 2.4 %collective-permute-start.15 = (bf16[24,2048]{1,0:T(8,128)(2,1)S(1)}, bf16[24,2048]{1,0:T(8,128)(2,1)S(1)}, u32[]{:S(2)}, u32[]{:S(2)}) collective-permute-start(bf16[24,2048]{1,0:T(8,128)(2,1)S(1)} %get-tuple-element.71), channel_id=1, source_target_pairs={{0,3},{1,2},{2,1},{3,0},{4,7},{5,6},{6,5},{7,4},{8,11},{9,10},{10,... | collective-permute-start | bytes 294920 | tf_op jit(solution)/shard_map/cond/branch_1_fun/gather_x/ppermute | solution.py:29
  86.0 6.2 %collective-permute-start.14 = (bf16[24,2048]{1,0:T(8,128)(2,1)S(1)}, bf16[24,2048]{1,0:T(8,128)(2,1)S(1)}, u32[]{:S(2)}, u32[]{:S(2)}) collective-permute-start(bf16[24,2048]{1,0:T(8,128)(2,1)S(1)} %get-tuple-element.71), channel_id=1, source_target_pairs={{0,2},{1,3},{2,0},{3,1},{4,6},{5,7},{6,4},{7,5},{8,10},{9,11},{10,... | collective-permute-start | bytes 294920 | tf_op jit(solution)/shard_map/cond/branch_1_fun/gather_x/ppermute | solution.py:29
  92.2 1.9 %collective-permute-start.13 = (bf16[24,2048]{1,0:T(8,128)(2,1)S(1)}, bf16[24,2048]{1,0:T(8,128)(2,1)S(1)}, u32[]{:S(2)}, u32[]{:S(2)}) collective-permute-start(bf16[24,2048]{1,0:T(8,128)(2,1)S(1)} %get-tuple-element.71), channel_id=1, source_target_pairs={{0,1},{1,0},{2,3},{3,2},{4,5},{5,4},{6,7},{7,6},{8,9},{9,8},{10,11... | collective-permute-start | bytes 294920 | tf_op jit(solution)/shard_map/cond/branch_1_fun/gather_x/ppermute | solution.py:29
  94.2 4.6 %collective-permute-done.13 = bf16[24,2048]{1,0:T(8,128)(2,1)S(1)} collective-permute-done((bf16[24,2048]{1,0:T(8,128)(2,1)S(1)}, bf16[24,2048]{1,0:T(8,128)(2,1)S(1)}, u32[]{:S(2)}, u32[]{:S(2)}) %collective-permute-start.13) | collective-permute-done | bytes 98336 | tf_op jit(solution)/shard_map/cond/branch_1_fun/gather_x/ppermute | solution.py:29
  98.8 1.9 %collective-permute-start.19 = (bf16[96,2048]{1,0:T(8,128)(2,1)S(1)}, bf16[96,2048]{1,0:T(8,128)(2,1)S(1)}, u32[]{:S(2)}, u32[]{:S(2)}) collective-permute-start(bf16[96,2048]{1,0:T(8,128)(2,1)S(1)} %constant_dynamic-update-slice_fusion.4.refs_0_.refs_1_), channel_id=1, source_target_pairs={{0,4},{1,5},{2,6},{3,7},{4,8},{5,9},{6,10},{7,11},{8,12},{9,13},{1... | collective-permute-start | bytes 1179656 | tf_op jit(solution)/shard_map/cond/branch_1_fun/gather_z/ppermute | solution.py:24
  100.7 5.0 %collective-permute-start.21 = (bf16[128,2048]{1,0:T(8,128)(2,1)S(1)}, bf16[128,2048]{1,0:T(8,128)(2,1)S(1)}, u32[]{:S(2)}, u32[]{:S(2)}) collective-permute-start(bf16[128,2048]{1,0:T(8,128)(2,1)S(1)} %get-tuple-element.72.refs_8_), channel_id=1, source_target_pairs={{0,64},{32,96},{64,128},{96,160},{128,192},{160,224},{192,256},{22... | collective-permute-start | bytes 1572872 | tf_op jit(solution)/shard_map/cond/branch_1_fun/early_partner/ppermute | solution.py:34
  105.8 5.1 %collective-permute-start.16 = (bf16[96,2048]{1,0:T(8,128)(2,1)S(1)}, bf16[96,2048]{1,0:T(8,128)(2,1)S(1)}, u32[]{:S(2)}, u32[]{:S(2)}) collective-permute-start(bf16[96,2048]{1,0:T(8,128)(2,1)S(1)} %constant_dynamic-update-slice_fusion.4.refs_0_.refs_1_), channel_id=1, source_target_pairs={{0,28},{1,29},{2,30},{3,31},{4,0},{5,1},{6,2},{7,3},{8,4},{9,5},{1... | collective-permute-start | bytes 1179656 | tf_op jit(solution)/shard_map/cond/branch_1_fun/gather_z/ppermute | solution.py:24
  110.9 1.9 %collective-permute-start.20 = (bf16[96,2048]{1,0:T(8,128)(2,1)S(1)}, bf16[96,2048]{1,0:T(8,128)(2,1)S(1)}, u32[]{:S(2)}, u32[]{:S(2)}) collective-permute-start(bf16[96,2048]{1,0:T(8,128)(2,1)S(1)} %collective-permute-done.19.refs_7_.refs_8_), channel_id=1, source_target_pairs={{0,4},{1,5},{2,6},{3,7},{4,8},{5,9},{6,10},{7,11},{8,12},{9,13},{1... | collective-permute-start | bytes 1179656 | tf_op jit(solution)/shard_map/cond/branch_1_fun/gather_z/ppermute | solution.py:24
  112.9 3.4 %collective-permute-done.16.refs_1_.refs_2_ = bf16[96,2048]{1,0:T(8,128)(2,1)S(1)} collective-permute-done((bf16[96,2048]{1,0:T(8,128)(2,1)S(1)}, bf16[96,2048]{1,0:T(8,128)(2,1)S(1)}, u32[]{:S(2)}, u32[]{:S(2)}) %collective-permute-start.16) | collective-permute-done | bytes 393248 | tf_op jit(solution)/shard_map/cond/branch_1_fun/gather_z/ppermute | solution.py:24
  116.3 5.6 %collective-permute-start.17 = (bf16[96,2048]{1,0:T(8,128)(2,1)S(1)}, bf16[96,2048]{1,0:T(8,128)(2,1)S(1)}, u32[]{:S(2)}, u32[]{:S(2)}) collective-permute-start(bf16[96,2048]{1,0:T(8,128)(2,1)S(1)} %collective-permute-done.16.refs_1_.refs_2_), channel_id=1, source_target_pairs={{0,28},{1,29},{2,30},{3,31},{4,0},{5,1},{6,2},{7,3},{8,4},{9,5},{1... | collective-permute-start | bytes 1179656 | tf_op jit(solution)/shard_map/cond/branch_1_fun/gather_z/ppermute | solution.py:24
  121.9 7.8 %collective-permute-done.21 = bf16[128,2048]{1,0:T(8,128)(2,1)S(1)} collective-permute-done((bf16[128,2048]{1,0:T(8,128)(2,1)S(1)}, bf16[128,2048]{1,0:T(8,128)(2,1)S(1)}, u32[]{:S(2)}, u32[]{:S(2)}) %collective-permute-start.21) | collective-permute-done | bytes 524320 | tf_op jit(solution)/shard_map/cond/branch_1_fun/early_partner/ppermute | solution.py:34
  129.6 0.8 copy-done.54
  130.4 1.9 %collective-permute-start.22 = (bf16[96,2048]{1,0:T(8,128)(2,1)S(1)}, bf16[96,2048]{1,0:T(8,128)(2,1)S(1)}, u32[]{:S(2)}, u32[]{:S(2)}) collective-permute-start(bf16[96,2048]{1,0:T(8,128)(2,1)S(1)} %collective-permute-done.20.refs_6_.refs_7_), channel_id=1, source_target_pairs={{0,4},{1,5},{2,6},{3,7},{4,8},{5,9},{6,10},{7,11},{8,12},{9,13},{1... | collective-permute-start | bytes 1179656 | tf_op jit(solution)/shard_map/cond/branch_1_fun/gather_z/ppermute | solution.py:24
  132.4 5.1 %collective-permute-start.18 = (bf16[96,2048]{1,0:T(8,128)(2,1)S(1)}, bf16[96,2048]{1,0:T(8,128)(2,1)S(1)}, u32[]{:S(2)}, u32[]{:S(2)}) collective-permute-start(bf16[96,2048]{1,0:T(8,128)(2,1)S(1)} %collective-permute-done.17.refs_2_.refs_3_), channel_id=1, source_target_pairs={{0,28},{1,29},{2,30},{3,31},{4,0},{5,1},{6,2},{7,3},{8,4},{9,5},{1... | collective-permute-start | bytes 1179656 | tf_op jit(solution)/shard_map/cond/branch_1_fun/gather_z/ppermute | solution.py:24
  137.5 5.0 %collective-permute-done.22.refs_5_.refs_6_ = bf16[96,2048]{1,0:T(8,128)(2,1)S(1)} collective-permute-done((bf16[96,2048]{1,0:T(8,128)(2,1)S(1)}, bf16[96,2048]{1,0:T(8,128)(2,1)S(1)}, u32[]{:S(2)}, u32[]{:S(2)}) %collective-permute-start.22) | collective-permute-done | bytes 393248 | tf_op jit(solution)/shard_map/cond/branch_1_fun/gather_z/ppermute | solution.py:24
  142.5 1.9 %collective-permute-start.23 = (bf16[96,2048]{1,0:T(8,128)(2,1)S(1)}, bf16[96,2048]{1,0:T(8,128)(2,1)S(1)}, u32[]{:S(2)}, u32[]{:S(2)}) collective-permute-start(bf16[96,2048]{1,0:T(8,128)(2,1)S(1)} %collective-permute-done.22.refs_5_.refs_6_), channel_id=1, source_target_pairs={{0,4},{1,5},{2,6},{3,7},{4,8},{5,9},{6,10},{7,11},{8,12},{9,13},{1... | collective-permute-start | bytes 1179656 | tf_op jit(solution)/shard_map/cond/branch_1_fun/gather_z/ppermute | solution.py:24
  144.4 9.2 %collective-permute-done.23.refs_4_.refs_5_ = bf16[96,2048]{1,0:T(8,128)(2,1)S(1)} collective-permute-done((bf16[96,2048]{1,0:T(8,128)(2,1)S(1)}, bf16[96,2048]{1,0:T(8,128)(2,1)S(1)}, u32[]{:S(2)}, u32[]{:S(2)}) %collective-permute-start.23) | collective-permute-done | bytes 393248 | tf_op jit(solution)/shard_map/cond/branch_1_fun/gather_z/ppermute | solution.py:24
  153.6 0.7 copy-done.38
  154.4 2.5 %moment.12 = bf16[128,1024]{1,0:T(8,128)(2,1)} custom-call(bf16[768,128]{1,0:T(8,128)(2,1)S(1)} %bitcast.96, bf16[96,2048]{1,0:T(8,128)(2,1)} %copy-done.3, bf16[96,2048]{1,0:T(8,128)(2,1)} %copy-done.13, bf16[96,2048]{1,0:T(8,128)(2,1)} %copy-done.23, bf16[96,2048]{1,0:T(8,128)(2,1)} %copy-done.33, bf16[96,2048]{1,0:T(8,128)(2,1)} %copy-done.38, ...), custom_call_target="tpu_custom_call" | custom-call | flops 201326592 | bytes 2097152 | tf_op jit(solution)/shard_map/cond/branch_1_fun/moment/pallas_call | solution.py:64
  156.9 3.2 %collective-permute-start.24 = (bf16[128,1024]{1,0:T(8,128)(2,1)}, bf16[128,1024]{1,0:T(8,128)(2,1)S(1)}, u32[]{:S(2)}, u32[]{:S(2)}) collective-permute-start(bf16[128,1024]{1,0:T(8,128)(2,1)} %moment.12), channel_id=1, source_target_pairs={{0,64},{32,96},{64,128},{96,160},{128,192},{160,224},{192,256},{22... | collective-permute-start | bytes 786440 | tf_op jit(solution)/shard_map/cond/branch_1_fun/partner/ppermute | solution.py:34
  160.1 2.6 %moment.13 = bf16[128,1024]{1,0:T(8,128)(2,1)} custom-call(bf16[768,128]{1,0:T(8,128)(2,1)S(1)} %bitcast.97, bf16[96,2048]{1,0:T(8,128)(2,1)} %copy-done.3, bf16[96,2048]{1,0:T(8,128)(2,1)} %copy-done.13, bf16[96,2048]{1,0:T(8,128)(2,1)} %copy-done.23, bf16[96,2048]{1,0:T(8,128)(2,1)} %copy-done.33, bf16[96,2048]{1,0:T(8,128)(2,1)} %copy-done.38, ...), custom_call_target="tpu_custom_call" | custom-call | flops 201326592 | bytes 2097152 | tf_op jit(solution)/shard_map/cond/branch_1_fun/moment/pallas_call | solution.py:64
  162.7 5.7 %collective-permute-start.25 = (bf16[128,1024]{1,0:T(8,128)(2,1)}, bf16[128,1024]{1,0:T(8,128)(2,1)S(1)}, u32[]{:S(2)}, u32[]{:S(2)}) collective-permute-start(bf16[128,1024]{1,0:T(8,128)(2,1)} %moment.13), channel_id=1, source_target_pairs={{0,64},{32,96},{64,128},{96,160},{128,192},{160,224},{192,256},{22... | collective-permute-start | bytes 786440 | tf_op jit(solution)/shard_map/cond/branch_1_fun/partner/ppermute | solution.py:34
  168.4 3.3 %back.6 = bf16[32,24,128]{2,1,0:T(8,128)(2,1)S(1)} custom-call(s32[2]{0:T(128)S(1)} %get-tuple-element.70.place_ref, bf16[96,2048]{1,0:T(8,128)(2,1)} %copy-done.3, bf16[96,2048]{1,0:T(8,128)(2,1)} %copy-done.13, bf16[96,2048]{1,0:T(8,128)(2,1)} %copy-done.23, bf16[96,2048]{1,0:T(8,128)(2,1)} %copy-done.33, bf16[96,2048]{1,0:T(8,128)(2,1)} %copy-done.38, ...), custom_call_target="tpu_custom_call" | custom-call | flops 402653184 | bytes 3145728 | tf_op jit(solution)/shard_map/cond/branch_1_fun/back/back/pallas_call | solution.py:174
  171.7 7.4 %collective-permute-done.24 = bf16[128,1024]{1,0:T(8,128)(2,1)S(1)} collective-permute-done((bf16[128,1024]{1,0:T(8,128)(2,1)}, bf16[128,1024]{1,0:T(8,128)(2,1)S(1)}, u32[]{:S(2)}, u32[]{:S(2)}) %collective-permute-start.24) | collective-permute-done | bytes 262176 | tf_op jit(solution)/shard_map/cond/branch_1_fun/partner/ppermute | solution.py:34
  179.2 4.3 %collective-permute-done.25 = bf16[128,1024]{1,0:T(8,128)(2,1)S(1)} collective-permute-done((bf16[128,1024]{1,0:T(8,128)(2,1)}, bf16[128,1024]{1,0:T(8,128)(2,1)S(1)}, u32[]{:S(2)}, u32[]{:S(2)}) %collective-permute-start.25) | collective-permute-done | bytes 262176 | tf_op jit(solution)/shard_map/cond/branch_1_fun/partner/ppermute | solution.py:34
  183.4 0.5 multiply_convert_fusion.3
  183.9 0.1 maximum_bitcast_fusion.2
  184.3 0.8 copy-done.62
  185.0 0.2 copy-done.63
  (49 shorter events, 0.3 us)
Async XLA Ops:
  0.6 24.4 %copy-start = (bf16[1,128,2048]{2,1,0:T(8,128)(2,1)S(1)}, bf16[1,128,2048]{2,1,0:T(8,128)(2,1)}, u32[]{:S(2)}) copy-start(bf16[1,128,2048]{2,1,0:T(8,128)(2,1)} %param.12) | copy-start | bytes 1572868
  3.1 26.4 %collective-permute-start.65 = (bf16[96,2048]{1,0:T(8,128)(2,1)S(1)}, bf16[96,2048]{1,0:T(8,128)(2,1)S(1)}, u32[]{:S(2)}, u32[]{:S(2)}) collective-permute-start(bf16[96,2048]{1,0:T(8,128)(2,1)S(1)} %fusion.60), channel_id=1, source_target_pairs={{0,4},{1,5},{2,6},{3,7},{4,8},{5,9},{6,10},{7,11},{8,12},{9,13},{1... | collective-permute-start | bytes 1179656 | tf_op jit(solution)/shard_map/sum_z/ppermute | solution.py:24
  9.6 22.4 %collective-permute-start.69 = (bf16[96,2048]{1,0:T(8,128)(2,1)S(1)}, bf16[96,2048]{1,0:T(8,128)(2,1)S(1)}, u32[]{:S(2)}, u32[]{:S(2)}) collective-permute-start(bf16[96,2048]{1,0:T(8,128)(2,1)S(1)} %fusion.61), channel_id=1, source_target_pairs={{0,28},{1,29},{2,30},{3,31},{4,0},{5,1},{6,2},{7,3},{8,4},{9,5},{1... | collective-permute-start | bytes 1179656 | tf_op jit(solution)/shard_map/sum_z/ppermute | solution.py:24
  29.8 13.4 %collective-permute-start.66 = (bf16[96,2048]{1,0:T(8,128)(2,1)S(1)}, bf16[96,2048]{1,0:T(8,128)(2,1)S(1)}, u32[]{:S(2)}, u32[]{:S(2)}) collective-permute-start(bf16[96,2048]{1,0:T(8,128)(2,1)S(1)} %add_convert_fusion.4), channel_id=1, source_target_pairs={{0,4},{1,5},{2,6},{3,7},{4,8},{5,9},{6,10},{7,11},{8,12},{9,13},{1... | collective-permute-start | bytes 1179656 | tf_op jit(solution)/shard_map/sum_z/ppermute | solution.py:24
  32.0 25.9 %copy-start.65 = (s32[1,768]{1,0:T(1,128)S(1)}, s32[1,768]{1,0:T(1,128)}, u32[]{:S(2)}) copy-start(s32[1,768]{1,0:T(1,128)} %param.15) | copy-start | bytes 9220
  32.3 13.1 %collective-permute-start.70 = (bf16[96,2048]{1,0:T(8,128)(2,1)S(1)}, bf16[96,2048]{1,0:T(8,128)(2,1)S(1)}, u32[]{:S(2)}, u32[]{:S(2)}) collective-permute-start(bf16[96,2048]{1,0:T(8,128)(2,1)S(1)} %add_convert_fusion.1), channel_id=1, source_target_pairs={{0,28},{1,29},{2,30},{3,31},{4,0},{5,1},{6,2},{7,3},{8,4},{9,5},{1... | collective-permute-start | bytes 1179656 | tf_op jit(solution)/shard_map/sum_z/ppermute | solution.py:24
  43.3 12.5 %collective-permute-start.67 = (bf16[96,2048]{1,0:T(8,128)(2,1)S(1)}, bf16[96,2048]{1,0:T(8,128)(2,1)S(1)}, u32[]{:S(2)}, u32[]{:S(2)}) collective-permute-start(bf16[96,2048]{1,0:T(8,128)(2,1)S(1)} %add_convert_fusion.3), channel_id=1, source_target_pairs={{0,4},{1,5},{2,6},{3,7},{4,8},{5,9},{6,10},{7,11},{8,12},{9,13},{1... | collective-permute-start | bytes 1179656 | tf_op jit(solution)/shard_map/sum_z/ppermute | solution.py:24
  45.5 13.0 %collective-permute-start.71 = (bf16[96,2048]{1,0:T(8,128)(2,1)S(1)}, bf16[96,2048]{1,0:T(8,128)(2,1)S(1)}, u32[]{:S(2)}, u32[]{:S(2)}) collective-permute-start(bf16[96,2048]{1,0:T(8,128)(2,1)S(1)} %add_convert_fusion), channel_id=1, source_target_pairs={{0,28},{1,29},{2,30},{3,31},{4,0},{5,1},{6,2},{7,3},{8,4},{9,5},{1... | collective-permute-start | bytes 1179656 | tf_op jit(solution)/shard_map/sum_z/ppermute | solution.py:24
  55.9 27.8 %copy-start.1 = (bf16[1,128,2048]{2,1,0:T(8,128)(2,1)S(1)}, bf16[1,128,2048]{2,1,0:T(8,128)(2,1)}, u32[]{:S(2)}) copy-start(bf16[1,128,2048]{2,1,0:T(8,128)(2,1)} %param.13) | copy-start | bytes 1572868
  55.9 11.7 %collective-permute-start.68 = (bf16[96,2048]{1,0:T(8,128)(2,1)S(1)}, bf16[96,2048]{1,0:T(8,128)(2,1)S(1)}, u32[]{:S(2)}, u32[]{:S(2)}) collective-permute-start(bf16[96,2048]{1,0:T(8,128)(2,1)S(1)} %add_convert_fusion.2), channel_id=1, source_target_pairs={{0,4},{1,5},{2,6},{3,7},{4,8},{5,9},{6,10},{7,11},{8,12},{9,13},{1... | collective-permute-start | bytes 1179656 | tf_op jit(solution)/shard_map/sum_z/ppermute | solution.py:24
  67.7 10.8 %collective-permute-start.72 = (bf16[24,2048]{1,0:T(8,128)(2,1)S(1)}, bf16[24,2048]{1,0:T(8,128)(2,1)S(1)}, u32[]{:S(2)}, u32[]{:S(2)}) collective-permute-start(bf16[24,2048]{1,0:T(8,128)(2,1)S(1)} %get-tuple-element.142), channel_id=1, source_target_pairs={{0,1},{1,0},{2,3},{3,2},{4,5},{5,4},{6,7},{7,6},{8,9},{9,8},{10,11... | collective-permute-start | bytes 294920 | tf_op jit(solution)/shard_map/sum_x/ppermute | solution.py:29
  70.2 9.9 %collective-permute-start.74 = (bf16[24,2048]{1,0:T(8,128)(2,1)S(1)}, bf16[24,2048]{1,0:T(8,128)(2,1)S(1)}, u32[]{:S(2)}, u32[]{:S(2)}) collective-permute-start(bf16[24,2048]{1,0:T(8,128)(2,1)S(1)} %get-tuple-element.143), channel_id=1, source_target_pairs={{0,3},{1,2},{2,1},{3,0},{4,7},{5,6},{6,5},{7,4},{8,11},{9,10},{10,... | collective-permute-start | bytes 294920 | tf_op jit(solution)/shard_map/sum_x/ppermute | solution.py:29
  74.6 7.5 %collective-permute-start.73 = (bf16[24,2048]{1,0:T(8,128)(2,1)S(1)}, bf16[24,2048]{1,0:T(8,128)(2,1)S(1)}, u32[]{:S(2)}, u32[]{:S(2)}) collective-permute-start(bf16[24,2048]{1,0:T(8,128)(2,1)S(1)} %get-tuple-element.144), channel_id=1, source_target_pairs={{0,2},{1,3},{2,0},{3,1},{4,6},{5,7},{6,4},{7,5},{8,10},{9,11},{10,... | collective-permute-start | bytes 294920 | tf_op jit(solution)/shard_map/sum_x/ppermute | solution.py:29
  83.7 15.1 %collective-permute-start.15 = (bf16[24,2048]{1,0:T(8,128)(2,1)S(1)}, bf16[24,2048]{1,0:T(8,128)(2,1)S(1)}, u32[]{:S(2)}, u32[]{:S(2)}) collective-permute-start(bf16[24,2048]{1,0:T(8,128)(2,1)S(1)} %get-tuple-element.71), channel_id=1, source_target_pairs={{0,3},{1,2},{2,1},{3,0},{4,7},{5,6},{6,5},{7,4},{8,11},{9,10},{10,... | collective-permute-start | bytes 294920 | tf_op jit(solution)/shard_map/cond/branch_1_fun/gather_x/ppermute | solution.py:29
  86.0 12.7 %collective-permute-start.14 = (bf16[24,2048]{1,0:T(8,128)(2,1)S(1)}, bf16[24,2048]{1,0:T(8,128)(2,1)S(1)}, u32[]{:S(2)}, u32[]{:S(2)}) collective-permute-start(bf16[24,2048]{1,0:T(8,128)(2,1)S(1)} %get-tuple-element.71), channel_id=1, source_target_pairs={{0,2},{1,3},{2,0},{3,1},{4,6},{5,7},{6,4},{7,5},{8,10},{9,11},{10,... | collective-permute-start | bytes 294920 | tf_op jit(solution)/shard_map/cond/branch_1_fun/gather_x/ppermute | solution.py:29
  92.2 6.5 %collective-permute-start.13 = (bf16[24,2048]{1,0:T(8,128)(2,1)S(1)}, bf16[24,2048]{1,0:T(8,128)(2,1)S(1)}, u32[]{:S(2)}, u32[]{:S(2)}) collective-permute-start(bf16[24,2048]{1,0:T(8,128)(2,1)S(1)} %get-tuple-element.71), channel_id=1, source_target_pairs={{0,1},{1,0},{2,3},{3,2},{4,5},{5,4},{6,7},{7,6},{8,9},{9,8},{10,11... | collective-permute-start | bytes 294920 | tf_op jit(solution)/shard_map/cond/branch_1_fun/gather_x/ppermute | solution.py:29
  98.8 55.5 %copy-start.3 = (bf16[96,2048]{1,0:T(8,128)(2,1)}, bf16[96,2048]{1,0:T(8,128)(2,1)S(1)}, u32[]{:S(2)}) copy-start(bf16[96,2048]{1,0:T(8,128)(2,1)S(1)} %constant_dynamic-update-slice_fusion.4.refs_0_.refs_1_) | copy-start | bytes 1179652 | tf_op jit(solution)/shard_map/cond
  98.8 12.1 %collective-permute-start.19 = (bf16[96,2048]{1,0:T(8,128)(2,1)S(1)}, bf16[96,2048]{1,0:T(8,128)(2,1)S(1)}, u32[]{:S(2)}, u32[]{:S(2)}) collective-permute-start(bf16[96,2048]{1,0:T(8,128)(2,1)S(1)} %constant_dynamic-update-slice_fusion.4.refs_0_.refs_1_), channel_id=1, source_target_pairs={{0,4},{1,5},{2,6},{3,7},{4,8},{5,9},{6,10},{7,11},{8,12},{9,13},{1... | collective-permute-start | bytes 1179656 | tf_op jit(solution)/shard_map/cond/branch_1_fun/gather_z/ppermute | solution.py:24
  100.7 28.9 %collective-permute-start.21 = (bf16[128,2048]{1,0:T(8,128)(2,1)S(1)}, bf16[128,2048]{1,0:T(8,128)(2,1)S(1)}, u32[]{:S(2)}, u32[]{:S(2)}) collective-permute-start(bf16[128,2048]{1,0:T(8,128)(2,1)S(1)} %get-tuple-element.72.refs_8_), channel_id=1, source_target_pairs={{0,64},{32,96},{64,128},{96,160},{128,192},{160,224},{192,256},{22... | collective-permute-start | bytes 1572872 | tf_op jit(solution)/shard_map/cond/branch_1_fun/early_partner/ppermute | solution.py:34
  105.8 10.5 %collective-permute-start.16 = (bf16[96,2048]{1,0:T(8,128)(2,1)S(1)}, bf16[96,2048]{1,0:T(8,128)(2,1)S(1)}, u32[]{:S(2)}, u32[]{:S(2)}) collective-permute-start(bf16[96,2048]{1,0:T(8,128)(2,1)S(1)} %constant_dynamic-update-slice_fusion.4.refs_0_.refs_1_), channel_id=1, source_target_pairs={{0,28},{1,29},{2,30},{3,31},{4,0},{5,1},{6,2},{7,3},{8,4},{9,5},{1... | collective-permute-start | bytes 1179656 | tf_op jit(solution)/shard_map/cond/branch_1_fun/gather_z/ppermute | solution.py:24
  110.9 43.4 %copy-start.8 = (bf16[96,2048]{1,0:T(8,128)(2,1)}, bf16[96,2048]{1,0:T(8,128)(2,1)S(1)}, u32[]{:S(2)}) copy-start(bf16[96,2048]{1,0:T(8,128)(2,1)S(1)} %collective-permute-done.19.refs_7_.refs_8_) | copy-start | bytes 1179652 | tf_op jit(solution)/shard_map/cond
  110.9 19.5 %collective-permute-start.20 = (bf16[96,2048]{1,0:T(8,128)(2,1)S(1)}, bf16[96,2048]{1,0:T(8,128)(2,1)S(1)}, u32[]{:S(2)}, u32[]{:S(2)}) collective-permute-start(bf16[96,2048]{1,0:T(8,128)(2,1)S(1)} %collective-permute-done.19.refs_7_.refs_8_), channel_id=1, source_target_pairs={{0,4},{1,5},{2,6},{3,7},{4,8},{5,9},{6,10},{7,11},{8,12},{9,13},{1... | collective-permute-start | bytes 1179656 | tf_op jit(solution)/shard_map/cond/branch_1_fun/gather_z/ppermute | solution.py:24
  116.3 38.1 %copy-start.13 = (bf16[96,2048]{1,0:T(8,128)(2,1)}, bf16[96,2048]{1,0:T(8,128)(2,1)S(1)}, u32[]{:S(2)}) copy-start(bf16[96,2048]{1,0:T(8,128)(2,1)S(1)} %collective-permute-done.16.refs_1_.refs_2_) | copy-start | bytes 1179652 | tf_op jit(solution)/shard_map/cond
  116.3 16.1 %collective-permute-start.17 = (bf16[96,2048]{1,0:T(8,128)(2,1)S(1)}, bf16[96,2048]{1,0:T(8,128)(2,1)S(1)}, u32[]{:S(2)}, u32[]{:S(2)}) collective-permute-start(bf16[96,2048]{1,0:T(8,128)(2,1)S(1)} %collective-permute-done.16.refs_1_.refs_2_), channel_id=1, source_target_pairs={{0,28},{1,29},{2,30},{3,31},{4,0},{5,1},{6,2},{7,3},{8,4},{9,5},{1... | collective-permute-start | bytes 1179656 | tf_op jit(solution)/shard_map/cond/branch_1_fun/gather_z/ppermute | solution.py:24
  129.6 0.8 copy-start.54
  130.4 23.9 %copy-start.18 = (bf16[96,2048]{1,0:T(8,128)(2,1)}, bf16[96,2048]{1,0:T(8,128)(2,1)S(1)}, u32[]{:S(2)}) copy-start(bf16[96,2048]{1,0:T(8,128)(2,1)S(1)} %collective-permute-done.20.refs_6_.refs_7_) | copy-start | bytes 1179652 | tf_op jit(solution)/shard_map/cond
  130.4 12.0 %collective-permute-start.22 = (bf16[96,2048]{1,0:T(8,128)(2,1)S(1)}, bf16[96,2048]{1,0:T(8,128)(2,1)S(1)}, u32[]{:S(2)}, u32[]{:S(2)}) collective-permute-start(bf16[96,2048]{1,0:T(8,128)(2,1)S(1)} %collective-permute-done.20.refs_6_.refs_7_), channel_id=1, source_target_pairs={{0,4},{1,5},{2,6},{3,7},{4,8},{5,9},{6,10},{7,11},{8,12},{9,13},{1... | collective-permute-start | bytes 1179656 | tf_op jit(solution)/shard_map/cond/branch_1_fun/gather_z/ppermute | solution.py:24
  132.4 22.0 %copy-start.23 = (bf16[96,2048]{1,0:T(8,128)(2,1)}, bf16[96,2048]{1,0:T(8,128)(2,1)S(1)}, u32[]{:S(2)}) copy-start(bf16[96,2048]{1,0:T(8,128)(2,1)S(1)} %collective-permute-done.17.refs_2_.refs_3_) | copy-start | bytes 1179652 | tf_op jit(solution)/shard_map/cond
  132.4 12.0 %collective-permute-start.18 = (bf16[96,2048]{1,0:T(8,128)(2,1)S(1)}, bf16[96,2048]{1,0:T(8,128)(2,1)S(1)}, u32[]{:S(2)}, u32[]{:S(2)}) collective-permute-start(bf16[96,2048]{1,0:T(8,128)(2,1)S(1)} %collective-permute-done.17.refs_2_.refs_3_), channel_id=1, source_target_pairs={{0,28},{1,29},{2,30},{3,31},{4,0},{5,1},{6,2},{7,3},{8,4},{9,5},{1... | collective-permute-start | bytes 1179656 | tf_op jit(solution)/shard_map/cond/branch_1_fun/gather_z/ppermute | solution.py:24
  142.5 1.9 %copy-start.28 = (bf16[96,2048]{1,0:T(8,128)(2,1)}, bf16[96,2048]{1,0:T(8,128)(2,1)S(1)}, u32[]{:S(2)}) copy-start(bf16[96,2048]{1,0:T(8,128)(2,1)S(1)} %collective-permute-done.22.refs_5_.refs_6_) | copy-start | bytes 1179652 | tf_op jit(solution)/shard_map/cond
  142.5 11.1 %collective-permute-start.23 = (bf16[96,2048]{1,0:T(8,128)(2,1)S(1)}, bf16[96,2048]{1,0:T(8,128)(2,1)S(1)}, u32[]{:S(2)}, u32[]{:S(2)}) collective-permute-start(bf16[96,2048]{1,0:T(8,128)(2,1)S(1)} %collective-permute-done.22.refs_5_.refs_6_), channel_id=1, source_target_pairs={{0,4},{1,5},{2,6},{3,7},{4,8},{5,9},{6,10},{7,11},{8,12},{9,13},{1... | collective-permute-start | bytes 1179656 | tf_op jit(solution)/shard_map/cond/branch_1_fun/gather_z/ppermute | solution.py:24
  144.4 9.2 %copy-start.33 = (bf16[96,2048]{1,0:T(8,128)(2,1)}, bf16[96,2048]{1,0:T(8,128)(2,1)S(1)}, u32[]{:S(2)}) copy-start(bf16[96,2048]{1,0:T(8,128)(2,1)S(1)} %collective-permute-done.18.refs_3_.refs_4_) | copy-start | bytes 1179652 | tf_op jit(solution)/shard_map/cond
  153.6 0.8 copy-start.38
  156.9 26.5 %copy-start.43 = (bf16[128,1024]{1,0:T(8,128)(2,1)S(1)}, bf16[128,1024]{1,0:T(8,128)(2,1)}, u32[]{:S(2)}) copy-start(bf16[128,1024]{1,0:T(8,128)(2,1)} %moment.12) | copy-start | bytes 786436 | tf_op jit(solution)/shard_map/cond
  156.9 26.5 %copy-start.55 = (bf16[128,2048]{1,0:T(8,128)(2,1)S(1)}, bf16[128,2048]{1,0:T(8,128)(2,1)}, u32[]{:S(2)}) copy-start(bf16[128,2048]{1,0:T(8,128)(2,1)} %copy-done.54) | copy-start | bytes 1572868 | tf_op jit(solution)/shard_map/cond
  156.9 22.3 %collective-permute-start.24 = (bf16[128,1024]{1,0:T(8,128)(2,1)}, bf16[128,1024]{1,0:T(8,128)(2,1)S(1)}, u32[]{:S(2)}, u32[]{:S(2)}) collective-permute-start(bf16[128,1024]{1,0:T(8,128)(2,1)} %moment.12), channel_id=1, source_target_pairs={{0,64},{32,96},{64,128},{96,160},{128,192},{160,224},{192,256},{22... | collective-permute-start | bytes 786440 | tf_op jit(solution)/shard_map/cond/branch_1_fun/partner/ppermute | solution.py:34
  162.7 20.7 %copy-start.48 = (bf16[128,1024]{1,0:T(8,128)(2,1)S(1)}, bf16[128,1024]{1,0:T(8,128)(2,1)}, u32[]{:S(2)}) copy-start(bf16[128,1024]{1,0:T(8,128)(2,1)} %moment.13) | copy-start | bytes 786436 | tf_op jit(solution)/shard_map/cond
  162.7 20.7 %collective-permute-start.25 = (bf16[128,1024]{1,0:T(8,128)(2,1)}, bf16[128,1024]{1,0:T(8,128)(2,1)S(1)}, u32[]{:S(2)}, u32[]{:S(2)}) collective-permute-start(bf16[128,1024]{1,0:T(8,128)(2,1)} %moment.13), channel_id=1, source_target_pairs={{0,64},{32,96},{64,128},{96,160},{128,192},{160,224},{192,256},{22... | collective-permute-start | bytes 786440 | tf_op jit(solution)/shard_map/cond/branch_1_fun/partner/ppermute | solution.py:34
  184.3 0.8 copy-start.62
  184.3 1.0 copy-start.63
  184.3 1.0 copy-start.64

commit v3 on v2

--- a/solution.py
+++ b/solution.py
@@ -11,7 +11,6 @@
 BETA_MOM = 0.9
 STEP_RATE = 0.1
 NX = 4
-PARTS = 2
 SCALARS = pl.BlockSpec(memory_space=pltpu.SMEM)
 
 
@@ -19,9 +18,10 @@
     return [pl.BlockSpec(memory_space=pltpu.VMEM)] * count
 
 
-def shift_z(x, by):
-    size = lax.axis_size("tensor")
-    return lax.ppermute(x, "tensor", [(i, (i + by * NX) % size) for i in range(size)])
+def swap_z(x, odd):
+    size = lax.axis_size("tensor")
+    step = lambda i: -NX if (i // NX + odd) % 2 else NX
+    return lax.ppermute(x, "tensor", [(i, (i + step(i)) % size) for i in range(size)])
 
 
 def swap_x(x, k):
@@ -35,7 +35,7 @@
 
 
 def place_of(j, k, z, x, nz):
-    return lax.rem(z + j, nz) * NX + (x ^ k)
+    return lax.rem(z + (1 - 2 * lax.rem(z, 2)) * j + nz, nz) * NX + (x ^ k)
 
 
 def order_kernel(nz, place_ref, rows_ref, out_ref):
@@ -57,31 +57,38 @@
 
 def moment_of(heads, blocks, mom, scaling, part):
     nz, (rows, width) = len(blocks), blocks[0].shape
-    deep, cols = heads.shape[1], width // PARTS
+    deep, cols = heads.shape[1], width // 2
     tile = min(512, cols)
     first = part * cols // tile
     column = lambda n: pl.BlockSpec((n, tile), lambda i: (0, first + i))
+    own = lambda n: pl.BlockSpec((n, tile), lambda i: (0, i))
     return pl.pallas_call(
         partial(moment_kernel, scaling, nz),
         grid=(cols // tile,),
         out_shape=jax.ShapeDtypeStruct((deep, cols), jnp.bfloat16),
-        in_specs=[pl.BlockSpec(heads.shape, lambda i: (0, 0))] + [column(rows)] * nz + [column(deep)],
-        out_specs=pl.BlockSpec((deep, tile), lambda i: (0, i)),
+        in_specs=[pl.BlockSpec(heads.shape, lambda i: (0, 0))]
+        + [own(rows) if j == nz // 2 else column(rows) for j in range(nz)]
+        + [column(deep)],
+        out_specs=own(deep),
         scratch_shapes=[pltpu.VMEM((nz * rows, tile), jnp.bfloat16)],
         cost_estimate=pl.CostEstimate(
             flops=2 * heads.size * cols, bytes_accessed=2 * (nz * rows * cols + 2 * deep * cols), transcendentals=0
         ),
         name="moment",
-    )(heads, *blocks, mom)
+    )(heads, *[b[part] if isinstance(b, tuple) else b for b in blocks], mom)
 
 
 def back_kernel(scaling, nz, place_ref, *refs):
     w_ref, out_ref = refs[-2], refs[-1]
-    rows = out_ref.shape[1]
+    rows, half = out_ref.shape[1], w_ref.shape[1] // 2
+    times = lambda a, w: lax.dot_general(
+        a, w, (((1,), (1,)), ((), ())), preferred_element_type=jnp.float32
+    )
     for j in range(nz):
-        total = lax.dot_general(
-            refs[j][...], w_ref[...], (((1,), (1,)), ((), ())), preferred_element_type=jnp.float32
-        )
+        if j == nz // 2:
+            total = times(refs[j][...], w_ref[:, :half]) + times(refs[nz][...], w_ref[:, half:])
+        else:
+            total = times(refs[j][...], w_ref[...])
         for k in range(NX):
             out_ref[place_of(j, k, place_ref[0], place_ref[1], nz)] = (
                 total[k * rows : (k + 1) * rows] * scaling
@@ -117,17 +124,16 @@
         )
 
     with jax.named_scope("sum_z"):
-        total = share(0)
-        flows = [[1, nz // 2, None], [-1, nz // 2 - 1, None]]
-        for s in range(nz // 2):
-            for flow in flows:
-                way, steps, cur = flow
-                if s < steps:
-                    term = share(way * (steps - s))
-                    if cur is not None:
-                        term = term + cur.astype(jnp.float32)
-                    flow[2] = shift_z(term.astype(jnp.bfloat16), way)
-        total = total + flows[0][2].astype(jnp.float32) + flows[1][2].astype(jnp.float32)
+        half = weight.shape[1] // 2
+        term = share(nz // 2).astype(jnp.bfloat16)
+        even, odd = swap_z(term[:, :half], 0), swap_z(term[:, half:], 1)
+        even = jnp.pad(even.astype(jnp.float32), ((0, 0), (0, half)))
+        odd = jnp.pad(odd.astype(jnp.float32), ((0, 0), (half, 0)))
+        for m in range(nz // 2 - 1, 0, -1):
+            to_even = (share(m) + odd).astype(jnp.bfloat16)
+            to_odd = (share(-m) + even).astype(jnp.bfloat16)
+            even, odd = swap_z(to_even, 0).astype(jnp.float32), swap_z(to_odd, 1).astype(jnp.float32)
+        total = share(0) + even + odd
     with jax.named_scope("sum_x"):
         mine = total[:rows]
         for k in range(1, NX):
@@ -149,18 +155,17 @@
         block = jnp.concatenate([grad] + [swap_x(grad, k) for k in range(1, NX)], axis=0)
     with jax.named_scope("gather_z"):
         held = [block] + [None] * (nz - 1)
-        flows = [[1, nz // 2, block], [-1, nz // 2 - 1, block]]
-        for s in range(nz // 2):
-            for flow in flows:
-                way, steps, cur = flow
-                if s < steps:
-                    if s == nz // 2 - 2 and way == 1:
-                        cur, partner_w = lax.optimization_barrier((cur, partner_w))
-                    flow[2] = shift_z(cur, way)
-                    held[(-way * (s + 1)) % nz] = flow[2]
+        even = odd = block
+        half = width // 2
+        for m in range(1, nz // 2):
+            if m == nz // 2 - 1:
+                even, odd, partner_w = lax.optimization_barrier((even, odd, partner_w))
+            even, odd = swap_z(odd, 0), swap_z(even, 1)
+            held[m], held[-m] = even, odd
+        held[nz // 2] = (swap_z(even[:, :half], 1), swap_z(odd[:, half:], 0))
     new_w, new_m = [], []
-    cols = width // PARTS
-    for c in range(PARTS):
+    cols = width // 2
+    for c in range(2):
         part = slice(c * cols, (c + 1) * cols)
         moment = moment_of(heads, held, moment_in, scaling, c)
         with jax.named_scope("partner"):
@@ -174,13 +179,13 @@
         attn_grad = pl.pallas_call(
             partial(back_kernel, scaling, nz),
             out_shape=jax.ShapeDtypeStruct((size, rows, deep), jnp.bfloat16),
-            in_specs=[SCALARS] + vmem(nz + 1),
+            in_specs=[SCALARS] + vmem(nz + 2),
             out_specs=vmem(1)[0],
             cost_estimate=pl.CostEstimate(
                 flops=2 * tokens * width * deep, bytes_accessed=2 * tokens * width, transcendentals=0
             ),
             name="back",
-        )(place, *held, weight).reshape(tokens, deep)
+        )(place, *[h[0] if isinstance(h, tuple) else h for h in held], held[nz // 2][1], weight).reshape(tokens, deep)
     join = lambda pieces: jnp.concatenate(pieces, axis=1)
     return attn_grad, join(new_w), join(new_m)
 

time: 186 us -> 179 us (0.962)
  the two profiles are of different devices: /device:TPU:66 before, /device:TPU:64 now
where the time goes in v3:
time: 179 us; the launch traced here: 178 us
  starting transfers between devices  88.3 us (49%)
  waiting for transfers between devices  65.4 us (37%)
  Pallas kernels  9.41 us (5%)
  matrix products  6.36 us (4%)
  local copies, waits for them, and re-layouts  3.3 us (2%)
  other arithmetic  2.85 us (2%)
    ppermute x16, starting transfers between devices, swap_z(): lax.ppermute(x, 'tensor', [(i, (i + step(i)) % size) for i in range(size)])  60.5 us
    ppermute x16, waiting for transfers between devices, swap_z(): lax.ppermute(x, 'tensor', [(i, (i + step(i)) % size) for i in range(size)])  40.5 us
    ppermute x6, starting transfers between devices, swap_x(): return lax.ppermute(x, 'tensor', [(i, i ^ k) for i in range(size)])  19.7 us
    ppermute x3, waiting for transfers between devices, pass_replica(): lax.ppermute(x, 'replica', [(i, (i + by) % size) for i in range(size)])  16.5 us
    ppermute x6, waiting for transfers between devices, swap_x(): return lax.ppermute(x, 'tensor', [(i, i ^ k) for i in range(size)])  8.39 us
    ppermute x3, starting transfers between devices, pass_replica(): lax.ppermute(x, 'replica', [(i, (i + by) % size) for i in range(size)])  8.03 us
    dot_general x8, matrix products, share(): jnp.dot(heads[j * chunk:(j + 1) * chunk], weight, preferred_element_type=...  6.36 us
    pallas_call x2, Pallas kernels, moment_of(): pl.pallas_call(partial(moment_kernel, scaling, nz), grid=(cols // tile,),...  5.08 us
  transfers between devices with their start and end apart: 25, of which 17 were waited for; matrix products, arithmetic and copies ran while one was open for 4% of the time, Pallas kernels for 5%

profile of v3, /device:TPU:64, one launch (start us, length us, event | category | flops | bytes accessed | tf_op | source)
XLA Modules:
  0.0 177.8 jit_solution(14532079195285643691)
XLA Ops:
  0.7 1.0 order.1
  1.8 0.6 fusion.76
  2.4 1.3 fusion.60
  3.8 17.3 %collective-permute-start.70 = (bf16[96,1024]{1,0:T(8,128)(2,1)S(1)}, bf16[96,1024]{1,0:T(8,128)(2,1)S(1)}, u32[]{:S(2)}, u32[]{:S(2)}) collective-permute-start(bf16[96,1024]{1,0:T(8,128)(2,1)S(1)} %get-tuple-element.150), channel_id=1, source_target_pairs={{0,28},{1,29},{2,30},{3,31},{4,8},{5,9},{6,10},{7,11},{8,4},{9,5},... | collective-permute-start | bytes 589832 | tf_op jit(solution)/shard_map/sum_z/ppermute | solution.py:24
  21.1 1.9 %collective-permute-start.74 = (bf16[96,1024]{1,0:T(8,128)(2,1)S(1)}, bf16[96,1024]{1,0:T(8,128)(2,1)S(1)}, u32[]{:S(2)}, u32[]{:S(2)}) collective-permute-start(bf16[96,1024]{1,0:T(8,128)(2,1)S(1)} %get-tuple-element.151), channel_id=1, source_target_pairs={{0,4},{1,5},{2,6},{3,7},{4,0},{5,1},{6,2},{7,3},{8,12},{9,13},{10,... | collective-permute-start | bytes 589832 | tf_op jit(solution)/shard_map/sum_z/ppermute | solution.py:24
  23.0 1.3 convolution_multiply_fusion.1
  24.3 1.0 convolution_multiply_fusion.2
  25.4 1.0 convolution_multiply_fusion.5
  26.4 3.0 %collective-permute-done.74 = bf16[96,1024]{1,0:T(8,128)(2,1)S(1)} collective-permute-done((bf16[96,1024]{1,0:T(8,128)(2,1)S(1)}, bf16[96,1024]{1,0:T(8,128)(2,1)S(1)}, u32[]{:S(2)}, u32[]{:S(2)}) %collective-permute-start.74) | collective-permute-done | bytes 196640 | tf_op jit(solution)/shard_map/sum_z/ppermute | solution.py:24
  29.4 0.3 add_convert_fusion.2
  29.6 2.2 %collective-permute-start.75 = (bf16[96,2048]{1,0:T(8,128)(2,1)S(1)}, bf16[96,2048]{1,0:T(8,128)(2,1)S(1)}, u32[]{:S(2)}, u32[]{:S(2)}) collective-permute-start(bf16[96,2048]{1,0:T(8,128)(2,1)S(1)} %add_convert_fusion.2), channel_id=1, source_target_pairs={{0,28},{1,29},{2,30},{3,31},{4,8},{5,9},{6,10},{7,11},{8,4},{9,5},... | collective-permute-start | bytes 1179656 | tf_op jit(solution)/shard_map/sum_z/ppermute | solution.py:24
  31.8 1.0 convolution_multiply_fusion.6
  32.9 0.3 add_convert_fusion.5
  33.1 1.9 %collective-permute-start.71 = (bf16[96,2048]{1,0:T(8,128)(2,1)S(1)}, bf16[96,2048]{1,0:T(8,128)(2,1)S(1)}, u32[]{:S(2)}, u32[]{:S(2)}) collective-permute-start(bf16[96,2048]{1,0:T(8,128)(2,1)S(1)} %add_convert_fusion.5), channel_id=1, source_target_pairs={{0,4},{1,5},{2,6},{3,7},{4,0},{5,1},{6,2},{7,3},{8,12},{9,13},{10,... | collective-permute-start | bytes 1179656 | tf_op jit(solution)/shard_map/sum_z/ppermute | solution.py:24
  35.1 7.3 %collective-permute-done.75 = bf16[96,2048]{1,0:T(8,128)(2,1)S(1)} collective-permute-done((bf16[96,2048]{1,0:T(8,128)(2,1)S(1)}, bf16[96,2048]{1,0:T(8,128)(2,1)S(1)}, u32[]{:S(2)}, u32[]{:S(2)}) %collective-permute-start.75) | collective-permute-done | bytes 393248 | tf_op jit(solution)/shard_map/sum_z/ppermute | solution.py:24
  42.5 1.9 %collective-permute-start.76 = (bf16[96,2048]{1,0:T(8,128)(2,1)S(1)}, bf16[96,2048]{1,0:T(8,128)(2,1)S(1)}, u32[]{:S(2)}, u32[]{:S(2)}) collective-permute-start(bf16[96,2048]{1,0:T(8,128)(2,1)S(1)} %add_convert_fusion.1), channel_id=1, source_target_pairs={{0,4},{1,5},{2,6},{3,7},{4,0},{5,1},{6,2},{7,3},{8,12},{9,13},{10,... | collective-permute-start | bytes 1179656 | tf_op jit(solution)/shard_map/sum_z/ppermute | solution.py:24
  44.4 0.3 collective-permute-done.71
  44.8 6.2 %collective-permute-start.72 = (bf16[96,2048]{1,0:T(8,128)(2,1)S(1)}, bf16[96,2048]{1,0:T(8,128)(2,1)S(1)}, u32[]{:S(2)}, u32[]{:S(2)}) collective-permute-start(bf16[96,2048]{1,0:T(8,128)(2,1)S(1)} %add_convert_fusion.4), channel_id=1, source_target_pairs={{0,28},{1,29},{2,30},{3,31},{4,8},{5,9},{6,10},{7,11},{8,4},{9,5},... | collective-permute-start | bytes 1179656 | tf_op jit(solution)/shard_map/sum_z/ppermute | solution.py:24
  51.0 2.1 %collective-permute-done.76 = bf16[96,2048]{1,0:T(8,128)(2,1)S(1)} collective-permute-done((bf16[96,2048]{1,0:T(8,128)(2,1)S(1)}, bf16[96,2048]{1,0:T(8,128)(2,1)S(1)}, u32[]{:S(2)}, u32[]{:S(2)}) %collective-permute-start.76) | collective-permute-done | bytes 393248 | tf_op jit(solution)/shard_map/sum_z/ppermute | solution.py:24
  53.2 4.5 %collective-permute-start.77 = (bf16[96,2048]{1,0:T(8,128)(2,1)S(1)}, bf16[96,2048]{1,0:T(8,128)(2,1)S(1)}, u32[]{:S(2)}, u32[]{:S(2)}) collective-permute-start(bf16[96,2048]{1,0:T(8,128)(2,1)S(1)} %add_convert_fusion), channel_id=1, source_target_pairs={{0,28},{1,29},{2,30},{3,31},{4,8},{5,9},{6,10},{7,11},{8,4},{9,5},... | collective-permute-start | bytes 1179656 | tf_op jit(solution)/shard_map/sum_z/ppermute | solution.py:24
  57.9 2.1 %collective-permute-start.73 = (bf16[96,2048]{1,0:T(8,128)(2,1)S(1)}, bf16[96,2048]{1,0:T(8,128)(2,1)S(1)}, u32[]{:S(2)}, u32[]{:S(2)}) collective-permute-start(bf16[96,2048]{1,0:T(8,128)(2,1)S(1)} %add_convert_fusion.3), channel_id=1, source_target_pairs={{0,4},{1,5},{2,6},{3,7},{4,0},{5,1},{6,2},{7,3},{8,12},{9,13},{10,... | collective-permute-start | bytes 1179656 | tf_op jit(solution)/shard_map/sum_z/ppermute | solution.py:24
  60.1 0.2 convert_reduce_fusion
  60.2 0.3 convolution_multiply_fusion.7
  60.5 5.0 %collective-permute-done.77 = bf16[96,2048]{1,0:T(8,128)(2,1)S(1)} collective-permute-done((bf16[96,2048]{1,0:T(8,128)(2,1)S(1)}, bf16[96,2048]{1,0:T(8,128)(2,1)S(1)}, u32[]{:S(2)}, u32[]{:S(2)}) %collective-permute-start.77) | collective-permute-done | bytes 393248 | tf_op jit(solution)/shard_map/sum_z/ppermute | solution.py:24
  65.5 3.6 %collective-permute-done.73 = bf16[96,2048]{1,0:T(8,128)(2,1)S(1)} collective-permute-done((bf16[96,2048]{1,0:T(8,128)(2,1)S(1)}, bf16[96,2048]{1,0:T(8,128)(2,1)S(1)}, u32[]{:S(2)}, u32[]{:S(2)}) %collective-permute-start.73) | collective-permute-done | bytes 393248 | tf_op jit(solution)/shard_map/sum_z/ppermute | solution.py:24
  69.1 0.1 fusion.73
  69.3 3.4 %collective-permute-start.78 = (bf16[24,2048]{1,0:T(8,128)(2,1)S(1)}, bf16[24,2048]{1,0:T(8,128)(2,1)S(1)}, u32[]{:S(2)}, u32[]{:S(2)}) collective-permute-start(bf16[24,2048]{1,0:T(8,128)(2,1)S(1)} %get-tuple-element.147), channel_id=1, source_target_pairs={{0,1},{1,0},{2,3},{3,2},{4,5},{5,4},{6,7},{7,6},{8,9},{9,8},{10,11... | collective-permute-start | bytes 294920 | tf_op jit(solution)/shard_map/sum_x/ppermute | solution.py:29
  72.7 4.3 %collective-permute-start.80 = (bf16[24,2048]{1,0:T(8,128)(2,1)S(1)}, bf16[24,2048]{1,0:T(8,128)(2,1)S(1)}, u32[]{:S(2)}, u32[]{:S(2)}) collective-permute-start(bf16[24,2048]{1,0:T(8,128)(2,1)S(1)} %get-tuple-element.148), channel_id=1, source_target_pairs={{0,3},{1,2},{2,1},{3,0},{4,7},{5,6},{6,5},{7,4},{8,11},{9,10},{10,... | collective-permute-start | bytes 294920 | tf_op jit(solution)/shard_map/sum_x/ppermute | solution.py:29
  77.0 1.9 %collective-permute-start.79 = (bf16[24,2048]{1,0:T(8,128)(2,1)S(1)}, bf16[24,2048]{1,0:T(8,128)(2,1)S(1)}, u32[]{:S(2)}, u32[]{:S(2)}) collective-permute-start(bf16[24,2048]{1,0:T(8,128)(2,1)S(1)} %get-tuple-element.149), channel_id=1, source_target_pairs={{0,2},{1,3},{2,0},{3,1},{4,6},{5,7},{6,4},{7,5},{8,10},{9,11},{10,... | collective-permute-start | bytes 294920 | tf_op jit(solution)/shard_map/sum_x/ppermute | solution.py:29
  79.6 1.7 collective-permute-done.80
  81.3 4.2 %collective-permute-done.79 = bf16[24,2048]{1,0:T(8,128)(2,1)S(1)} collective-permute-done((bf16[24,2048]{1,0:T(8,128)(2,1)S(1)}, bf16[24,2048]{1,0:T(8,128)(2,1)S(1)}, u32[]{:S(2)}, u32[]{:S(2)}) %collective-permute-start.79) | collective-permute-done | bytes 98336 | tf_op jit(solution)/shard_map/sum_x/ppermute | solution.py:29
  85.4 1.6 fusion.64
  87.0 89.7 %conditional.1 = (bf16[1,768,128]{2,1,0:T(8,128)(2,1)S(1)}, bf16[1,128,2048]{2,1,0:T(8,128)(2,1)S(1)}, bf16[1,128,2048]{2,1,0:T(8,128)(2,1)S(1)}) conditional(s32[]{:T(128)} %clamp.3, (bf16[24,2048]{1,0:T(8,128)(2,1)S(1)}, bf16[128,2048]{1,0:T(8,128)(2,1)S(1)}, s32[2]{0:T(128)S(1)}, ...), branch_computations={%region_1.2_spmd, %region_2.3_spmd, %region_3.4_spmd, %region_4.5_... | conditional | flops 812122112 | bytes 48628632 | solution.py:197
  87.0 3.0 %collective-permute-start.2 = (bf16[24,2048]{1,0:T(8,128)(2,1)S(1)}, bf16[24,2048]{1,0:T(8,128)(2,1)S(1)}, u32[]{:S(2)}, u32[]{:S(2)}) collective-permute-start(bf16[24,2048]{1,0:T(8,128)(2,1)S(1)} %get-tuple-element.64), channel_id=1, source_target_pairs={{0,3},{1,2},{2,1},{3,0},{4,7},{5,6},{6,5},{7,4},{8,11},{9,10},{10,... | collective-permute-start | bytes 294920 | tf_op jit(solution)/shard_map/cond/branch_0_fun/gather_x/ppermute | solution.py:29
  90.1 1.9 %collective-permute-start.1 = (bf16[24,2048]{1,0:T(8,128)(2,1)S(1)}, bf16[24,2048]{1,0:T(8,128)(2,1)S(1)}, u32[]{:S(2)}, u32[]{:S(2)}) collective-permute-start(bf16[24,2048]{1,0:T(8,128)(2,1)S(1)} %get-tuple-element.64), channel_id=1, source_target_pairs={{0,2},{1,3},{2,0},{3,1},{4,6},{5,7},{6,4},{7,5},{8,10},{9,11},{10,... | collective-permute-start | bytes 294920 | tf_op jit(solution)/shard_map/cond/branch_0_fun/gather_x/ppermute | solution.py:29
  92.0 5.1 %collective-permute-start = (bf16[24,2048]{1,0:T(8,128)(2,1)S(1)}, bf16[24,2048]{1,0:T(8,128)(2,1)S(1)}, u32[]{:S(2)}, u32[]{:S(2)}) collective-permute-start(bf16[24,2048]{1,0:T(8,128)(2,1)S(1)} %get-tuple-element.64), channel_id=1, source_target_pairs={{0,1},{1,0},{2,3},{3,2},{4,5},{5,4},{6,7},{7,6},{8,9},{9,8},{10,11... | collective-permute-start | bytes 294920 | tf_op jit(solution)/shard_map/cond/branch_0_fun/gather_x/ppermute | solution.py:29
  97.2 2.6 %collective-permute-done = bf16[24,2048]{1,0:T(8,128)(2,1)S(1)} collective-permute-done((bf16[24,2048]{1,0:T(8,128)(2,1)S(1)}, bf16[24,2048]{1,0:T(8,128)(2,1)S(1)}, u32[]{:S(2)}, u32[]{:S(2)}) %collective-permute-start) | collective-permute-done | bytes 98336 | tf_op jit(solution)/shard_map/cond/branch_0_fun/gather_x/ppermute | solution.py:29
  99.8 2.7 %collective-permute-start.4 = (bf16[96,2048]{1,0:T(8,128)(2,1)S(1)}, bf16[96,2048]{1,0:T(8,128)(2,1)S(1)}, u32[]{:S(2)}, u32[]{:S(2)}) collective-permute-start(bf16[96,2048]{1,0:T(8,128)(2,1)S(1)} %constant_dynamic-update-slice_fusion.refs_0_.refs_1_), channel_id=1, source_target_pairs={{0,28},{1,29},{2,30},{3,31},{4,8},{5,9},{6,10},{7,11},{8,4},{9,5},... | collective-permute-start | bytes 1179656 | tf_op jit(solution)/shard_map/cond/branch_0_fun/gather_z/ppermute | solution.py:24
  102.5 1.9 %collective-permute-start.3 = (bf16[96,2048]{1,0:T(8,128)(2,1)S(1)}, bf16[96,2048]{1,0:T(8,128)(2,1)S(1)}, u32[]{:S(2)}, u32[]{:S(2)}) collective-permute-start(bf16[96,2048]{1,0:T(8,128)(2,1)S(1)} %constant_dynamic-update-slice_fusion.refs_0_.refs_1_), channel_id=1, source_target_pairs={{0,4},{1,5},{2,6},{3,7},{4,0},{5,1},{6,2},{7,3},{8,12},{9,13},{10,... | collective-permute-start | bytes 1179656 | tf_op jit(solution)/shard_map/cond/branch_0_fun/gather_z/ppermute | solution.py:24
  104.5 1.9 %collective-permute-start.7 = (bf16[128,2048]{1,0:T(8,128)(2,1)S(1)}, bf16[128,2048]{1,0:T(8,128)(2,1)S(1)}, u32[]{:S(2)}, u32[]{:S(2)}) collective-permute-start(bf16[128,2048]{1,0:T(8,128)(2,1)S(1)} %get-tuple-element.65.refs_9_), channel_id=1, source_target_pairs={{0,32},{32,64},{64,96},{96,128},{128,160},{160,192},{192,224},{224... | collective-permute-start | bytes 1572872 | tf_op jit(solution)/shard_map/cond/branch_0_fun/early_partner/ppermute | solution.py:34
  106.4 5.1 %collective-permute-done.4.refs_7_.refs_8_ = bf16[96,2048]{1,0:T(8,128)(2,1)S(1)} collective-permute-done((bf16[96,2048]{1,0:T(8,128)(2,1)S(1)}, bf16[96,2048]{1,0:T(8,128)(2,1)S(1)}, u32[]{:S(2)}, u32[]{:S(2)}) %collective-permute-start.4) | collective-permute-done | bytes 393248 | tf_op jit(solution)/shard_map/cond/branch_0_fun/gather_z/ppermute | solution.py:24
  111.5 1.9 %collective-permute-start.5 = (bf16[96,2048]{1,0:T(8,128)(2,1)S(1)}, bf16[96,2048]{1,0:T(8,128)(2,1)S(1)}, u32[]{:S(2)}, u32[]{:S(2)}) collective-permute-start(bf16[96,2048]{1,0:T(8,128)(2,1)S(1)} %collective-permute-done.4.refs_7_.refs_8_), channel_id=1, source_target_pairs={{0,4},{1,5},{2,6},{3,7},{4,0},{5,1},{6,2},{7,3},{8,12},{9,13},{10,... | collective-permute-start | bytes 1179656 | tf_op jit(solution)/shard_map/cond/branch_0_fun/gather_z/ppermute | solution.py:24
  113.5 3.6 %collective-permute-start.6 = (bf16[96,2048]{1,0:T(8,128)(2,1)S(1)}, bf16[96,2048]{1,0:T(8,128)(2,1)S(1)}, u32[]{:S(2)}, u32[]{:S(2)}) collective-permute-start(bf16[96,2048]{1,0:T(8,128)(2,1)S(1)} %collective-permute-done.3.refs_1_.refs_2_), channel_id=1, source_target_pairs={{0,28},{1,29},{2,30},{3,31},{4,8},{5,9},{6,10},{7,11},{8,4},{9,5},... | collective-permute-start | bytes 1179656 | tf_op jit(solution)/shard_map/cond/branch_0_fun/gather_z/ppermute | solution.py:24
  117.1 5.2 %collective-permute-done.7 = bf16[128,2048]{1,0:T(8,128)(2,1)S(1)} collective-permute-done((bf16[128,2048]{1,0:T(8,128)(2,1)S(1)}, bf16[128,2048]{1,0:T(8,128)(2,1)S(1)}, u32[]{:S(2)}, u32[]{:S(2)}) %collective-permute-start.7) | collective-permute-done | bytes 524320 | tf_op jit(solution)/shard_map/cond/branch_0_fun/early_partner/ppermute | solution.py:34
  122.3 1.2 collective-permute-done.5.refs_2_.refs_3_
  123.4 4.6 %collective-permute-done.6.refs_6_.refs_7_ = bf16[96,2048]{1,0:T(8,128)(2,1)S(1)} collective-permute-done((bf16[96,2048]{1,0:T(8,128)(2,1)S(1)}, bf16[96,2048]{1,0:T(8,128)(2,1)S(1)}, u32[]{:S(2)}, u32[]{:S(2)}) %collective-permute-start.6) | collective-permute-done | bytes 393248 | tf_op jit(solution)/shard_map/cond/branch_0_fun/gather_z/ppermute | solution.py:24
  128.0 1.9 %collective-permute-start.8 = (bf16[96,2048]{1,0:T(8,128)(2,1)S(1)}, bf16[96,2048]{1,0:T(8,128)(2,1)S(1)}, u32[]{:S(2)}, u32[]{:S(2)}) collective-permute-start(bf16[96,2048]{1,0:T(8,128)(2,1)S(1)} %collective-permute-done.6.refs_6_.refs_7_), channel_id=1, source_target_pairs={{0,4},{1,5},{2,6},{3,7},{4,0},{5,1},{6,2},{7,3},{8,12},{9,13},{10,... | collective-permute-start | bytes 1179656 | tf_op jit(solution)/shard_map/cond/branch_0_fun/gather_z/ppermute | solution.py:24
  130.0 4.0 %collective-permute-start.10 = (bf16[96,2048]{1,0:T(8,128)(2,1)S(1)}, bf16[96,2048]{1,0:T(8,128)(2,1)S(1)}, u32[]{:S(2)}, u32[]{:S(2)}) collective-permute-start(bf16[96,2048]{1,0:T(8,128)(2,1)S(1)} %collective-permute-done.5.refs_2_.refs_3_), channel_id=1, source_target_pairs={{0,28},{1,29},{2,30},{3,31},{4,8},{5,9},{6,10},{7,11},{8,4},{9,5},... | collective-permute-start | bytes 1179656 | tf_op jit(solution)/shard_map/cond/branch_0_fun/gather_z/ppermute | solution.py:24
  134.0 6.6 %collective-permute-done.8.refs_3_.refs_4_ = bf16[96,2048]{1,0:T(8,128)(2,1)S(1)} collective-permute-done((bf16[96,2048]{1,0:T(8,128)(2,1)S(1)}, bf16[96,2048]{1,0:T(8,128)(2,1)S(1)}, u32[]{:S(2)}, u32[]{:S(2)}) %collective-permute-start.8) | collective-permute-done | bytes 393248 | tf_op jit(solution)/shard_map/cond/branch_0_fun/gather_z/ppermute | solution.py:24
  140.6 4.4 %collective-permute-start.9 = (bf16[96,1024]{1,0:T(8,128)(2,1)S(1)}, bf16[96,1024]{1,0:T(8,128)(2,1)S(1)}, u32[]{:S(2)}, u32[]{:S(2)}) collective-permute-start(bf16[96,1024]{1,0:T(8,128)(2,1)S(1)} %slice.181), channel_id=1, source_target_pairs={{0,28},{1,29},{2,30},{3,31},{4,8},{5,9},{6,10},{7,11},{8,4},{9,5},... | collective-permute-start | bytes 589832 | tf_op jit(solution)/shard_map/cond/branch_0_fun/gather_z/ppermute | solution.py:24
  145.1 0.8 slice.182
  145.9 1.9 %collective-permute-start.11 = (bf16[96,1024]{1,0:T(8,128)(2,1)}, bf16[96,1024]{1,0:T(8,128)(2,1)}, u32[]{:S(2)}, u32[]{:S(2)}) collective-permute-start(bf16[96,1024]{1,0:T(8,128)(2,1)} %slice.182), channel_id=1, source_target_pairs={{0,4},{1,5},{2,6},{3,7},{4,0},{5,1},{6,2},{7,3},{8,12},{9,13},{10,... | collective-permute-start | bytes 589832 | tf_op jit(solution)/shard_map/cond/branch_0_fun/gather_z/ppermute | solution.py:24
  147.8 1.6 collective-permute-done.9.refs_4_.refs_5_
  149.4 0.6 copy-done.47
  150.1 2.5 %moment.10 = bf16[128,1024]{1,0:T(8,128)(2,1)} custom-call(bf16[768,128]{1,0:T(8,128)(2,1)S(1)} %bitcast.94, bf16[96,2048]{1,0:T(8,128)(2,1)} %copy-done.12, bf16[96,2048]{1,0:T(8,128)(2,1)} %copy-done.22, bf16[96,2048]{1,0:T(8,128)(2,1)} %copy-done.27, bf16[96,2048]{1,0:T(8,128)(2,1)} %copy-done.2, bf16[96,1024]{1,0:T(8,128)(2,1)} %copy-done.47, ...), custom_call_target="tpu_custom_call" | custom-call | flops 201326592 | bytes 2097152 | tf_op jit(solution)/shard_map/cond/branch_0_fun/moment/pallas_call | solution.py:65
  152.6 2.1 %collective-permute-start.12 = (bf16[128,1024]{1,0:T(8,128)(2,1)}, bf16[128,1024]{1,0:T(8,128)(2,1)S(1)}, u32[]{:S(2)}, u32[]{:S(2)}) collective-permute-start(bf16[128,1024]{1,0:T(8,128)(2,1)} %moment.10), channel_id=1, source_target_pairs={{0,32},{32,64},{64,96},{96,128},{128,160},{160,192},{192,224},{224... | collective-permute-start | bytes 786440 | tf_op jit(solution)/shard_map/cond/branch_0_fun/partner/ppermute | solution.py:34
  154.7 2.6 %moment.11 = bf16[128,1024]{1,0:T(8,128)(2,1)} custom-call(bf16[768,128]{1,0:T(8,128)(2,1)S(1)} %bitcast.95, bf16[96,2048]{1,0:T(8,128)(2,1)} %copy-done.12, bf16[96,2048]{1,0:T(8,128)(2,1)} %copy-done.22, bf16[96,2048]{1,0:T(8,128)(2,1)} %copy-done.27, bf16[96,2048]{1,0:T(8,128)(2,1)} %copy-done.2, ...), custom_call_target="tpu_custom_call" | custom-call | flops 201326592 | bytes 2097152 | tf_op jit(solution)/shard_map/cond/branch_0_fun/moment/pallas_call | solution.py:65
  157.3 4.1 %collective-permute-start.13 = (bf16[128,1024]{1,0:T(8,128)(2,1)}, bf16[128,1024]{1,0:T(8,128)(2,1)S(1)}, u32[]{:S(2)}, u32[]{:S(2)}) collective-permute-start(bf16[128,1024]{1,0:T(8,128)(2,1)} %moment.11), channel_id=1, source_target_pairs={{0,32},{32,64},{64,96},{96,128},{128,160},{160,192},{192,224},{224... | collective-permute-start | bytes 786440 | tf_op jit(solution)/shard_map/cond/branch_0_fun/partner/ppermute | solution.py:34
  161.3 3.3 %back.5 = bf16[32,24,128]{2,1,0:T(8,128)(2,1)S(1)} custom-call(s32[2]{0:T(128)S(1)} %get-tuple-element.63.place_ref, bf16[96,2048]{1,0:T(8,128)(2,1)} %copy-done.12, bf16[96,2048]{1,0:T(8,128)(2,1)} %copy-done.22, bf16[96,2048]{1,0:T(8,128)(2,1)} %copy-done.27, bf16[96,2048]{1,0:T(8,128)(2,1)} %copy-done.2, bf16[96,1024]{1,0:T(8,128)(2,1)} %copy-done.47, ...), custom_call_target="tpu_custom_call" | custom-call | flops 402653184 | bytes 3145728 | tf_op jit(solution)/shard_map/cond/branch_0_fun/back/back/pallas_call | solution.py:179
  164.6 3.2 %collective-permute-done.12 = bf16[128,1024]{1,0:T(8,128)(2,1)S(1)} collective-permute-done((bf16[128,1024]{1,0:T(8,128)(2,1)}, bf16[128,1024]{1,0:T(8,128)(2,1)S(1)}, u32[]{:S(2)}, u32[]{:S(2)}) %collective-permute-start.12) | collective-permute-done | bytes 262176 | tf_op jit(solution)/shard_map/cond/branch_0_fun/partner/ppermute | solution.py:34
  167.8 8.1 %collective-permute-done.13 = bf16[128,1024]{1,0:T(8,128)(2,1)S(1)} collective-permute-done((bf16[128,1024]{1,0:T(8,128)(2,1)}, bf16[128,1024]{1,0:T(8,128)(2,1)S(1)}, u32[]{:S(2)}, u32[]{:S(2)}) %collective-permute-start.13) | collective-permute-done | bytes 262176 | tf_op jit(solution)/shard_map/cond/branch_0_fun/partner/ppermute | solution.py:34
  175.9 0.5 multiply_convert_fusion.1
  176.8 0.8 copy-done.62
  177.5 0.2 copy-done.63
  (61 shorter events, 0.8 us)
Async XLA Ops:
  0.6 23.7 %copy-start = (bf16[1,128,2048]{2,1,0:T(8,128)(2,1)S(1)}, bf16[1,128,2048]{2,1,0:T(8,128)(2,1)}, u32[]{:S(2)}) copy-start(bf16[1,128,2048]{2,1,0:T(8,128)(2,1)} %param.12) | copy-start | bytes 1572868
  0.7 1.7 copy-start.65
  3.8 29.1 %collective-permute-start.70 = (bf16[96,1024]{1,0:T(8,128)(2,1)S(1)}, bf16[96,1024]{1,0:T(8,128)(2,1)S(1)}, u32[]{:S(2)}, u32[]{:S(2)}) collective-permute-start(bf16[96,1024]{1,0:T(8,128)(2,1)S(1)} %get-tuple-element.150), channel_id=1, source_target_pairs={{0,28},{1,29},{2,30},{3,31},{4,8},{5,9},{6,10},{7,11},{8,4},{9,5},... | collective-permute-start | bytes 589832 | tf_op jit(solution)/shard_map/sum_z/ppermute | solution.py:24
  21.1 8.3 %collective-permute-start.74 = (bf16[96,1024]{1,0:T(8,128)(2,1)S(1)}, bf16[96,1024]{1,0:T(8,128)(2,1)S(1)}, u32[]{:S(2)}, u32[]{:S(2)}) collective-permute-start(bf16[96,1024]{1,0:T(8,128)(2,1)S(1)} %get-tuple-element.151), channel_id=1, source_target_pairs={{0,4},{1,5},{2,6},{3,7},{4,0},{5,1},{6,2},{7,3},{8,12},{9,13},{10,... | collective-permute-start | bytes 589832 | tf_op jit(solution)/shard_map/sum_z/ppermute | solution.py:24
  29.6 12.8 %collective-permute-start.75 = (bf16[96,2048]{1,0:T(8,128)(2,1)S(1)}, bf16[96,2048]{1,0:T(8,128)(2,1)S(1)}, u32[]{:S(2)}, u32[]{:S(2)}) collective-permute-start(bf16[96,2048]{1,0:T(8,128)(2,1)S(1)} %add_convert_fusion.2), channel_id=1, source_target_pairs={{0,28},{1,29},{2,30},{3,31},{4,8},{5,9},{6,10},{7,11},{8,4},{9,5},... | collective-permute-start | bytes 1179656 | tf_op jit(solution)/shard_map/sum_z/ppermute | solution.py:24
  33.1 26.8 %copy-start.67 = (s32[1,768]{1,0:T(1,128)S(1)}, s32[1,768]{1,0:T(1,128)}, u32[]{:S(2)}) copy-start(s32[1,768]{1,0:T(1,128)} %param.15) | copy-start | bytes 9220
  33.1 11.6 %collective-permute-start.71 = (bf16[96,2048]{1,0:T(8,128)(2,1)S(1)}, bf16[96,2048]{1,0:T(8,128)(2,1)S(1)}, u32[]{:S(2)}, u32[]{:S(2)}) collective-permute-start(bf16[96,2048]{1,0:T(8,128)(2,1)S(1)} %add_convert_fusion.5), channel_id=1, source_target_pairs={{0,4},{1,5},{2,6},{3,7},{4,0},{5,1},{6,2},{7,3},{8,12},{9,13},{10,... | collective-permute-start | bytes 1179656 | tf_op jit(solution)/shard_map/sum_z/ppermute | solution.py:24
  42.5 10.7 %collective-permute-start.76 = (bf16[96,2048]{1,0:T(8,128)(2,1)S(1)}, bf16[96,2048]{1,0:T(8,128)(2,1)S(1)}, u32[]{:S(2)}, u32[]{:S(2)}) collective-permute-start(bf16[96,2048]{1,0:T(8,128)(2,1)S(1)} %add_convert_fusion.1), channel_id=1, source_target_pairs={{0,4},{1,5},{2,6},{3,7},{4,0},{5,1},{6,2},{7,3},{8,12},{9,13},{10,... | collective-permute-start | bytes 1179656 | tf_op jit(solution)/shard_map/sum_z/ppermute | solution.py:24
  44.8 13.0 %collective-permute-start.72 = (bf16[96,2048]{1,0:T(8,128)(2,1)S(1)}, bf16[96,2048]{1,0:T(8,128)(2,1)S(1)}, u32[]{:S(2)}, u32[]{:S(2)}) collective-permute-start(bf16[96,2048]{1,0:T(8,128)(2,1)S(1)} %add_convert_fusion.4), channel_id=1, source_target_pairs={{0,28},{1,29},{2,30},{3,31},{4,8},{5,9},{6,10},{7,11},{8,4},{9,5},... | collective-permute-start | bytes 1179656 | tf_op jit(solution)/shard_map/sum_z/ppermute | solution.py:24
  53.2 12.2 %collective-permute-start.77 = (bf16[96,2048]{1,0:T(8,128)(2,1)S(1)}, bf16[96,2048]{1,0:T(8,128)(2,1)S(1)}, u32[]{:S(2)}, u32[]{:S(2)}) collective-permute-start(bf16[96,2048]{1,0:T(8,128)(2,1)S(1)} %add_convert_fusion), channel_id=1, source_target_pairs={{0,28},{1,29},{2,30},{3,31},{4,8},{5,9},{6,10},{7,11},{8,4},{9,5},... | collective-permute-start | bytes 1179656 | tf_op jit(solution)/shard_map/sum_z/ppermute | solution.py:24
  57.9 29.2 %copy-start.1 = (bf16[1,128,2048]{2,1,0:T(8,128)(2,1)S(1)}, bf16[1,128,2048]{2,1,0:T(8,128)(2,1)}, u32[]{:S(2)}) copy-start(bf16[1,128,2048]{2,1,0:T(8,128)(2,1)} %param.13) | copy-start | bytes 1572868
  57.9 29.1 %copy-start.66 = (s32[2]{0:T(128)S(1)}, s32[2]{0:T(128)}, u32[]{:S(2)}) copy-start(s32[2]{0:T(128)} %copy-done.65) | copy-start | bytes 28
  57.9 11.2 %collective-permute-start.73 = (bf16[96,2048]{1,0:T(8,128)(2,1)S(1)}, bf16[96,2048]{1,0:T(8,128)(2,1)S(1)}, u32[]{:S(2)}, u32[]{:S(2)}) collective-permute-start(bf16[96,2048]{1,0:T(8,128)(2,1)S(1)} %add_convert_fusion.3), channel_id=1, source_target_pairs={{0,4},{1,5},{2,6},{3,7},{4,0},{5,1},{6,2},{7,3},{8,12},{9,13},{10,... | collective-permute-start | bytes 1179656 | tf_op jit(solution)/shard_map/sum_z/ppermute | solution.py:24
  69.3 10.4 %collective-permute-start.78 = (bf16[24,2048]{1,0:T(8,128)(2,1)S(1)}, bf16[24,2048]{1,0:T(8,128)(2,1)S(1)}, u32[]{:S(2)}, u32[]{:S(2)}) collective-permute-start(bf16[24,2048]{1,0:T(8,128)(2,1)S(1)} %get-tuple-element.147), channel_id=1, source_target_pairs={{0,1},{1,0},{2,3},{3,2},{4,5},{5,4},{6,7},{7,6},{8,9},{9,8},{10,11... | collective-permute-start | bytes 294920 | tf_op jit(solution)/shard_map/sum_x/ppermute | solution.py:29
  72.7 8.6 %collective-permute-start.80 = (bf16[24,2048]{1,0:T(8,128)(2,1)S(1)}, bf16[24,2048]{1,0:T(8,128)(2,1)S(1)}, u32[]{:S(2)}, u32[]{:S(2)}) collective-permute-start(bf16[24,2048]{1,0:T(8,128)(2,1)S(1)} %get-tuple-element.148), channel_id=1, source_target_pairs={{0,3},{1,2},{2,1},{3,0},{4,7},{5,6},{6,5},{7,4},{8,11},{9,10},{10,... | collective-permute-start | bytes 294920 | tf_op jit(solution)/shard_map/sum_x/ppermute | solution.py:29
  77.0 8.5 %collective-permute-start.79 = (bf16[24,2048]{1,0:T(8,128)(2,1)S(1)}, bf16[24,2048]{1,0:T(8,128)(2,1)S(1)}, u32[]{:S(2)}, u32[]{:S(2)}) collective-permute-start(bf16[24,2048]{1,0:T(8,128)(2,1)S(1)} %get-tuple-element.149), channel_id=1, source_target_pairs={{0,2},{1,3},{2,0},{3,1},{4,6},{5,7},{6,4},{7,5},{8,10},{9,11},{10,... | collective-permute-start | bytes 294920 | tf_op jit(solution)/shard_map/sum_x/ppermute | solution.py:29
  87.0 12.7 %collective-permute-start.2 = (bf16[24,2048]{1,0:T(8,128)(2,1)S(1)}, bf16[24,2048]{1,0:T(8,128)(2,1)S(1)}, u32[]{:S(2)}, u32[]{:S(2)}) collective-permute-start(bf16[24,2048]{1,0:T(8,128)(2,1)S(1)} %get-tuple-element.64), channel_id=1, source_target_pairs={{0,3},{1,2},{2,1},{3,0},{4,7},{5,6},{6,5},{7,4},{8,11},{9,10},{10,... | collective-permute-start | bytes 294920 | tf_op jit(solution)/shard_map/cond/branch_0_fun/gather_x/ppermute | solution.py:29
  90.1 9.7 %collective-permute-start.1 = (bf16[24,2048]{1,0:T(8,128)(2,1)S(1)}, bf16[24,2048]{1,0:T(8,128)(2,1)S(1)}, u32[]{:S(2)}, u32[]{:S(2)}) collective-permute-start(bf16[24,2048]{1,0:T(8,128)(2,1)S(1)} %get-tuple-element.64), channel_id=1, source_target_pairs={{0,2},{1,3},{2,0},{3,1},{4,6},{5,7},{6,4},{7,5},{8,10},{9,11},{10,... | collective-permute-start | bytes 294920 | tf_op jit(solution)/shard_map/cond/branch_0_fun/gather_x/ppermute | solution.py:29
  92.0 7.7 %collective-permute-start = (bf16[24,2048]{1,0:T(8,128)(2,1)S(1)}, bf16[24,2048]{1,0:T(8,128)(2,1)S(1)}, u32[]{:S(2)}, u32[]{:S(2)}) collective-permute-start(bf16[24,2048]{1,0:T(8,128)(2,1)S(1)} %get-tuple-element.64), channel_id=1, source_target_pairs={{0,1},{1,0},{2,3},{3,2},{4,5},{5,4},{6,7},{7,6},{8,9},{9,8},{10,11... | collective-permute-start | bytes 294920 | tf_op jit(solution)/shard_map/cond/branch_0_fun/gather_x/ppermute | solution.py:29
  99.8 49.6 %copy-start.12 = (bf16[96,2048]{1,0:T(8,128)(2,1)}, bf16[96,2048]{1,0:T(8,128)(2,1)S(1)}, u32[]{:S(2)}) copy-start(bf16[96,2048]{1,0:T(8,128)(2,1)S(1)} %constant_dynamic-update-slice_fusion.refs_0_.refs_1_) | copy-start | bytes 1179652 | tf_op jit(solution)/shard_map/cond
  99.8 11.7 %collective-permute-start.4 = (bf16[96,2048]{1,0:T(8,128)(2,1)S(1)}, bf16[96,2048]{1,0:T(8,128)(2,1)S(1)}, u32[]{:S(2)}, u32[]{:S(2)}) collective-permute-start(bf16[96,2048]{1,0:T(8,128)(2,1)S(1)} %constant_dynamic-update-slice_fusion.refs_0_.refs_1_), channel_id=1, source_target_pairs={{0,28},{1,29},{2,30},{3,31},{4,8},{5,9},{6,10},{7,11},{8,4},{9,5},... | collective-permute-start | bytes 1179656 | tf_op jit(solution)/shard_map/cond/branch_0_fun/gather_z/ppermute | solution.py:24
  102.5 10.9 %collective-permute-start.3 = (bf16[96,2048]{1,0:T(8,128)(2,1)S(1)}, bf16[96,2048]{1,0:T(8,128)(2,1)S(1)}, u32[]{:S(2)}, u32[]{:S(2)}) collective-permute-start(bf16[96,2048]{1,0:T(8,128)(2,1)S(1)} %constant_dynamic-update-slice_fusion.refs_0_.refs_1_), channel_id=1, source_target_pairs={{0,4},{1,5},{2,6},{3,7},{4,0},{5,1},{6,2},{7,3},{8,12},{9,13},{10,... | collective-permute-start | bytes 1179656 | tf_op jit(solution)/shard_map/cond/branch_0_fun/gather_z/ppermute | solution.py:24
  104.5 17.8 %collective-permute-start.7 = (bf16[128,2048]{1,0:T(8,128)(2,1)S(1)}, bf16[128,2048]{1,0:T(8,128)(2,1)S(1)}, u32[]{:S(2)}, u32[]{:S(2)}) collective-permute-start(bf16[128,2048]{1,0:T(8,128)(2,1)S(1)} %get-tuple-element.65.refs_9_), channel_id=1, source_target_pairs={{0,32},{32,64},{64,96},{96,128},{128,160},{160,192},{192,224},{224... | collective-permute-start | bytes 1572872 | tf_op jit(solution)/shard_map/cond/branch_0_fun/early_partner/ppermute | solution.py:34
  111.5 37.9 %copy-start.17 = (bf16[96,2048]{1,0:T(8,128)(2,1)}, bf16[96,2048]{1,0:T(8,128)(2,1)S(1)}, u32[]{:S(2)}) copy-start(bf16[96,2048]{1,0:T(8,128)(2,1)S(1)} %collective-permute-done.4.refs_7_.refs_8_) | copy-start | bytes 1179652 | tf_op jit(solution)/shard_map/cond
  111.5 11.9 %collective-permute-start.5 = (bf16[96,2048]{1,0:T(8,128)(2,1)S(1)}, bf16[96,2048]{1,0:T(8,128)(2,1)S(1)}, u32[]{:S(2)}, u32[]{:S(2)}) collective-permute-start(bf16[96,2048]{1,0:T(8,128)(2,1)S(1)} %collective-permute-done.4.refs_7_.refs_8_), channel_id=1, source_target_pairs={{0,4},{1,5},{2,6},{3,7},{4,0},{5,1},{6,2},{7,3},{8,12},{9,13},{10,... | collective-permute-start | bytes 1179656 | tf_op jit(solution)/shard_map/cond/branch_0_fun/gather_z/ppermute | solution.py:24
  113.4 36.0 %copy-start.22 = (bf16[96,2048]{1,0:T(8,128)(2,1)}, bf16[96,2048]{1,0:T(8,128)(2,1)S(1)}, u32[]{:S(2)}) copy-start(bf16[96,2048]{1,0:T(8,128)(2,1)S(1)} %collective-permute-done.3.refs_1_.refs_2_) | copy-start | bytes 1179652 | tf_op jit(solution)/shard_map/cond
  113.5 14.6 %collective-permute-start.6 = (bf16[96,2048]{1,0:T(8,128)(2,1)S(1)}, bf16[96,2048]{1,0:T(8,128)(2,1)S(1)}, u32[]{:S(2)}, u32[]{:S(2)}) collective-permute-start(bf16[96,2048]{1,0:T(8,128)(2,1)S(1)} %collective-permute-done.3.refs_1_.refs_2_), channel_id=1, source_target_pairs={{0,28},{1,29},{2,30},{3,31},{4,8},{5,9},{6,10},{7,11},{8,4},{9,5},... | collective-permute-start | bytes 1179656 | tf_op jit(solution)/shard_map/cond/branch_0_fun/gather_z/ppermute | solution.py:24
  122.3 11.7 %copy-start.52 = (bf16[128,2048]{1,0:T(8,128)(2,1)}, bf16[128,2048]{1,0:T(8,128)(2,1)S(1)}, u32[]{:S(2)}) copy-start(bf16[128,2048]{1,0:T(8,128)(2,1)S(1)} %collective-permute-done.7) | copy-start | bytes 1572868 | tf_op jit(solution)/shard_map/cond
  123.4 21.7 %copy-start.27 = (bf16[96,2048]{1,0:T(8,128)(2,1)}, bf16[96,2048]{1,0:T(8,128)(2,1)S(1)}, u32[]{:S(2)}) copy-start(bf16[96,2048]{1,0:T(8,128)(2,1)S(1)} %collective-permute-done.5.refs_2_.refs_3_) | copy-start | bytes 1179652 | tf_op jit(solution)/shard_map/cond
  128.0 1.9 %copy-start.32 = (bf16[96,2048]{1,0:T(8,128)(2,1)}, bf16[96,2048]{1,0:T(8,128)(2,1)S(1)}, u32[]{:S(2)}) copy-start(bf16[96,2048]{1,0:T(8,128)(2,1)S(1)} %collective-permute-done.6.refs_6_.refs_7_) | copy-start | bytes 1179652 | tf_op jit(solution)/shard_map/cond
  128.0 12.6 %collective-permute-start.8 = (bf16[96,2048]{1,0:T(8,128)(2,1)S(1)}, bf16[96,2048]{1,0:T(8,128)(2,1)S(1)}, u32[]{:S(2)}, u32[]{:S(2)}) collective-permute-start(bf16[96,2048]{1,0:T(8,128)(2,1)S(1)} %collective-permute-done.6.refs_6_.refs_7_), channel_id=1, source_target_pairs={{0,4},{1,5},{2,6},{3,7},{4,0},{5,1},{6,2},{7,3},{8,12},{9,13},{10,... | collective-permute-start | bytes 1179656 | tf_op jit(solution)/shard_map/cond/branch_0_fun/gather_z/ppermute | solution.py:24
  130.0 15.1 %collective-permute-start.10 = (bf16[96,2048]{1,0:T(8,128)(2,1)S(1)}, bf16[96,2048]{1,0:T(8,128)(2,1)S(1)}, u32[]{:S(2)}, u32[]{:S(2)}) collective-permute-start(bf16[96,2048]{1,0:T(8,128)(2,1)S(1)} %collective-permute-done.5.refs_2_.refs_3_), channel_id=1, source_target_pairs={{0,28},{1,29},{2,30},{3,31},{4,8},{5,9},{6,10},{7,11},{8,4},{9,5},... | collective-permute-start | bytes 1179656 | tf_op jit(solution)/shard_map/cond/branch_0_fun/gather_z/ppermute | solution.py:24
  140.6 8.8 %copy-start.2 = (bf16[96,2048]{1,0:T(8,128)(2,1)}, bf16[96,2048]{1,0:T(8,128)(2,1)S(1)}, u32[]{:S(2)}) copy-start(bf16[96,2048]{1,0:T(8,128)(2,1)S(1)} %collective-permute-done.8.refs_3_.refs_4_) | copy-start | bytes 1179652 | tf_op jit(solution)/shard_map/cond
  140.6 8.8 %collective-permute-start.9 = (bf16[96,1024]{1,0:T(8,128)(2,1)S(1)}, bf16[96,1024]{1,0:T(8,128)(2,1)S(1)}, u32[]{:S(2)}, u32[]{:S(2)}) collective-permute-start(bf16[96,1024]{1,0:T(8,128)(2,1)S(1)} %slice.181), channel_id=1, source_target_pairs={{0,28},{1,29},{2,30},{3,31},{4,8},{5,9},{6,10},{7,11},{8,4},{9,5},... | collective-permute-start | bytes 589832 | tf_op jit(solution)/shard_map/cond/branch_0_fun/gather_z/ppermute | solution.py:24
  145.1 4.3 %copy-start.7 = (bf16[96,2048]{1,0:T(8,128)(2,1)}, bf16[96,2048]{1,0:T(8,128)(2,1)S(1)}, u32[]{:S(2)}) copy-start(bf16[96,2048]{1,0:T(8,128)(2,1)S(1)} %collective-permute-done.10.refs_5_.refs_6_) | copy-start | bytes 1179652 | tf_op jit(solution)/shard_map/cond
  145.9 8.8 %collective-permute-start.11 = (bf16[96,1024]{1,0:T(8,128)(2,1)}, bf16[96,1024]{1,0:T(8,128)(2,1)}, u32[]{:S(2)}, u32[]{:S(2)}) collective-permute-start(bf16[96,1024]{1,0:T(8,128)(2,1)} %slice.182), channel_id=1, source_target_pairs={{0,4},{1,5},{2,6},{3,7},{4,0},{5,1},{6,2},{7,3},{8,12},{9,13},{10,... | collective-permute-start | bytes 589832 | tf_op jit(solution)/shard_map/cond/branch_0_fun/gather_z/ppermute | solution.py:24
  149.4 0.7 copy-start.47
  152.6 23.3 %copy-start.37 = (bf16[128,1024]{1,0:T(8,128)(2,1)S(1)}, bf16[128,1024]{1,0:T(8,128)(2,1)}, u32[]{:S(2)}) copy-start(bf16[128,1024]{1,0:T(8,128)(2,1)} %moment.10) | copy-start | bytes 786436 | tf_op jit(solution)/shard_map/cond
  152.6 23.3 %copy-start.53 = (bf16[128,2048]{1,0:T(8,128)(2,1)S(1)}, bf16[128,2048]{1,0:T(8,128)(2,1)}, u32[]{:S(2)}) copy-start(bf16[128,2048]{1,0:T(8,128)(2,1)} %copy-done.52) | copy-start | bytes 1572868 | tf_op jit(solution)/shard_map/cond
  152.6 15.2 %collective-permute-start.12 = (bf16[128,1024]{1,0:T(8,128)(2,1)}, bf16[128,1024]{1,0:T(8,128)(2,1)S(1)}, u32[]{:S(2)}, u32[]{:S(2)}) collective-permute-start(bf16[128,1024]{1,0:T(8,128)(2,1)} %moment.10), channel_id=1, source_target_pairs={{0,32},{32,64},{64,96},{96,128},{128,160},{160,192},{192,224},{224... | collective-permute-start | bytes 786440 | tf_op jit(solution)/shard_map/cond/branch_0_fun/partner/ppermute | solution.py:34
  157.2 18.7 %copy-start.42 = (bf16[128,1024]{1,0:T(8,128)(2,1)S(1)}, bf16[128,1024]{1,0:T(8,128)(2,1)}, u32[]{:S(2)}) copy-start(bf16[128,1024]{1,0:T(8,128)(2,1)} %moment.11) | copy-start | bytes 786436 | tf_op jit(solution)/shard_map/cond
  157.3 18.7 %collective-permute-start.13 = (bf16[128,1024]{1,0:T(8,128)(2,1)}, bf16[128,1024]{1,0:T(8,128)(2,1)S(1)}, u32[]{:S(2)}, u32[]{:S(2)}) collective-permute-start(bf16[128,1024]{1,0:T(8,128)(2,1)} %moment.11), channel_id=1, source_target_pairs={{0,32},{32,64},{64,96},{96,128},{128,160},{160,192},{192,224},{224... | collective-permute-start | bytes 786440 | tf_op jit(solution)/shard_map/cond/branch_0_fun/partner/ppermute | solution.py:34
  176.7 0.8 copy-start.62
  176.8 1.0 copy-start.63
  176.8 1.0 copy-start.64

commit v4 on v3

--- a/solution.py
+++ b/solution.py
@@ -24,9 +24,10 @@
     return lax.ppermute(x, "tensor", [(i, (i + step(i)) % size) for i in range(size)])
 
 
-def swap_x(x, k):
-    size = lax.axis_size("tensor")
-    return lax.ppermute(x, "tensor", [(i, i ^ k) for i in range(size)])
+def exchange_x(x):
+    size = lax.axis_size("tensor")
+    runs = [list(range(i, i + NX)) for i in range(0, size, NX)]
+    return lax.all_to_all(x, "tensor", 0, 0, axis_index_groups=runs, tiled=True)
 
 
 def pass_replica(x, by):
@@ -34,14 +35,14 @@
     return lax.ppermute(x, "replica", [(i, (i + by) % size) for i in range(size)])
 
 
-def place_of(j, k, z, x, nz):
-    return lax.rem(z + (1 - 2 * lax.rem(z, 2)) * j + nz, nz) * NX + (x ^ k)
+def place_of(j, k, z, nz):
+    return lax.rem(z + (1 - 2 * lax.rem(z, 2)) * j + nz, nz) * NX + k
 
 
 def order_kernel(nz, place_ref, rows_ref, out_ref):
     for j in range(nz):
         for k in range(NX):
-            out_ref[j * NX + k] = rows_ref[place_of(j, k, place_ref[0], place_ref[1], nz)]
+            out_ref[j * NX + k] = rows_ref[place_of(j, k, place_ref[0], nz)]
 
 
 def moment_kernel(scaling, nz, *refs):
@@ -90,7 +91,7 @@
         else:
             total = times(refs[j][...], w_ref[...])
         for k in range(NX):
-            out_ref[place_of(j, k, place_ref[0], place_ref[1], nz)] = (
+            out_ref[place_of(j, k, place_ref[0], nz)] = (
                 total[k * rows : (k + 1) * rows] * scaling
             ).astype(jnp.bfloat16)
 
@@ -102,7 +103,7 @@
     chunk = rows * NX
     scaling = (deep * size) ** (-0.5)
     own = lax.axis_index("tensor")
-    place = jnp.stack([own // NX, own % NX]).astype(jnp.int32)
+    place = (own // NX).astype(jnp.int32)[None]
     with jax.named_scope("order"):
         heads = pl.pallas_call(
             partial(order_kernel, nz),
@@ -135,10 +136,8 @@
             even, odd = swap_z(to_even, 0).astype(jnp.float32), swap_z(to_odd, 1).astype(jnp.float32)
         total = share(0) + even + odd
     with jax.named_scope("sum_x"):
-        mine = total[:rows]
-        for k in range(1, NX):
-            sent = swap_x(total[k * rows : (k + 1) * rows].astype(jnp.bfloat16), k)
-            mine = mine + sent.astype(jnp.float32)
+        parts = exchange_x(total.astype(jnp.bfloat16)).reshape(NX, rows, -1)
+        mine = jnp.sum(parts.astype(jnp.float32), axis=0)
     grad = ((mine - own_targets) * own_weights).astype(jnp.bfloat16)
     return mine.astype(jnp.bfloat16), grad, heads, place
 
@@ -150,29 +149,29 @@
     nz = size // NX
     scaling = (deep * size) ** (-0.5)
     with jax.named_scope("early_partner"):
-        partner_w = pass_replica(weight, hop)
+        half = width // 2
+        partner_w = [pass_replica(weight[:, :half], hop), pass_replica(weight[:, half:], hop)]
     with jax.named_scope("gather_x"):
-        block = jnp.concatenate([grad] + [swap_x(grad, k) for k in range(1, NX)], axis=0)
+        block = exchange_x(jnp.tile(grad, (NX, 1)))
     with jax.named_scope("gather_z"):
         held = [block] + [None] * (nz - 1)
         even = odd = block
-        half = width // 2
         for m in range(1, nz // 2):
             if m == nz // 2 - 1:
-                even, odd, partner_w = lax.optimization_barrier((even, odd, partner_w))
+                even, odd, partner_w[0] = lax.optimization_barrier((even, odd, partner_w[0]))
             even, odd = swap_z(odd, 0), swap_z(even, 1)
             held[m], held[-m] = even, odd
+        even, odd, partner_w[1] = lax.optimization_barrier((even, odd, partner_w[1]))
         held[nz // 2] = (swap_z(even[:, :half], 1), swap_z(odd[:, half:], 0))
     new_w, new_m = [], []
-    cols = width // 2
     for c in range(2):
-        part = slice(c * cols, (c + 1) * cols)
+        part = slice(c * half, (c + 1) * half)
         moment = moment_of(heads, held, moment_in, scaling, c)
         with jax.named_scope("partner"):
             partner_m = pass_replica(moment, hop).astype(jnp.float32)
         moment = moment.astype(jnp.float32)
         updated = (weight[:, part].astype(jnp.float32) - STEP_RATE * moment).astype(jnp.bfloat16)
-        partner_u = (partner_w[:, part].astype(jnp.float32) - STEP_RATE * partner_m).astype(jnp.bfloat16)
+        partner_u = (partner_w[c].astype(jnp.float32) - STEP_RATE * partner_m).astype(jnp.bfloat16)
         new_w.append(((updated.astype(jnp.float32) + partner_u.astype(jnp.float32)) * 0.5).astype(jnp.bfloat16))
         new_m.append(((moment + partner_m) * 0.5).astype(jnp.bfloat16))
     with jax.named_scope("back"):

time: 179 us -> 194 us (1.084)
  the two profiles are of different devices: /device:TPU:64 before, /device:TPU:14 now
where the time goes in v4:
time: 194 us; the launch traced here: 193 us
  starting transfers between devices  94.2 us (49%)
  waiting for transfers between devices  65 us (34%)
  blocking collectives  11.2 us (6%)
  Pallas kernels  9.33 us (5%)
  matrix products  4.15 us (2%)
  other arithmetic  3.53 us (2%)
  local copies, waits for them, and re-layouts  3.32 us (2%)
    ppermute x16, starting transfers between devices, swap_z(): lax.ppermute(x, 'tensor', [(i, (i + step(i)) % size) for i in range(size)])  61.1 us
    ppermute x16, waiting for transfers between devices, swap_z(): lax.ppermute(x, 'tensor', [(i, (i + step(i)) % size) for i in range(size)])  36.6 us
    ppermute x4, starting transfers between devices, pass_replica(): lax.ppermute(x, 'replica', [(i, (i + by) % size) for i in range(size)])  26.4 us
    ppermute x4, waiting for transfers between devices, pass_replica(): lax.ppermute(x, 'replica', [(i, (i + by) % size) for i in range(size)])  22.7 us
    all_to_all x1, blocking collectives, exchange_x(): return lax.all_to_all(x, 'tensor', 0, 0, axis_index_groups=runs, tiled=True)  11.2 us
    all_to_all x1, starting transfers between devices, exchange_x(): return lax.all_to_all(x, 'tensor', 0, 0, axis_index_groups=runs, tiled=True)  6.62 us
    all_to_all x1, waiting for transfers between devices, exchange_x(): return lax.all_to_all(x, 'tensor', 0, 0, axis_index_groups=runs, tiled=True)  5.68 us
    pallas_call x2, Pallas kernels, moment_of(): pl.pallas_call(partial(moment_kernel, scaling, nz), grid=(cols // tile,),...  5.07 us
  transfers between devices with their start and end apart: 21, of which 13 were waited for; matrix products, arithmetic and copies ran while one was open for 2% of the time, Pallas kernels for 4%

profile of v4, /device:TPU:14, one launch (start us, length us, event | category | flops | bytes accessed | tf_op | source)
XLA Modules:
  0.0 192.8 jit_solution(11655597853290033979)
XLA Ops:
  0.7 1.0 order.1
  1.7 1.3 fusion.60
  3.0 17.3 %collective-permute-start.60 = (bf16[96,1024]{1,0:T(8,128)(2,1)S(1)}, bf16[96,1024]{1,0:T(8,128)(2,1)S(1)}, u32[]{:S(2)}, u32[]{:S(2)}) collective-permute-start(bf16[96,1024]{1,0:T(8,128)(2,1)S(1)} %get-tuple-element.168), channel_id=1, source_target_pairs={{0,28},{1,29},{2,30},{3,31},{4,8},{5,9},{6,10},{7,11},{8,4},{9,5},... | collective-permute-start | bytes 589832 | tf_op jit(solution)/shard_map/sum_z/ppermute | solution.py:24
  20.4 1.9 collective-permute-start.64
  22.3 1.3 convolution_multiply_fusion.1
  23.6 0.3 convolution_multiply_fusion.2
  23.9 0.3 convolution_multiply_fusion.5
  24.1 4.5 %collective-permute-done.64 = bf16[96,1024]{1,0:T(8,128)(2,1)S(1)} collective-permute-done((bf16[96,1024]{1,0:T(8,128)(2,1)S(1)}, bf16[96,1024]{1,0:T(8,128)(2,1)S(1)}, u32[]{:S(2)}, u32[]{:S(2)}) %collective-permute-start.64) | collective-permute-done | bytes 196640 | tf_op jit(solution)/shard_map/sum_z/ppermute | solution.py:24
  28.6 0.3 add_convert_fusion.3
  28.9 2.2 %collective-permute-start.65 = (bf16[96,2048]{1,0:T(8,128)(2,1)S(1)}, bf16[96,2048]{1,0:T(8,128)(2,1)S(1)}, u32[]{:S(2)}, u32[]{:S(2)}) collective-permute-start(bf16[96,2048]{1,0:T(8,128)(2,1)S(1)} %add_convert_fusion.3), channel_id=1, source_target_pairs={{0,28},{1,29},{2,30},{3,31},{4,8},{5,9},{6,10},{7,11},{8,4},{9,5},... | collective-permute-start | bytes 1179656 | tf_op jit(solution)/shard_map/sum_z/ppermute | solution.py:24
  31.1 0.3 convolution_multiply_fusion.6
  31.4 0.3 add_convert_fusion.6
  31.6 1.9 collective-permute-start.61
  33.6 8.1 %collective-permute-done.65 = bf16[96,2048]{1,0:T(8,128)(2,1)S(1)} collective-permute-done((bf16[96,2048]{1,0:T(8,128)(2,1)S(1)}, bf16[96,2048]{1,0:T(8,128)(2,1)S(1)}, u32[]{:S(2)}, u32[]{:S(2)}) %collective-permute-start.65) | collective-permute-done | bytes 393248 | tf_op jit(solution)/shard_map/sum_z/ppermute | solution.py:24
  41.6 0.1 add_convert_fusion.2
  41.7 1.9 collective-permute-start.66
  43.7 0.1 add_convert_fusion.5
  43.7 5.0 %collective-permute-start.62 = (bf16[96,2048]{1,0:T(8,128)(2,1)S(1)}, bf16[96,2048]{1,0:T(8,128)(2,1)S(1)}, u32[]{:S(2)}, u32[]{:S(2)}) collective-permute-start(bf16[96,2048]{1,0:T(8,128)(2,1)S(1)} %add_convert_fusion.5), channel_id=1, source_target_pairs={{0,28},{1,29},{2,30},{3,31},{4,8},{5,9},{6,10},{7,11},{8,4},{9,5},... | collective-permute-start | bytes 1179656 | tf_op jit(solution)/shard_map/sum_z/ppermute | solution.py:24
  48.8 3.6 %collective-permute-done.66 = bf16[96,2048]{1,0:T(8,128)(2,1)S(1)} collective-permute-done((bf16[96,2048]{1,0:T(8,128)(2,1)S(1)}, bf16[96,2048]{1,0:T(8,128)(2,1)S(1)}, u32[]{:S(2)}, u32[]{:S(2)}) %collective-permute-start.66) | collective-permute-done | bytes 393248 | tf_op jit(solution)/shard_map/sum_z/ppermute | solution.py:24
  52.4 0.1 add_convert_fusion.1
  52.5 4.0 %collective-permute-start.67 = (bf16[96,2048]{1,0:T(8,128)(2,1)S(1)}, bf16[96,2048]{1,0:T(8,128)(2,1)S(1)}, u32[]{:S(2)}, u32[]{:S(2)}) collective-permute-start(bf16[96,2048]{1,0:T(8,128)(2,1)S(1)} %add_convert_fusion.1), channel_id=1, source_target_pairs={{0,28},{1,29},{2,30},{3,31},{4,8},{5,9},{6,10},{7,11},{8,4},{9,5},... | collective-permute-start | bytes 1179656 | tf_op jit(solution)/shard_map/sum_z/ppermute | solution.py:24
  56.4 0.1 add_convert_fusion.4
  56.5 2.5 %collective-permute-start.63 = (bf16[96,2048]{1,0:T(8,128)(2,1)S(1)}, bf16[96,2048]{1,0:T(8,128)(2,1)S(1)}, u32[]{:S(2)}, u32[]{:S(2)}) collective-permute-start(bf16[96,2048]{1,0:T(8,128)(2,1)S(1)} %add_convert_fusion.4), channel_id=1, source_target_pairs={{0,4},{1,5},{2,6},{3,7},{4,0},{5,1},{6,2},{7,3},{8,12},{9,13},{10,... | collective-permute-start | bytes 1179656 | tf_op jit(solution)/shard_map/sum_z/ppermute | solution.py:24
  59.1 0.3 convolution_multiply_fusion.7
  59.3 4.7 %collective-permute-done.67 = bf16[96,2048]{1,0:T(8,128)(2,1)S(1)} collective-permute-done((bf16[96,2048]{1,0:T(8,128)(2,1)S(1)}, bf16[96,2048]{1,0:T(8,128)(2,1)S(1)}, u32[]{:S(2)}, u32[]{:S(2)}) %collective-permute-start.67) | collective-permute-done | bytes 393248 | tf_op jit(solution)/shard_map/sum_z/ppermute | solution.py:24
  64.0 3.2 %collective-permute-done.63 = bf16[96,2048]{1,0:T(8,128)(2,1)S(1)} collective-permute-done((bf16[96,2048]{1,0:T(8,128)(2,1)S(1)}, bf16[96,2048]{1,0:T(8,128)(2,1)S(1)}, u32[]{:S(2)}, u32[]{:S(2)}) %collective-permute-start.63) | collective-permute-done | bytes 393248 | tf_op jit(solution)/shard_map/sum_z/ppermute | solution.py:24
  67.3 0.9 add_convert_fusion
  68.1 6.6 %all-to-all-start.5 = ((bf16[4,24,2048]{2,1,0:T(8,128)(2,1)}), bf16[4,24,2048]{2,1,0:T(8,128)(2,1)S(1)}, u32[]{:S(2)}, u32[]{:S(2)}) async-start(bf16[4,24,2048]{2,1,0:T(8,128)(2,1)} %bitcast.41), calls=%async_computation.5 | async-start | bytes 786432 | tf_op jit(solution)/shard_map/sum_x/all_to_all | solution.py:30
  75.5 0.1 dynamic-slice_bitcast_fusion
  75.5 0.2 convert_reduce_fusion.1
  75.7 5.7 %all-to-all-done.5 = bf16[4,24,2048]{2,1,0:T(8,128)(2,1)S(1)} async-done(((bf16[4,24,2048]{2,1,0:T(8,128)(2,1)}), bf16[4,24,2048]{2,1,0:T(8,128)(2,1)S(1)}, u32[]{:S(2)}, u32[]{:S(2)}) %all-to-all-start.5) | async-done | bytes 393248 | tf_op jit(solution)/shard_map/sum_x/all_to_all | solution.py:30
  81.5 1.6 fusion.62
  83.0 108.7 %conditional.1 = (bf16[1,768,128]{2,1,0:T(8,128)(2,1)S(1)}, bf16[1,128,2048]{2,1,0:T(8,128)(2,1)S(1)}, bf16[1,128,2048]{2,1,0:T(8,128)(2,1)S(1)}) conditional(s32[]{:T(128)} %clamp.3, (bf16[24,2048]{1,0:T(8,128)(2,1)S(1)}, bf16[128,2048]{1,0:T(8,128)(2,1)S(1)}, s32[1]{0:T(128)}, bf16[32,24,128]{2,1,0:T(8,128)(2,1)S(1)}, ...), branch_computations={%region_2.3_spmd, %region_3.4_spmd, %region_4.5_spmd, %region_5.6_... | conditional | flops 812122112 | bytes 48989056 | solution.py:196
  83.1 11.2 %all_to_all.43 = bf16[4,24,2048]{2,1,0:T(8,128)(2,1)S(1)} all-to-all(bf16[4,24,2048]{2,1,0:T(8,128)(2,1)S(1)} %tile.14), channel_id=1, replica_groups={{0,1,2,3},{4,5,6,7},{8,9,10,11},{12,13,14,15},{16,17,18,19},{20,21,22,2..., dimensions={0} | all-to-all | bytes 786432 | tf_op jit(solution)/shard_map/cond/branch_4_fun/gather_x/all_to_all | solution.py:30
  94.3 2.0 %collective-permute-start.49 = (bf16[96,2048]{1,0:T(8,128)(2,1)S(1)}, bf16[96,2048]{1,0:T(8,128)(2,1)S(1)}, u32[]{:S(2)}, u32[]{:S(2)}) collective-permute-start(bf16[96,2048]{1,0:T(8,128)(2,1)S(1)} %bitcast.129), channel_id=1, source_target_pairs={{0,28},{1,29},{2,30},{3,31},{4,8},{5,9},{6,10},{7,11},{8,4},{9,5},... | collective-permute-start | bytes 1179656 | tf_op jit(solution)/shard_map/cond/branch_4_fun/gather_z/ppermute | solution.py:24
  96.3 1.9 collective-permute-start.48
  98.2 6.9 %collective-permute-done.49.refs_7_.refs_8_ = bf16[96,2048]{1,0:T(8,128)(2,1)S(1)} collective-permute-done((bf16[96,2048]{1,0:T(8,128)(2,1)S(1)}, bf16[96,2048]{1,0:T(8,128)(2,1)S(1)}, u32[]{:S(2)}, u32[]{:S(2)}) %collective-permute-start.49) | collective-permute-done | bytes 393248 | tf_op jit(solution)/shard_map/cond/branch_4_fun/gather_z/ppermute | solution.py:24
  105.1 1.9 collective-permute-start.50
  107.1 1.9 collective-permute-done.48.refs_1_.refs_2_
  109.0 3.6 %collective-permute-start.51 = (bf16[96,2048]{1,0:T(8,128)(2,1)S(1)}, bf16[96,2048]{1,0:T(8,128)(2,1)S(1)}, u32[]{:S(2)}, u32[]{:S(2)}) collective-permute-start(bf16[96,2048]{1,0:T(8,128)(2,1)S(1)} %collective-permute-done.48.refs_1_.refs_2_), channel_id=1, source_target_pairs={{0,28},{1,29},{2,30},{3,31},{4,8},{5,9},{6,10},{7,11},{8,4},{9,5},... | collective-permute-start | bytes 1179656 | tf_op jit(solution)/shard_map/cond/branch_4_fun/gather_z/ppermute | solution.py:24
  112.6 8.2 %collective-permute-start.52 = (bf16[128,1024]{1,0:T(8,128)(2,1)S(1)}, bf16[128,1024]{1,0:T(8,128)(2,1)S(1)}, u32[]{:S(2)}, u32[]{:S(2)}) collective-permute-start(bf16[128,1024]{1,0:T(8,128)(2,1)S(1)} %get-tuple-element.165), channel_id=1, source_target_pairs={{0,512},{32,544},{64,576},{96,608},{128,640},{160,672},{192,704},{... | collective-permute-start | bytes 786440 | tf_op jit(solution)/shard_map/cond/branch_4_fun/early_partner/ppermute | solution.py:35
  120.8 5.9 %collective-permute-done.52 = bf16[128,1024]{1,0:T(8,128)(2,1)S(1)} collective-permute-done((bf16[128,1024]{1,0:T(8,128)(2,1)S(1)}, bf16[128,1024]{1,0:T(8,128)(2,1)S(1)}, u32[]{:S(2)}, u32[]{:S(2)}) %collective-permute-start.52) | collective-permute-done | bytes 262176 | tf_op jit(solution)/shard_map/cond/branch_4_fun/early_partner/ppermute | solution.py:35
  126.7 3.5 %collective-permute-start.53 = (bf16[96,2048]{1,0:T(8,128)(2,1)S(1)}, bf16[96,2048]{1,0:T(8,128)(2,1)S(1)}, u32[]{:S(2)}, u32[]{:S(2)}) collective-permute-start(bf16[96,2048]{1,0:T(8,128)(2,1)S(1)} %collective-permute-done.51.refs_6_.refs_7_), channel_id=1, source_target_pairs={{0,4},{1,5},{2,6},{3,7},{4,0},{5,1},{6,2},{7,3},{8,12},{9,13},{10,... | collective-permute-start | bytes 1179656 | tf_op jit(solution)/shard_map/cond/branch_4_fun/gather_z/ppermute | solution.py:24
  130.2 7.1 %collective-permute-start.54 = (bf16[96,2048]{1,0:T(8,128)(2,1)S(1)}, bf16[96,2048]{1,0:T(8,128)(2,1)S(1)}, u32[]{:S(2)}, u32[]{:S(2)}) collective-permute-start(bf16[96,2048]{1,0:T(8,128)(2,1)S(1)} %collective-permute-done.50.refs_2_.refs_3_), channel_id=1, source_target_pairs={{0,28},{1,29},{2,30},{3,31},{4,8},{5,9},{6,10},{7,11},{8,4},{9,5},... | collective-permute-start | bytes 1179656 | tf_op jit(solution)/shard_map/cond/branch_4_fun/gather_z/ppermute | solution.py:24
  137.3 8.3 %collective-permute-start.55 = (bf16[128,1024]{1,0:T(8,128)(2,1)S(1)}, bf16[128,1024]{1,0:T(8,128)(2,1)S(1)}, u32[]{:S(2)}, u32[]{:S(2)}) collective-permute-start(bf16[128,1024]{1,0:T(8,128)(2,1)S(1)} %get-tuple-element.164), channel_id=1, source_target_pairs={{0,512},{32,544},{64,576},{96,608},{128,640},{160,672},{192,704},{... | collective-permute-start | bytes 786440 | tf_op jit(solution)/shard_map/cond/branch_4_fun/early_partner/ppermute | solution.py:35
  145.5 10.0 %collective-permute-done.55 = bf16[128,1024]{1,0:T(8,128)(2,1)S(1)} collective-permute-done((bf16[128,1024]{1,0:T(8,128)(2,1)S(1)}, bf16[128,1024]{1,0:T(8,128)(2,1)S(1)}, u32[]{:S(2)}, u32[]{:S(2)}) %collective-permute-start.55) | collective-permute-done | bytes 262176 | tf_op jit(solution)/shard_map/cond/branch_4_fun/early_partner/ppermute | solution.py:35
  155.5 0.7 copy-done.72
  156.3 2.4 %collective-permute-start.56 = (bf16[96,1024]{1,0:T(8,128)(2,1)S(1)}, bf16[96,1024]{1,0:T(8,128)(2,1)S(1)}, u32[]{:S(2)}, u32[]{:S(2)}) collective-permute-start(bf16[96,1024]{1,0:T(8,128)(2,1)S(1)} %slice.104), channel_id=1, source_target_pairs={{0,28},{1,29},{2,30},{3,31},{4,8},{5,9},{6,10},{7,11},{8,4},{9,5},... | collective-permute-start | bytes 589832 | tf_op jit(solution)/shard_map/cond/branch_4_fun/gather_z/ppermute | solution.py:24
  158.6 0.7 slice.105
  159.3 1.9 collective-permute-start.57
  161.3 3.8 %collective-permute-done.56.refs_4_.refs_5_ = bf16[96,1024]{1,0:T(8,128)(2,1)S(1)} collective-permute-done((bf16[96,1024]{1,0:T(8,128)(2,1)S(1)}, bf16[96,1024]{1,0:T(8,128)(2,1)S(1)}, u32[]{:S(2)}, u32[]{:S(2)}) %collective-permute-start.56) | collective-permute-done | bytes 196640 | tf_op jit(solution)/shard_map/cond/branch_4_fun/gather_z/ppermute | solution.py:24
  165.1 0.6 copy-done.51
  165.7 2.5 %moment.18 = bf16[128,1024]{1,0:T(8,128)(2,1)} custom-call(bf16[768,128]{1,0:T(8,128)(2,1)S(1)} %bitcast.107, bf16[96,2048]{1,0:T(8,128)(2,1)} %bitcast.131, bf16[96,2048]{1,0:T(8,128)(2,1)} %copy-done.26, bf16[96,2048]{1,0:T(8,128)(2,1)} %copy-done.31, bf16[96,2048]{1,0:T(8,128)(2,1)} %copy-done.11, bf16[96,1024]{1,0:T(8,128)(2,1)} %copy-done.51, ...), custom_call_target="tpu_custom_call" | custom-call | flops 201326592 | bytes 2097152 | tf_op jit(solution)/shard_map/cond/branch_4_fun/moment/pallas_call | solution.py:66
  168.2 5.6 %collective-permute-start.58 = (bf16[128,1024]{1,0:T(8,128)(2,1)}, bf16[128,1024]{1,0:T(8,128)(2,1)S(1)}, u32[]{:S(2)}, u32[]{:S(2)}) collective-permute-start(bf16[128,1024]{1,0:T(8,128)(2,1)} %moment.18), channel_id=1, source_target_pairs={{0,512},{32,544},{64,576},{96,608},{128,640},{160,672},{192,704},{... | collective-permute-start | bytes 786440 | tf_op jit(solution)/shard_map/cond/branch_4_fun/partner/ppermute | solution.py:35
  173.9 2.6 %moment.19 = bf16[128,1024]{1,0:T(8,128)(2,1)} custom-call(bf16[768,128]{1,0:T(8,128)(2,1)S(1)} %bitcast.108, bf16[96,2048]{1,0:T(8,128)(2,1)} %bitcast.132, bf16[96,2048]{1,0:T(8,128)(2,1)} %copy-done.26, bf16[96,2048]{1,0:T(8,128)(2,1)} %copy-done.31, bf16[96,2048]{1,0:T(8,128)(2,1)} %copy-done.11, ...), custom_call_target="tpu_custom_call" | custom-call | flops 201326592 | bytes 2097152 | tf_op jit(solution)/shard_map/cond/branch_4_fun/moment/pallas_call | solution.py:66
  176.4 4.4 %collective-permute-start.59 = (bf16[128,1024]{1,0:T(8,128)(2,1)}, bf16[128,1024]{1,0:T(8,128)(2,1)S(1)}, u32[]{:S(2)}, u32[]{:S(2)}) collective-permute-start(bf16[128,1024]{1,0:T(8,128)(2,1)} %moment.19), channel_id=1, source_target_pairs={{0,512},{32,544},{64,576},{96,608},{128,640},{160,672},{192,704},{... | collective-permute-start | bytes 786440 | tf_op jit(solution)/shard_map/cond/branch_4_fun/partner/ppermute | solution.py:35
  180.8 3.3 %back.9 = bf16[32,24,128]{2,1,0:T(8,128)(2,1)S(1)} custom-call(s32[1]{0:T(128)} %get-tuple-element.107.place_ref, bf16[96,2048]{1,0:T(8,128)(2,1)} %bitcast.133, bf16[96,2048]{1,0:T(8,128)(2,1)} %copy-done.26, bf16[96,2048]{1,0:T(8,128)(2,1)} %copy-done.31, bf16[96,2048]{1,0:T(8,128)(2,1)} %copy-done.11, bf16[96,1024]{1,0:T(8,128)(2,1)} %copy-done.51, ...), custom_call_target="tpu_custom_call" | custom-call | flops 402653184 | bytes 3145728 | tf_op jit(solution)/shard_map/cond/branch_4_fun/back/back/pallas_call | solution.py:178
  184.1 3.0 %collective-permute-done.58 = bf16[128,1024]{1,0:T(8,128)(2,1)S(1)} collective-permute-done((bf16[128,1024]{1,0:T(8,128)(2,1)}, bf16[128,1024]{1,0:T(8,128)(2,1)S(1)}, u32[]{:S(2)}, u32[]{:S(2)}) %collective-permute-start.58) | collective-permute-done | bytes 262176 | tf_op jit(solution)/shard_map/cond/branch_4_fun/partner/ppermute | solution.py:35
  187.1 3.9 %collective-permute-done.59 = bf16[128,1024]{1,0:T(8,128)(2,1)S(1)} collective-permute-done((bf16[128,1024]{1,0:T(8,128)(2,1)}, bf16[128,1024]{1,0:T(8,128)(2,1)S(1)}, u32[]{:S(2)}, u32[]{:S(2)}) %collective-permute-start.59) | collective-permute-done | bytes 262176 | tf_op jit(solution)/shard_map/cond/branch_4_fun/partner/ppermute | solution.py:35
  191.0 0.5 fusion.53
  191.5 0.1 maximum_bitcast_fusion.8
  191.8 0.8 copy-done.52
  192.6 0.2 copy-done.53
  192.7 0.1 copy-done.74
  (51 shorter events, 0.3 us)
Async XLA Ops:
  0.6 23.0 %copy-start = (bf16[1,128,2048]{2,1,0:T(8,128)(2,1)S(1)}, bf16[1,128,2048]{2,1,0:T(8,128)(2,1)}, u32[]{:S(2)}) copy-start(bf16[1,128,2048]{2,1,0:T(8,128)(2,1)} %param.12) | copy-start | bytes 1572868
  3.0 28.3 %collective-permute-start.60 = (bf16[96,1024]{1,0:T(8,128)(2,1)S(1)}, bf16[96,1024]{1,0:T(8,128)(2,1)S(1)}, u32[]{:S(2)}, u32[]{:S(2)}) collective-permute-start(bf16[96,1024]{1,0:T(8,128)(2,1)S(1)} %get-tuple-element.168), channel_id=1, source_target_pairs={{0,28},{1,29},{2,30},{3,31},{4,8},{5,9},{6,10},{7,11},{8,4},{9,5},... | collective-permute-start | bytes 589832 | tf_op jit(solution)/shard_map/sum_z/ppermute | solution.py:24
  20.4 8.3 %collective-permute-start.64 = (bf16[96,1024]{1,0:T(8,128)(2,1)S(1)}, bf16[96,1024]{1,0:T(8,128)(2,1)S(1)}, u32[]{:S(2)}, u32[]{:S(2)}) collective-permute-start(bf16[96,1024]{1,0:T(8,128)(2,1)S(1)} %get-tuple-element.169), channel_id=1, source_target_pairs={{0,4},{1,5},{2,6},{3,7},{4,0},{5,1},{6,2},{7,3},{8,12},{9,13},{10,... | collective-permute-start | bytes 589832 | tf_op jit(solution)/shard_map/sum_z/ppermute | solution.py:24
  28.9 12.8 %collective-permute-start.65 = (bf16[96,2048]{1,0:T(8,128)(2,1)S(1)}, bf16[96,2048]{1,0:T(8,128)(2,1)S(1)}, u32[]{:S(2)}, u32[]{:S(2)}) collective-permute-start(bf16[96,2048]{1,0:T(8,128)(2,1)S(1)} %add_convert_fusion.3), channel_id=1, source_target_pairs={{0,28},{1,29},{2,30},{3,31},{4,8},{5,9},{6,10},{7,11},{8,4},{9,5},... | collective-permute-start | bytes 1179656 | tf_op jit(solution)/shard_map/sum_z/ppermute | solution.py:24
  31.6 12.0 %collective-permute-start.61 = (bf16[96,2048]{1,0:T(8,128)(2,1)S(1)}, bf16[96,2048]{1,0:T(8,128)(2,1)S(1)}, u32[]{:S(2)}, u32[]{:S(2)}) collective-permute-start(bf16[96,2048]{1,0:T(8,128)(2,1)S(1)} %add_convert_fusion.6), channel_id=1, source_target_pairs={{0,4},{1,5},{2,6},{3,7},{4,0},{5,1},{6,2},{7,3},{8,12},{9,13},{10,... | collective-permute-start | bytes 1179656 | tf_op jit(solution)/shard_map/sum_z/ppermute | solution.py:24
  41.7 10.6 %collective-permute-start.66 = (bf16[96,2048]{1,0:T(8,128)(2,1)S(1)}, bf16[96,2048]{1,0:T(8,128)(2,1)S(1)}, u32[]{:S(2)}, u32[]{:S(2)}) collective-permute-start(bf16[96,2048]{1,0:T(8,128)(2,1)S(1)} %add_convert_fusion.2), channel_id=1, source_target_pairs={{0,4},{1,5},{2,6},{3,7},{4,0},{5,1},{6,2},{7,3},{8,12},{9,13},{10,... | collective-permute-start | bytes 1179656 | tf_op jit(solution)/shard_map/sum_z/ppermute | solution.py:24
  43.7 12.7 %collective-permute-start.62 = (bf16[96,2048]{1,0:T(8,128)(2,1)S(1)}, bf16[96,2048]{1,0:T(8,128)(2,1)S(1)}, u32[]{:S(2)}, u32[]{:S(2)}) collective-permute-start(bf16[96,2048]{1,0:T(8,128)(2,1)S(1)} %add_convert_fusion.5), channel_id=1, source_target_pairs={{0,28},{1,29},{2,30},{3,31},{4,8},{5,9},{6,10},{7,11},{8,4},{9,5},... | collective-permute-start | bytes 1179656 | tf_op jit(solution)/shard_map/sum_z/ppermute | solution.py:24
  52.4 23.0 %copy-start.75 = (s32[1,768]{1,0:T(1,128)S(1)}, s32[1,768]{1,0:T(1,128)}, u32[]{:S(2)}) copy-start(s32[1,768]{1,0:T(1,128)} %param.15) | copy-start | bytes 9220
  52.4 30.6 %copy-start.1 = (bf16[1,128,2048]{2,1,0:T(8,128)(2,1)S(1)}, bf16[1,128,2048]{2,1,0:T(8,128)(2,1)}, u32[]{:S(2)}) copy-start(bf16[1,128,2048]{2,1,0:T(8,128)(2,1)} %param.13) | copy-start | bytes 1572868
  52.5 11.6 %collective-permute-start.67 = (bf16[96,2048]{1,0:T(8,128)(2,1)S(1)}, bf16[96,2048]{1,0:T(8,128)(2,1)S(1)}, u32[]{:S(2)}, u32[]{:S(2)}) collective-permute-start(bf16[96,2048]{1,0:T(8,128)(2,1)S(1)} %add_convert_fusion.1), channel_id=1, source_target_pairs={{0,28},{1,29},{2,30},{3,31},{4,8},{5,9},{6,10},{7,11},{8,4},{9,5},... | collective-permute-start | bytes 1179656 | tf_op jit(solution)/shard_map/sum_z/ppermute | solution.py:24
  56.5 10.7 %collective-permute-start.63 = (bf16[96,2048]{1,0:T(8,128)(2,1)S(1)}, bf16[96,2048]{1,0:T(8,128)(2,1)S(1)}, u32[]{:S(2)}, u32[]{:S(2)}) collective-permute-start(bf16[96,2048]{1,0:T(8,128)(2,1)S(1)} %add_convert_fusion.4), channel_id=1, source_target_pairs={{0,4},{1,5},{2,6},{3,7},{4,0},{5,1},{6,2},{7,3},{8,12},{9,13},{10,... | collective-permute-start | bytes 1179656 | tf_op jit(solution)/shard_map/sum_z/ppermute | solution.py:24
  68.1 13.3 %all-to-all-start.5 = ((bf16[4,24,2048]{2,1,0:T(8,128)(2,1)}), bf16[4,24,2048]{2,1,0:T(8,128)(2,1)S(1)}, u32[]{:S(2)}, u32[]{:S(2)}) async-start(bf16[4,24,2048]{2,1,0:T(8,128)(2,1)} %bitcast.41), calls=%async_computation.5 | async-start | bytes 786432 | tf_op jit(solution)/shard_map/sum_x/all_to_all | solution.py:30
  94.3 70.8 %copy-start.6 = (bf16[4,24,2048]{2,1,0:T(8,128)(2,1)}, bf16[4,24,2048]{2,1,0:T(8,128)(2,1)S(1)}, u32[]{:S(2)}) copy-start(bf16[4,24,2048]{2,1,0:T(8,128)(2,1)S(1)} %all_to_all.43) | copy-start | bytes 1179652 | tf_op jit(solution)/shard_map/cond
  94.3 10.9 %collective-permute-start.49 = (bf16[96,2048]{1,0:T(8,128)(2,1)S(1)}, bf16[96,2048]{1,0:T(8,128)(2,1)S(1)}, u32[]{:S(2)}, u32[]{:S(2)}) collective-permute-start(bf16[96,2048]{1,0:T(8,128)(2,1)S(1)} %bitcast.129), channel_id=1, source_target_pairs={{0,28},{1,29},{2,30},{3,31},{4,8},{5,9},{6,10},{7,11},{8,4},{9,5},... | collective-permute-start | bytes 1179656 | tf_op jit(solution)/shard_map/cond/branch_4_fun/gather_z/ppermute | solution.py:24
  96.3 12.6 %collective-permute-start.48 = (bf16[96,2048]{1,0:T(8,128)(2,1)S(1)}, bf16[96,2048]{1,0:T(8,128)(2,1)S(1)}, u32[]{:S(2)}, u32[]{:S(2)}) collective-permute-start(bf16[96,2048]{1,0:T(8,128)(2,1)S(1)} %bitcast.130), channel_id=1, source_target_pairs={{0,4},{1,5},{2,6},{3,7},{4,0},{5,1},{6,2},{7,3},{8,12},{9,13},{10,... | collective-permute-start | bytes 1179656 | tf_op jit(solution)/shard_map/cond/branch_4_fun/gather_z/ppermute | solution.py:24
  105.1 59.9 %copy-start.21 = (bf16[96,2048]{1,0:T(8,128)(2,1)}, bf16[96,2048]{1,0:T(8,128)(2,1)S(1)}, u32[]{:S(2)}) copy-start(bf16[96,2048]{1,0:T(8,128)(2,1)S(1)} %collective-permute-done.49.refs_7_.refs_8_) | copy-start | bytes 1179652 | tf_op jit(solution)/shard_map/cond
  105.1 21.5 %collective-permute-start.50 = (bf16[96,2048]{1,0:T(8,128)(2,1)S(1)}, bf16[96,2048]{1,0:T(8,128)(2,1)S(1)}, u32[]{:S(2)}, u32[]{:S(2)}) collective-permute-start(bf16[96,2048]{1,0:T(8,128)(2,1)S(1)} %collective-permute-done.49.refs_7_.refs_8_), channel_id=1, source_target_pairs={{0,4},{1,5},{2,6},{3,7},{4,0},{5,1},{6,2},{7,3},{8,12},{9,13},{10,... | collective-permute-start | bytes 1179656 | tf_op jit(solution)/shard_map/cond/branch_4_fun/gather_z/ppermute | solution.py:24
  109.0 56.1 %copy-start.26 = (bf16[96,2048]{1,0:T(8,128)(2,1)}, bf16[96,2048]{1,0:T(8,128)(2,1)S(1)}, u32[]{:S(2)}) copy-start(bf16[96,2048]{1,0:T(8,128)(2,1)S(1)} %collective-permute-done.48.refs_1_.refs_2_) | copy-start | bytes 1179652 | tf_op jit(solution)/shard_map/cond
  109.0 17.7 %collective-permute-start.51 = (bf16[96,2048]{1,0:T(8,128)(2,1)S(1)}, bf16[96,2048]{1,0:T(8,128)(2,1)S(1)}, u32[]{:S(2)}, u32[]{:S(2)}) collective-permute-start(bf16[96,2048]{1,0:T(8,128)(2,1)S(1)} %collective-permute-done.48.refs_1_.refs_2_), channel_id=1, source_target_pairs={{0,28},{1,29},{2,30},{3,31},{4,8},{5,9},{6,10},{7,11},{8,4},{9,5},... | collective-permute-start | bytes 1179656 | tf_op jit(solution)/shard_map/cond/branch_4_fun/gather_z/ppermute | solution.py:24
  112.6 14.1 %collective-permute-start.52 = (bf16[128,1024]{1,0:T(8,128)(2,1)S(1)}, bf16[128,1024]{1,0:T(8,128)(2,1)S(1)}, u32[]{:S(2)}, u32[]{:S(2)}) collective-permute-start(bf16[128,1024]{1,0:T(8,128)(2,1)S(1)} %get-tuple-element.165), channel_id=1, source_target_pairs={{0,512},{32,544},{64,576},{96,608},{128,640},{160,672},{192,704},{... | collective-permute-start | bytes 786440 | tf_op jit(solution)/shard_map/cond/branch_4_fun/early_partner/ppermute | solution.py:35
  126.7 28.8 %copy-start.62 = (bf16[128,1024]{1,0:T(8,128)(2,1)}, bf16[128,1024]{1,0:T(8,128)(2,1)S(1)}, u32[]{:S(2)}) copy-start(bf16[128,1024]{1,0:T(8,128)(2,1)S(1)} %collective-permute-done.52) | copy-start | bytes 786436 | tf_op jit(solution)/shard_map/cond
  126.7 29.5 %copy-start.31 = (bf16[96,2048]{1,0:T(8,128)(2,1)}, bf16[96,2048]{1,0:T(8,128)(2,1)S(1)}, u32[]{:S(2)}) copy-start(bf16[96,2048]{1,0:T(8,128)(2,1)S(1)} %collective-permute-done.50.refs_2_.refs_3_) | copy-start | bytes 1179652 | tf_op jit(solution)/shard_map/cond
  126.7 29.5 %copy-start.36 = (bf16[96,2048]{1,0:T(8,128)(2,1)}, bf16[96,2048]{1,0:T(8,128)(2,1)S(1)}, u32[]{:S(2)}) copy-start(bf16[96,2048]{1,0:T(8,128)(2,1)S(1)} %collective-permute-done.51.refs_6_.refs_7_) | copy-start | bytes 1179652 | tf_op jit(solution)/shard_map/cond
  126.7 28.8 %collective-permute-start.53 = (bf16[96,2048]{1,0:T(8,128)(2,1)S(1)}, bf16[96,2048]{1,0:T(8,128)(2,1)S(1)}, u32[]{:S(2)}, u32[]{:S(2)}) collective-permute-start(bf16[96,2048]{1,0:T(8,128)(2,1)S(1)} %collective-permute-done.51.refs_6_.refs_7_), channel_id=1, source_target_pairs={{0,4},{1,5},{2,6},{3,7},{4,0},{5,1},{6,2},{7,3},{8,12},{9,13},{10,... | collective-permute-start | bytes 1179656 | tf_op jit(solution)/shard_map/cond/branch_4_fun/gather_z/ppermute | solution.py:24
  130.2 26.0 %collective-permute-start.54 = (bf16[96,2048]{1,0:T(8,128)(2,1)S(1)}, bf16[96,2048]{1,0:T(8,128)(2,1)S(1)}, u32[]{:S(2)}, u32[]{:S(2)}) collective-permute-start(bf16[96,2048]{1,0:T(8,128)(2,1)S(1)} %collective-permute-done.50.refs_2_.refs_3_), channel_id=1, source_target_pairs={{0,28},{1,29},{2,30},{3,31},{4,8},{5,9},{6,10},{7,11},{8,4},{9,5},... | collective-permute-start | bytes 1179656 | tf_op jit(solution)/shard_map/cond/branch_4_fun/gather_z/ppermute | solution.py:24
  137.3 18.2 %collective-permute-start.55 = (bf16[128,1024]{1,0:T(8,128)(2,1)S(1)}, bf16[128,1024]{1,0:T(8,128)(2,1)S(1)}, u32[]{:S(2)}, u32[]{:S(2)}) collective-permute-start(bf16[128,1024]{1,0:T(8,128)(2,1)S(1)} %get-tuple-element.164), channel_id=1, source_target_pairs={{0,512},{32,544},{64,576},{96,608},{128,640},{160,672},{192,704},{... | collective-permute-start | bytes 786440 | tf_op jit(solution)/shard_map/cond/branch_4_fun/early_partner/ppermute | solution.py:35
  155.5 0.7 copy-start.72
  156.2 8.8 %copy-start.11 = (bf16[96,2048]{1,0:T(8,128)(2,1)}, bf16[96,2048]{1,0:T(8,128)(2,1)S(1)}, u32[]{:S(2)}) copy-start(bf16[96,2048]{1,0:T(8,128)(2,1)S(1)} %collective-permute-done.53.refs_3_.refs_4_) | copy-start | bytes 1179652 | tf_op jit(solution)/shard_map/cond
  156.2 8.8 %copy-start.16 = (bf16[96,2048]{1,0:T(8,128)(2,1)}, bf16[96,2048]{1,0:T(8,128)(2,1)S(1)}, u32[]{:S(2)}) copy-start(bf16[96,2048]{1,0:T(8,128)(2,1)S(1)} %collective-permute-done.54.refs_5_.refs_6_) | copy-start | bytes 1179652 | tf_op jit(solution)/shard_map/cond
  156.3 8.8 %collective-permute-start.56 = (bf16[96,1024]{1,0:T(8,128)(2,1)S(1)}, bf16[96,1024]{1,0:T(8,128)(2,1)S(1)}, u32[]{:S(2)}, u32[]{:S(2)}) collective-permute-start(bf16[96,1024]{1,0:T(8,128)(2,1)S(1)} %slice.104), channel_id=1, source_target_pairs={{0,28},{1,29},{2,30},{3,31},{4,8},{5,9},{6,10},{7,11},{8,4},{9,5},... | collective-permute-start | bytes 589832 | tf_op jit(solution)/shard_map/cond/branch_4_fun/gather_z/ppermute | solution.py:24
  159.3 14.5 %collective-permute-start.57 = (bf16[96,1024]{1,0:T(8,128)(2,1)}, bf16[96,1024]{1,0:T(8,128)(2,1)}, u32[]{:S(2)}, u32[]{:S(2)}) collective-permute-start(bf16[96,1024]{1,0:T(8,128)(2,1)} %slice.105), channel_id=1, source_target_pairs={{0,4},{1,5},{2,6},{3,7},{4,0},{5,1},{6,2},{7,3},{8,12},{9,13},{10,... | collective-permute-start | bytes 589832 | tf_op jit(solution)/shard_map/cond/branch_4_fun/gather_z/ppermute | solution.py:24
  165.0 0.7 copy-start.51
  168.2 22.7 %copy-start.41 = (bf16[128,1024]{1,0:T(8,128)(2,1)S(1)}, bf16[128,1024]{1,0:T(8,128)(2,1)}, u32[]{:S(2)}) copy-start(bf16[128,1024]{1,0:T(8,128)(2,1)} %moment.18) | copy-start | bytes 786436 | tf_op jit(solution)/shard_map/cond
  168.2 22.7 %copy-start.63 = (bf16[128,1024]{1,0:T(8,128)(2,1)S(1)}, bf16[128,1024]{1,0:T(8,128)(2,1)}, u32[]{:S(2)}) copy-start(bf16[128,1024]{1,0:T(8,128)(2,1)} %copy-done.62) | copy-start | bytes 786436 | tf_op jit(solution)/shard_map/cond
  168.2 22.7 %copy-start.73 = (bf16[128,1024]{1,0:T(8,128)(2,1)S(1)}, bf16[128,1024]{1,0:T(8,128)(2,1)}, u32[]{:S(2)}) copy-start(bf16[128,1024]{1,0:T(8,128)(2,1)} %copy-done.72) | copy-start | bytes 786436 | tf_op jit(solution)/shard_map/cond
  168.2 18.8 %collective-permute-start.58 = (bf16[128,1024]{1,0:T(8,128)(2,1)}, bf16[128,1024]{1,0:T(8,128)(2,1)S(1)}, u32[]{:S(2)}, u32[]{:S(2)}) collective-permute-start(bf16[128,1024]{1,0:T(8,128)(2,1)} %moment.18), channel_id=1, source_target_pairs={{0,512},{32,544},{64,576},{96,608},{128,640},{160,672},{192,704},{... | collective-permute-start | bytes 786440 | tf_op jit(solution)/shard_map/cond/branch_4_fun/partner/ppermute | solution.py:35
  176.4 14.5 %copy-start.46 = (bf16[128,1024]{1,0:T(8,128)(2,1)S(1)}, bf16[128,1024]{1,0:T(8,128)(2,1)}, u32[]{:S(2)}) copy-start(bf16[128,1024]{1,0:T(8,128)(2,1)} %moment.19) | copy-start | bytes 786436 | tf_op jit(solution)/shard_map/cond
  176.4 14.5 %collective-permute-start.59 = (bf16[128,1024]{1,0:T(8,128)(2,1)}, bf16[128,1024]{1,0:T(8,128)(2,1)S(1)}, u32[]{:S(2)}, u32[]{:S(2)}) collective-permute-start(bf16[128,1024]{1,0:T(8,128)(2,1)} %moment.19), channel_id=1, source_target_pairs={{0,512},{32,544},{64,576},{96,608},{128,640},{160,672},{192,704},{... | collective-permute-start | bytes 786440 | tf_op jit(solution)/shard_map/cond/branch_4_fun/partner/ppermute | solution.py:35
  191.8 0.8 copy-start.52
  191.8 1.0 copy-start.53
  191.8 1.0 copy-start.74

commit v5 on v4

--- a/solution.py
+++ b/solution.py
@@ -45,38 +45,77 @@
             out_ref[j * NX + k] = rows_ref[place_of(j, k, place_ref[0], nz)]
 
 
-def moment_kernel(scaling, nz, *refs):
-    heads_ref, blocks, mom_ref, out_ref, held = refs[0], refs[1 : 1 + nz], refs[-3], refs[-2], refs[-1]
+def times_rows(heads_ref, blocks, first, held):
     rows = blocks[0].shape[0]
-    for j in range(nz):
-        held[j * rows : (j + 1) * rows, :] = blocks[j][...]
-    total = lax.dot_general(
-        heads_ref[...], held[...], (((0,), (0,)), ((), ())), preferred_element_type=jnp.float32
-    )
+    for j, block in enumerate(blocks):
+        held[j * rows : (j + 1) * rows, :] = block[...]
+    count = len(blocks) * rows
+    return lax.dot_general(
+        heads_ref[first * rows : first * rows + count, :],
+        held[:count, :],
+        (((0,), (0,)), ((), ())),
+        preferred_element_type=jnp.float32,
+    )
+
+
+def near_kernel(nz, heads_ref, *refs):
+    blocks, out_ref, held, other = refs[:-3], refs[-3], refs[-2], refs[-1]
+    low = nz // 2 - 1
+    out_ref[...] = times_rows(heads_ref, blocks[:low], 0, held) + times_rows(
+        heads_ref, blocks[low:], nz // 2 + 2, other
+    )
+
+
+def moment_kernel(scaling, nz, heads_ref, *refs):
+    blocks, near_ref, mom_ref, out_ref, held = refs[:-4], refs[-4], refs[-3], refs[-2], refs[-1]
+    total = near_ref[...] + times_rows(heads_ref, blocks, nz // 2 - 1, held)
     out_ref[...] = (BETA_MOM * mom_ref[...].astype(jnp.float32) + total * scaling).astype(jnp.bfloat16)
 
 
-def moment_of(heads, blocks, mom, scaling, part):
+def near_of(heads, blocks):
+    nz, (rows, width) = len(blocks), blocks[0].shape
+    deep = heads.shape[1]
+    tile = min(512, width)
+    near = [blocks[j] for j in range(nz) if abs(j - nz // 2) > 1]
+    column = lambda n: pl.BlockSpec((n, tile), lambda i: (0, i))
+    return pl.pallas_call(
+        partial(near_kernel, nz),
+        grid=(width // tile,),
+        out_shape=jax.ShapeDtypeStruct((deep, width), jnp.float32),
+        in_specs=[pl.BlockSpec(heads.shape, lambda i: (0, 0))] + [column(rows)] * len(near),
+        out_specs=column(deep),
+        scratch_shapes=[
+            pltpu.VMEM(((nz // 2 - 1) * rows, tile), jnp.bfloat16),
+            pltpu.VMEM(((nz // 2 - 2) * rows, tile), jnp.bfloat16),
+        ],
+        cost_estimate=pl.CostEstimate(
+            flops=2 * deep * len(near) * rows * width, bytes_accessed=2 * len(near) * rows * width, transcendentals=0
+        ),
+        name="near",
+    )(heads, *near)
+
+
+def moment_of(heads, blocks, near, mom, scaling, part):
     nz, (rows, width) = len(blocks), blocks[0].shape
     deep, cols = heads.shape[1], width // 2
     tile = min(512, cols)
     first = part * cols // tile
     column = lambda n: pl.BlockSpec((n, tile), lambda i: (0, first + i))
     own = lambda n: pl.BlockSpec((n, tile), lambda i: (0, i))
+    far = [blocks[nz // 2 - 1], blocks[nz // 2][part], blocks[nz // 2 + 1]]
     return pl.pallas_call(
         partial(moment_kernel, scaling, nz),
         grid=(cols // tile,),
         out_shape=jax.ShapeDtypeStruct((deep, cols), jnp.bfloat16),
-        in_specs=[pl.BlockSpec(heads.shape, lambda i: (0, 0))]
-        + [own(rows) if j == nz // 2 else column(rows) for j in range(nz)]
-        + [column(deep)],
+        in_specs=[pl.BlockSpec(heads.shape, lambda i: (0, 0)), column(rows), own(rows), column(rows)]
+        + [column(deep)] * 2,
         out_specs=own(deep),
-        scratch_shapes=[pltpu.VMEM((nz * rows, tile), jnp.bfloat16)],
+        scratch_shapes=[pltpu.VMEM((len(far) * rows, tile), jnp.bfloat16)],
         cost_estimate=pl.CostEstimate(
-            flops=2 * heads.size * cols, bytes_accessed=2 * (nz * rows * cols + 2 * deep * cols), transcendentals=0
+            flops=2 * deep * len(far) * rows * cols, bytes_accessed=8 * deep * cols, transcendentals=0
         ),
         name="moment",
-    )(heads, *[b[part] if isinstance(b, tuple) else b for b in blocks], mom)
+    )(heads, *far, near, mom)
 
 
 def back_kernel(scaling, nz, place_ref, *refs):
@@ -150,28 +189,30 @@
     scaling = (deep * size) ** (-0.5)
     with jax.named_scope("early_partner"):
         half = width // 2
-        partner_w = [pass_replica(weight[:, :half], hop), pass_replica(weight[:, half:], hop)]
+        partner_w = pass_replica(weight, hop)
     with jax.named_scope("gather_x"):
         block = exchange_x(jnp.tile(grad, (NX, 1)))
     with jax.named_scope("gather_z"):
         held = [block] + [None] * (nz - 1)
         even = odd = block
         for m in range(1, nz // 2):
-            if m == nz // 2 - 1:
-                even, odd, partner_w[0] = lax.optimization_barrier((even, odd, partner_w[0]))
             even, odd = swap_z(odd, 0), swap_z(even, 1)
             held[m], held[-m] = even, odd
-        even, odd, partner_w[1] = lax.optimization_barrier((even, odd, partner_w[1]))
+        near = near_of(heads, held)
+        even = lax.optimization_barrier((near, even))[1]
+        odd = lax.optimization_barrier((near, odd))[1]
         held[nz // 2] = (swap_z(even[:, :half], 1), swap_z(odd[:, half:], 0))
     new_w, new_m = [], []
     for c in range(2):
         part = slice(c * half, (c + 1) * half)
-        moment = moment_of(heads, held, moment_in, scaling, c)
+        if c == 1:
+            moment_in, partner_w = lax.optimization_barrier((moment_in, partner_w))
+        moment = moment_of(heads, held, near, moment_in, scaling, c)
         with jax.named_scope("partner"):
             partner_m = pass_replica(moment, hop).astype(jnp.float32)
         moment = moment.astype(jnp.float32)
         updated = (weight[:, part].astype(jnp.float32) - STEP_RATE * moment).astype(jnp.bfloat16)
-        partner_u = (partner_w[c].astype(jnp.float32) - STEP_RATE * partner_m).astype(jnp.bfloat16)
+        partner_u = (partner_w[:, part].astype(jnp.float32) - STEP_RATE * partner_m).astype(jnp.bfloat16)
         new_w.append(((updated.astype(jnp.float32) + partner_u.astype(jnp.float32)) * 0.5).astype(jnp.bfloat16))
         new_m.append(((moment + partner_m) * 0.5).astype(jnp.bfloat16))
     with jax.named_scope("back"):

time: 194 us -> 180 us (0.928)
  the two profiles are of different devices: /device:TPU:14 before, /device:TPU:6 now
where the time goes in v5:
time: 180 us; the launch traced here: 179 us
  starting transfers between devices  76.8 us (43%)
  waiting for transfers between devices  64.8 us (36%)
  Pallas kernels  13.2 us (7%)
  blocking collectives  11.2 us (6%)
  other arithmetic  4.56 us (3%)
  matrix products  4.15 us (2%)
  local copies, waits for them, and re-layouts  2.58 us (1%)
    ppermute x16, starting transfers between devices, swap_z(): lax.ppermute(x, 'tensor', [(i, (i + step(i)) % size) for i in range(size)])  60.8 us
    ppermute x16, waiting for transfers between devices, swap_z(): lax.ppermute(x, 'tensor', [(i, (i + step(i)) % size) for i in range(size)])  33.2 us
    ppermute x3, waiting for transfers between devices, pass_replica(): lax.ppermute(x, 'replica', [(i, (i + by) % size) for i in range(size)])  26.1 us
    all_to_all x1, blocking collectives, exchange_x(): return lax.all_to_all(x, 'tensor', 0, 0, axis_index_groups=runs, tiled=True)  11.2 us
    ppermute x3, starting transfers between devices, pass_replica(): lax.ppermute(x, 'replica', [(i, (i + by) % size) for i in range(size)])  10.9 us
    all_to_all x1, waiting for transfers between devices, exchange_x(): return lax.all_to_all(x, 'tensor', 0, 0, axis_index_groups=runs, tiled=True)  5.54 us
    all_to_all x1, starting transfers between devices, exchange_x(): return lax.all_to_all(x, 'tensor', 0, 0, axis_index_groups=runs, tiled=True)  5.09 us
    pallas_call x2, Pallas kernels, moment_of(): pl.pallas_call(partial(moment_kernel, scaling, nz), grid=(cols // tile,),...  4.66 us
  transfers between devices with their start and end apart: 20, of which 13 were waited for; matrix products, arithmetic and copies ran while one was open for 2% of the time, Pallas kernels for 7%

profile of v5, /device:TPU:6, one launch (start us, length us, event | category | flops | bytes accessed | tf_op | source)
XLA Modules:
  0.0 179.3 jit_solution(14219301205070595347)
XLA Ops:
  0.6 0.0 copy-start
  0.7 1.0 order.1
  1.7 1.3 fusion.60
  3.0 5.2 %collective-permute-start.59 = (bf16[96,1024]{1,0:T(8,128)(2,1)S(1)}, bf16[96,1024]{1,0:T(8,128)(2,1)S(1)}, u32[]{:S(2)}, u32[]{:S(2)}) collective-permute-start(bf16[96,1024]{1,0:T(8,128)(2,1)S(1)} %get-tuple-element.149), channel_id=1, source_target_pairs={{0,4},{1,5},{2,6},{3,7},{4,0},{5,1},{6,2},{7,3},{8,12},{9,13},{10,... | collective-permute-start | bytes 589832 | tf_op jit(solution)/shard_map/sum_z/ppermute | solution.py:24
  8.2 14.0 %collective-permute-start.55 = (bf16[96,1024]{1,0:T(8,128)(2,1)S(1)}, bf16[96,1024]{1,0:T(8,128)(2,1)S(1)}, u32[]{:S(2)}, u32[]{:S(2)}) collective-permute-start(bf16[96,1024]{1,0:T(8,128)(2,1)S(1)} %get-tuple-element.148), channel_id=1, source_target_pairs={{0,28},{1,29},{2,30},{3,31},{4,8},{5,9},{6,10},{7,11},{8,4},{9,5},... | collective-permute-start | bytes 589832 | tf_op jit(solution)/shard_map/sum_z/ppermute | solution.py:24
  22.3 1.3 convolution_multiply_fusion.2
  23.6 0.3 convolution_multiply_fusion.1
  23.9 0.3 convolution_multiply_fusion.6
  24.1 0.3 add_convert_fusion.3
  24.4 4.7 %collective-permute-start.60 = (bf16[96,2048]{1,0:T(8,128)(2,1)S(1)}, bf16[96,2048]{1,0:T(8,128)(2,1)S(1)}, u32[]{:S(2)}, u32[]{:S(2)}) collective-permute-start(bf16[96,2048]{1,0:T(8,128)(2,1)S(1)} %add_convert_fusion.3), channel_id=1, source_target_pairs={{0,28},{1,29},{2,30},{3,31},{4,8},{5,9},{6,10},{7,11},{8,4},{9,5},... | collective-permute-start | bytes 1179656 | tf_op jit(solution)/shard_map/sum_z/ppermute | solution.py:24
  29.2 0.3 convolution_multiply_fusion.5
  29.4 0.3 add_convert_fusion.6
  29.7 1.9 %collective-permute-start.56 = (bf16[96,2048]{1,0:T(8,128)(2,1)S(1)}, bf16[96,2048]{1,0:T(8,128)(2,1)S(1)}, u32[]{:S(2)}, u32[]{:S(2)}) collective-permute-start(bf16[96,2048]{1,0:T(8,128)(2,1)S(1)} %add_convert_fusion.6), channel_id=1, source_target_pairs={{0,4},{1,5},{2,6},{3,7},{4,0},{5,1},{6,2},{7,3},{8,12},{9,13},{10,... | collective-permute-start | bytes 1179656 | tf_op jit(solution)/shard_map/sum_z/ppermute | solution.py:24
  31.6 6.5 %collective-permute-done.60 = bf16[96,2048]{1,0:T(8,128)(2,1)S(1)} collective-permute-done((bf16[96,2048]{1,0:T(8,128)(2,1)S(1)}, bf16[96,2048]{1,0:T(8,128)(2,1)S(1)}, u32[]{:S(2)}, u32[]{:S(2)}) %collective-permute-start.60) | collective-permute-done | bytes 393248 | tf_op jit(solution)/shard_map/sum_z/ppermute | solution.py:24
  38.1 0.1 add_convert_fusion.2
  38.2 1.9 %collective-permute-start.61 = (bf16[96,2048]{1,0:T(8,128)(2,1)S(1)}, bf16[96,2048]{1,0:T(8,128)(2,1)S(1)}, u32[]{:S(2)}, u32[]{:S(2)}) collective-permute-start(bf16[96,2048]{1,0:T(8,128)(2,1)S(1)} %add_convert_fusion.2), channel_id=1, source_target_pairs={{0,4},{1,5},{2,6},{3,7},{4,0},{5,1},{6,2},{7,3},{8,12},{9,13},{10,... | collective-permute-start | bytes 1179656 | tf_op jit(solution)/shard_map/sum_z/ppermute | solution.py:24
  40.1 1.2 collective-permute-done.56
  41.3 0.1 add_convert_fusion.5
  41.4 3.0 %collective-permute-start.57 = (bf16[96,2048]{1,0:T(8,128)(2,1)S(1)}, bf16[96,2048]{1,0:T(8,128)(2,1)S(1)}, u32[]{:S(2)}, u32[]{:S(2)}) collective-permute-start(bf16[96,2048]{1,0:T(8,128)(2,1)S(1)} %add_convert_fusion.5), channel_id=1, source_target_pairs={{0,28},{1,29},{2,30},{3,31},{4,8},{5,9},{6,10},{7,11},{8,4},{9,5},... | collective-permute-start | bytes 1179656 | tf_op jit(solution)/shard_map/sum_z/ppermute | solution.py:24
  44.3 5.4 %collective-permute-done.61 = bf16[96,2048]{1,0:T(8,128)(2,1)S(1)} collective-permute-done((bf16[96,2048]{1,0:T(8,128)(2,1)S(1)}, bf16[96,2048]{1,0:T(8,128)(2,1)S(1)}, u32[]{:S(2)}, u32[]{:S(2)}) %collective-permute-start.61) | collective-permute-done | bytes 393248 | tf_op jit(solution)/shard_map/sum_z/ppermute | solution.py:24
  49.7 0.1 add_convert_fusion.1
  49.8 3.7 %collective-permute-start.62 = (bf16[96,2048]{1,0:T(8,128)(2,1)S(1)}, bf16[96,2048]{1,0:T(8,128)(2,1)S(1)}, u32[]{:S(2)}, u32[]{:S(2)}) collective-permute-start(bf16[96,2048]{1,0:T(8,128)(2,1)S(1)} %add_convert_fusion.1), channel_id=1, source_target_pairs={{0,28},{1,29},{2,30},{3,31},{4,8},{5,9},{6,10},{7,11},{8,4},{9,5},... | collective-permute-start | bytes 1179656 | tf_op jit(solution)/shard_map/sum_z/ppermute | solution.py:24
  53.5 0.1 add_convert_fusion.4
  53.6 2.5 %collective-permute-start.58 = (bf16[96,2048]{1,0:T(8,128)(2,1)S(1)}, bf16[96,2048]{1,0:T(8,128)(2,1)S(1)}, u32[]{:S(2)}, u32[]{:S(2)}) collective-permute-start(bf16[96,2048]{1,0:T(8,128)(2,1)S(1)} %add_convert_fusion.4), channel_id=1, source_target_pairs={{0,4},{1,5},{2,6},{3,7},{4,0},{5,1},{6,2},{7,3},{8,12},{9,13},{10,... | collective-permute-start | bytes 1179656 | tf_op jit(solution)/shard_map/sum_z/ppermute | solution.py:24
  56.2 0.3 convolution_multiply_fusion.7
  56.4 5.4 %collective-permute-done.62 = bf16[96,2048]{1,0:T(8,128)(2,1)S(1)} collective-permute-done((bf16[96,2048]{1,0:T(8,128)(2,1)S(1)}, bf16[96,2048]{1,0:T(8,128)(2,1)S(1)}, u32[]{:S(2)}, u32[]{:S(2)}) %collective-permute-start.62) | collective-permute-done | bytes 393248 | tf_op jit(solution)/shard_map/sum_z/ppermute | solution.py:24
  61.8 1.5 collective-permute-done.58
  63.4 0.9 add_convert_fusion
  64.2 5.1 %all-to-all-start.5 = ((bf16[4,24,2048]{2,1,0:T(8,128)(2,1)}), bf16[4,24,2048]{2,1,0:T(8,128)(2,1)S(1)}, u32[]{:S(2)}, u32[]{:S(2)}) async-start(bf16[4,24,2048]{2,1,0:T(8,128)(2,1)} %bitcast.41), calls=%async_computation.5 | async-start | bytes 786432 | tf_op jit(solution)/shard_map/sum_x/all_to_all | solution.py:30
  70.0 0.1 dynamic-slice_bitcast_fusion
  70.1 0.2 convert_reduce_fusion.1
  70.3 5.5 %all-to-all-done.5 = bf16[4,24,2048]{2,1,0:T(8,128)(2,1)S(1)} async-done(((bf16[4,24,2048]{2,1,0:T(8,128)(2,1)}), bf16[4,24,2048]{2,1,0:T(8,128)(2,1)S(1)}, u32[]{:S(2)}, u32[]{:S(2)}) %all-to-all-start.5) | async-done | bytes 393248 | tf_op jit(solution)/shard_map/sum_x/all_to_all | solution.py:30
  75.9 1.6 fusion.62
  77.4 100.8 %conditional.1 = (bf16[1,768,128]{2,1,0:T(8,128)(2,1)S(1)}, bf16[1,128,2048]{2,1,0:T(8,128)(2,1)S(1)}, bf16[1,128,2048]{2,1,0:T(8,128)(2,1)S(1)}) conditional(s32[]{:T(128)} %clamp.3, (bf16[24,2048]{1,0:T(8,128)(2,1)S(1)}, bf16[32,24,128]{2,1,0:T(8,128)(2,1)S(1)}, s32[1]{0:T(128)}, bf16[128,2048]{1,0:T(8,128)(2,1)S(1)}, ...), branch_computations={%region_2.3_spmd, %region_3.4_spmd, %region_4.5_spmd, %region_5.6_... | conditional | flops 812122112 | bytes 41255628 | solution.py:237
  77.5 11.2 %all_to_all.40 = bf16[4,24,2048]{2,1,0:T(8,128)(2,1)S(1)} all-to-all(bf16[4,24,2048]{2,1,0:T(8,128)(2,1)S(1)} %tile.11), channel_id=1, replica_groups={{0,1,2,3},{4,5,6,7},{8,9,10,11},{12,13,14,15},{16,17,18,19},{20,21,22,2..., dimensions={0} | all-to-all | bytes 786432 | tf_op jit(solution)/shard_map/cond/branch_1_fun/gather_x/all_to_all | solution.py:30
  88.7 2.5 %collective-permute-start.11 = (bf16[96,2048]{1,0:T(8,128)(2,1)S(1)}, bf16[96,2048]{1,0:T(8,128)(2,1)S(1)}, u32[]{:S(2)}, u32[]{:S(2)}) collective-permute-start(bf16[96,2048]{1,0:T(8,128)(2,1)S(1)} %bitcast.118), channel_id=1, source_target_pairs={{0,4},{1,5},{2,6},{3,7},{4,0},{5,1},{6,2},{7,3},{8,12},{9,13},{10,... | collective-permute-start | bytes 1179656 | tf_op jit(solution)/shard_map/cond/branch_1_fun/gather_z/ppermute | solution.py:24
  91.2 4.1 %collective-permute-start.12 = (bf16[96,2048]{1,0:T(8,128)(2,1)S(1)}, bf16[96,2048]{1,0:T(8,128)(2,1)S(1)}, u32[]{:S(2)}, u32[]{:S(2)}) collective-permute-start(bf16[96,2048]{1,0:T(8,128)(2,1)S(1)} %bitcast.119), channel_id=1, source_target_pairs={{0,28},{1,29},{2,30},{3,31},{4,8},{5,9},{6,10},{7,11},{8,4},{9,5},... | collective-permute-start | bytes 1179656 | tf_op jit(solution)/shard_map/cond/branch_1_fun/gather_z/ppermute | solution.py:24
  95.3 3.0 %collective-permute-done.11.refs_1_ = bf16[96,2048]{1,0:T(8,128)(2,1)S(1)} collective-permute-done((bf16[96,2048]{1,0:T(8,128)(2,1)S(1)}, bf16[96,2048]{1,0:T(8,128)(2,1)S(1)}, u32[]{:S(2)}, u32[]{:S(2)}) %collective-permute-start.11) | collective-permute-done | bytes 393248 | tf_op jit(solution)/shard_map/cond/branch_1_fun/gather_z/ppermute | solution.py:24
  98.4 4.1 %collective-permute-start.14 = (bf16[96,2048]{1,0:T(8,128)(2,1)S(1)}, bf16[96,2048]{1,0:T(8,128)(2,1)}, u32[]{:S(2)}, u32[]{:S(2)}) collective-permute-start(bf16[96,2048]{1,0:T(8,128)(2,1)S(1)} %collective-permute-done.11.refs_1_), channel_id=1, source_target_pairs={{0,28},{1,29},{2,30},{3,31},{4,8},{5,9},{6,10},{7,11},{8,4},{9,5},... | collective-permute-start | bytes 1179656 | tf_op jit(solution)/shard_map/cond/branch_1_fun/gather_z/ppermute | solution.py:24
  102.5 2.2 %collective-permute-done.12.refs_4_.refs_7_ = bf16[96,2048]{1,0:T(8,128)(2,1)S(1)} collective-permute-done((bf16[96,2048]{1,0:T(8,128)(2,1)S(1)}, bf16[96,2048]{1,0:T(8,128)(2,1)S(1)}, u32[]{:S(2)}, u32[]{:S(2)}) %collective-permute-start.12) | collective-permute-done | bytes 393248 | tf_op jit(solution)/shard_map/cond/branch_1_fun/gather_z/ppermute | solution.py:24
  104.7 1.9 %collective-permute-start.13 = (bf16[96,2048]{1,0:T(8,128)(2,1)S(1)}, bf16[96,2048]{1,0:T(8,128)(2,1)}, u32[]{:S(2)}, u32[]{:S(2)}) collective-permute-start(bf16[96,2048]{1,0:T(8,128)(2,1)S(1)} %collective-permute-done.12.refs_4_.refs_7_), channel_id=1, source_target_pairs={{0,4},{1,5},{2,6},{3,7},{4,0},{5,1},{6,2},{7,3},{8,12},{9,13},{10,... | collective-permute-start | bytes 1179656 | tf_op jit(solution)/shard_map/cond/branch_1_fun/gather_z/ppermute | solution.py:24
  106.6 2.7 %collective-permute-done.14.refs_3_.refs_6_ = bf16[96,2048]{1,0:T(8,128)(2,1)} collective-permute-done((bf16[96,2048]{1,0:T(8,128)(2,1)S(1)}, bf16[96,2048]{1,0:T(8,128)(2,1)}, u32[]{:S(2)}, u32[]{:S(2)}) %collective-permute-start.14) | collective-permute-done | bytes 393248 | tf_op jit(solution)/shard_map/cond/branch_1_fun/gather_z/ppermute | solution.py:24
  109.3 1.9 %collective-permute-start.15 = (bf16[96,2048]{1,0:T(8,128)(2,1)}, bf16[96,2048]{1,0:T(8,128)(2,1)S(1)}, u32[]{:S(2)}, u32[]{:S(2)}) collective-permute-start(bf16[96,2048]{1,0:T(8,128)(2,1)} %collective-permute-done.14.refs_3_.refs_6_), channel_id=1, source_target_pairs={{0,4},{1,5},{2,6},{3,7},{4,0},{5,1},{6,2},{7,3},{8,12},{9,13},{10,... | collective-permute-start | bytes 1179656 | tf_op jit(solution)/shard_map/cond/branch_1_fun/gather_z/ppermute | solution.py:24
  111.2 5.2 %collective-permute-done.13.refs_2_ = bf16[96,2048]{1,0:T(8,128)(2,1)} collective-permute-done((bf16[96,2048]{1,0:T(8,128)(2,1)S(1)}, bf16[96,2048]{1,0:T(8,128)(2,1)}, u32[]{:S(2)}, u32[]{:S(2)}) %collective-permute-start.13) | collective-permute-done | bytes 393248 | tf_op jit(solution)/shard_map/cond/branch_1_fun/gather_z/ppermute | solution.py:24
  116.4 5.4 %collective-permute-start.17 = (bf16[96,2048]{1,0:T(8,128)(2,1)}, bf16[96,2048]{1,0:T(8,128)(2,1)S(1)}, u32[]{:S(2)}, u32[]{:S(2)}) collective-permute-start(bf16[96,2048]{1,0:T(8,128)(2,1)} %collective-permute-done.13.refs_2_), channel_id=1, source_target_pairs={{0,28},{1,29},{2,30},{3,31},{4,8},{5,9},{6,10},{7,11},{8,4},{9,5},... | collective-permute-start | bytes 1179656 | tf_op jit(solution)/shard_map/cond/branch_1_fun/gather_z/ppermute | solution.py:24
  121.9 6.8 %collective-permute-start.19 = (bf16[128,2048]{1,0:T(8,128)(2,1)S(1)}, bf16[128,2048]{1,0:T(8,128)(2,1)}, u32[]{:S(2)}, u32[]{:S(2)}) collective-permute-start(bf16[128,2048]{1,0:T(8,128)(2,1)S(1)} %get-tuple-element.77.refs_9_), channel_id=1, source_target_pairs={{0,64},{32,96},{64,128},{96,160},{128,192},{160,224},{192,256},{22... | collective-permute-start | bytes 1572872 | tf_op jit(solution)/shard_map/cond/branch_1_fun/early_partner/ppermute | solution.py:35
  128.7 4.2 %near.6.refs_3_ = f32[128,2048]{1,0:T(8,128)} custom-call(bf16[768,128]{1,0:T(8,128)(2,1)S(1)} %bitcast.92, bf16[96,2048]{1,0:T(8,128)(2,1)} %bitcast.120, bf16[96,2048]{1,0:T(8,128)(2,1)} %copy-done.18, bf16[96,2048]{1,0:T(8,128)(2,1)} %collective-permute-done.13.refs_2_, bf16[96,2048]{1,0:T(8,128)(2,1)} %collective-permute-done.14.refs_3_.refs_6_, ...), custom_call_target="tpu_custom_call" | custom-call | flops 251658240 | bytes 1966080 | tf_op jit(solution)/shard_map/cond/branch_1_fun/gather_z/near/pallas_call | solution.py:81
  133.0 1.9 %collective-permute-start.16 = (bf16[96,1024]{1,0:T(8,128)(2,1)S(1)}, bf16[96,1024]{1,0:T(8,128)(2,1)S(1)}, u32[]{:S(2)}, u32[]{:S(2)}) collective-permute-start(bf16[96,1024]{1,0:T(8,128)(2,1)S(1)} %slice.102), channel_id=1, source_target_pairs={{0,28},{1,29},{2,30},{3,31},{4,8},{5,9},{6,10},{7,11},{8,4},{9,5},... | collective-permute-start | bytes 589832 | tf_op jit(solution)/shard_map/cond/branch_1_fun/gather_z/ppermute | solution.py:24
  135.0 1.9 %collective-permute-start.18 = (bf16[96,1024]{1,0:T(8,128)(2,1)S(1)}, bf16[96,1024]{1,0:T(8,128)(2,1)S(1)}, u32[]{:S(2)}, u32[]{:S(2)}) collective-permute-start(bf16[96,1024]{1,0:T(8,128)(2,1)S(1)} %slice.103), channel_id=1, source_target_pairs={{0,4},{1,5},{2,6},{3,7},{4,0},{5,1},{6,2},{7,3},{8,12},{9,13},{10,... | collective-permute-start | bytes 589832 | tf_op jit(solution)/shard_map/cond/branch_1_fun/gather_z/ppermute | solution.py:24
  136.9 13.5 %collective-permute-done.19 = bf16[128,2048]{1,0:T(8,128)(2,1)} collective-permute-done((bf16[128,2048]{1,0:T(8,128)(2,1)S(1)}, bf16[128,2048]{1,0:T(8,128)(2,1)}, u32[]{:S(2)}, u32[]{:S(2)}) %collective-permute-start.19) | collective-permute-done | bytes 524320 | tf_op jit(solution)/shard_map/cond/branch_1_fun/early_partner/ppermute | solution.py:35
  150.4 0.7 copy-done.38
  151.0 2.3 %moment.12 = bf16[128,1024]{1,0:T(8,128)(2,1)} custom-call(bf16[768,128]{1,0:T(8,128)(2,1)S(1)} %bitcast.93, bf16[96,2048]{1,0:T(8,128)(2,1)} %copy-done.3, bf16[96,1024]{1,0:T(8,128)(2,1)} %copy-done.38, bf16[96,2048]{1,0:T(8,128)(2,1)} %copy-done.8, f32[128,2048]{1,0:T(8,128)} %near.6.refs_3_, bf16[128,2048]{1,0:T(8,128)(2,1)S(1)} %bitcast.106), custom_call_target="tpu_custom_call" | custom-call | flops 75497472 | bytes 1048576 | tf_op jit(solution)/shard_map/cond/branch_1_fun/moment/pallas_call | solution.py:106
  153.4 2.0 %collective-permute-start.20 = (bf16[128,1024]{1,0:T(8,128)(2,1)}, bf16[128,1024]{1,0:T(8,128)(2,1)S(1)}, u32[]{:S(2)}, u32[]{:S(2)}) collective-permute-start(bf16[128,1024]{1,0:T(8,128)(2,1)} %moment.12), channel_id=1, source_target_pairs={{0,64},{32,96},{64,128},{96,160},{128,192},{160,224},{192,256},{22... | collective-permute-start | bytes 786440 | tf_op jit(solution)/shard_map/cond/branch_1_fun/partner/ppermute | solution.py:35
  155.4 0.7 copy-done.43
  156.1 2.3 %moment.13 = bf16[128,1024]{1,0:T(8,128)(2,1)} custom-call(bf16[768,128]{1,0:T(8,128)(2,1)S(1)} %bitcast.94, bf16[96,2048]{1,0:T(8,128)(2,1)} %copy-done.3, bf16[96,1024]{1,0:T(8,128)(2,1)} %copy-done.43, bf16[96,2048]{1,0:T(8,128)(2,1)} %copy-done.8, f32[128,2048]{1,0:T(8,128)} %near.6.refs_3_, bf16[128,2048]{1,0:T(8,128)(2,1)S(1)} %bitcast.107), custom_call_target="tpu_custom_call" | custom-call | flops 75497472 | bytes 1048576 | tf_op jit(solution)/shard_map/cond/branch_1_fun/moment/pallas_call | solution.py:106
  158.4 2.0 %collective-permute-start.21 = (bf16[128,1024]{1,0:T(8,128)(2,1)}, bf16[128,1024]{1,0:T(8,128)(2,1)S(1)}, u32[]{:S(2)}, u32[]{:S(2)}) collective-permute-start(bf16[128,1024]{1,0:T(8,128)(2,1)} %moment.13), channel_id=1, source_target_pairs={{0,64},{32,96},{64,128},{96,160},{128,192},{160,224},{192,256},{22... | collective-permute-start | bytes 786440 | tf_op jit(solution)/shard_map/cond/branch_1_fun/partner/ppermute | solution.py:35
  160.5 3.3 %back.6 = bf16[32,24,128]{2,1,0:T(8,128)(2,1)S(1)} custom-call(s32[1]{0:T(128)} %get-tuple-element.72.place_ref, bf16[96,2048]{1,0:T(8,128)(2,1)} %bitcast.121, bf16[96,2048]{1,0:T(8,128)(2,1)} %copy-done.18, bf16[96,2048]{1,0:T(8,128)(2,1)} %collective-permute-done.13.refs_2_, bf16[96,2048]{1,0:T(8,128)(2,1)} %copy-done.3, bf16[96,1024]{1,0:T(8,128)(2,1)} %copy-done.38, ...), custom_call_target="tpu_custom_call" | custom-call | flops 402653184 | bytes 3145728 | tf_op jit(solution)/shard_map/cond/branch_1_fun/back/back/pallas_call | solution.py:219
  163.8 9.9 %collective-permute-done.20 = bf16[128,1024]{1,0:T(8,128)(2,1)S(1)} collective-permute-done((bf16[128,1024]{1,0:T(8,128)(2,1)}, bf16[128,1024]{1,0:T(8,128)(2,1)S(1)}, u32[]{:S(2)}, u32[]{:S(2)}) %collective-permute-start.20) | collective-permute-done | bytes 262176 | tf_op jit(solution)/shard_map/cond/branch_1_fun/partner/ppermute | solution.py:35
  173.6 2.8 %collective-permute-done.21 = bf16[128,1024]{1,0:T(8,128)(2,1)S(1)} collective-permute-done((bf16[128,1024]{1,0:T(8,128)(2,1)}, bf16[128,1024]{1,0:T(8,128)(2,1)S(1)}, u32[]{:S(2)}, u32[]{:S(2)}) %collective-permute-start.21) | collective-permute-done | bytes 262176 | tf_op jit(solution)/shard_map/cond/branch_1_fun/partner/ppermute | solution.py:35
  176.4 1.5 fusion.17
  178.0 0.1 maximum_bitcast_fusion.2
  178.3 0.8 copy-done.47
  179.1 0.2 copy-done.48
  179.2 0.1 copy-done.49
  (39 shorter events, 0.3 us)
Async XLA Ops:
  0.6 23.0 %copy-start = (bf16[1,128,2048]{2,1,0:T(8,128)(2,1)S(1)}, bf16[1,128,2048]{2,1,0:T(8,128)(2,1)}, u32[]{:S(2)}) copy-start(bf16[1,128,2048]{2,1,0:T(8,128)(2,1)} %param.12) | copy-start | bytes 1572868
  3.0 21.1 %collective-permute-start.59 = (bf16[96,1024]{1,0:T(8,128)(2,1)S(1)}, bf16[96,1024]{1,0:T(8,128)(2,1)S(1)}, u32[]{:S(2)}, u32[]{:S(2)}) collective-permute-start(bf16[96,1024]{1,0:T(8,128)(2,1)S(1)} %get-tuple-element.149), channel_id=1, source_target_pairs={{0,4},{1,5},{2,6},{3,7},{4,0},{5,1},{6,2},{7,3},{8,12},{9,13},{10,... | collective-permute-start | bytes 589832 | tf_op jit(solution)/shard_map/sum_z/ppermute | solution.py:24
  8.2 21.2 %collective-permute-start.55 = (bf16[96,1024]{1,0:T(8,128)(2,1)S(1)}, bf16[96,1024]{1,0:T(8,128)(2,1)S(1)}, u32[]{:S(2)}, u32[]{:S(2)}) collective-permute-start(bf16[96,1024]{1,0:T(8,128)(2,1)S(1)} %get-tuple-element.148), channel_id=1, source_target_pairs={{0,28},{1,29},{2,30},{3,31},{4,8},{5,9},{6,10},{7,11},{8,4},{9,5},... | collective-permute-start | bytes 589832 | tf_op jit(solution)/shard_map/sum_z/ppermute | solution.py:24
  24.4 13.7 %collective-permute-start.60 = (bf16[96,2048]{1,0:T(8,128)(2,1)S(1)}, bf16[96,2048]{1,0:T(8,128)(2,1)S(1)}, u32[]{:S(2)}, u32[]{:S(2)}) collective-permute-start(bf16[96,2048]{1,0:T(8,128)(2,1)S(1)} %add_convert_fusion.3), channel_id=1, source_target_pairs={{0,28},{1,29},{2,30},{3,31},{4,8},{5,9},{6,10},{7,11},{8,4},{9,5},... | collective-permute-start | bytes 1179656 | tf_op jit(solution)/shard_map/sum_z/ppermute | solution.py:24
  29.7 11.6 %collective-permute-start.56 = (bf16[96,2048]{1,0:T(8,128)(2,1)S(1)}, bf16[96,2048]{1,0:T(8,128)(2,1)S(1)}, u32[]{:S(2)}, u32[]{:S(2)}) collective-permute-start(bf16[96,2048]{1,0:T(8,128)(2,1)S(1)} %add_convert_fusion.6), channel_id=1, source_target_pairs={{0,4},{1,5},{2,6},{3,7},{4,0},{5,1},{6,2},{7,3},{8,12},{9,13},{10,... | collective-permute-start | bytes 1179656 | tf_op jit(solution)/shard_map/sum_z/ppermute | solution.py:24
  38.2 11.6 %collective-permute-start.61 = (bf16[96,2048]{1,0:T(8,128)(2,1)S(1)}, bf16[96,2048]{1,0:T(8,128)(2,1)S(1)}, u32[]{:S(2)}, u32[]{:S(2)}) collective-permute-start(bf16[96,2048]{1,0:T(8,128)(2,1)S(1)} %add_convert_fusion.2), channel_id=1, source_target_pairs={{0,4},{1,5},{2,6},{3,7},{4,0},{5,1},{6,2},{7,3},{8,12},{9,13},{10,... | collective-permute-start | bytes 1179656 | tf_op jit(solution)/shard_map/sum_z/ppermute | solution.py:24
  41.4 12.1 %collective-permute-start.57 = (bf16[96,2048]{1,0:T(8,128)(2,1)S(1)}, bf16[96,2048]{1,0:T(8,128)(2,1)S(1)}, u32[]{:S(2)}, u32[]{:S(2)}) collective-permute-start(bf16[96,2048]{1,0:T(8,128)(2,1)S(1)} %add_convert_fusion.5), channel_id=1, source_target_pairs={{0,28},{1,29},{2,30},{3,31},{4,8},{5,9},{6,10},{7,11},{8,4},{9,5},... | collective-permute-start | bytes 1179656 | tf_op jit(solution)/shard_map/sum_z/ppermute | solution.py:24
  49.8 20.2 %copy-start.50 = (s32[1,768]{1,0:T(1,128)S(1)}, s32[1,768]{1,0:T(1,128)}, u32[]{:S(2)}) copy-start(s32[1,768]{1,0:T(1,128)} %param.15) | copy-start | bytes 9220
  49.8 27.6 %copy-start.1 = (bf16[1,128,2048]{2,1,0:T(8,128)(2,1)S(1)}, bf16[1,128,2048]{2,1,0:T(8,128)(2,1)}, u32[]{:S(2)}) copy-start(bf16[1,128,2048]{2,1,0:T(8,128)(2,1)} %param.13) | copy-start | bytes 1572868
  49.8 12.0 %collective-permute-start.62 = (bf16[96,2048]{1,0:T(8,128)(2,1)S(1)}, bf16[96,2048]{1,0:T(8,128)(2,1)S(1)}, u32[]{:S(2)}, u32[]{:S(2)}) collective-permute-start(bf16[96,2048]{1,0:T(8,128)(2,1)S(1)} %add_convert_fusion.1), channel_id=1, source_target_pairs={{0,28},{1,29},{2,30},{3,31},{4,8},{5,9},{6,10},{7,11},{8,4},{9,5},... | collective-permute-start | bytes 1179656 | tf_op jit(solution)/shard_map/sum_z/ppermute | solution.py:24
  53.6 9.7 %collective-permute-start.58 = (bf16[96,2048]{1,0:T(8,128)(2,1)S(1)}, bf16[96,2048]{1,0:T(8,128)(2,1)S(1)}, u32[]{:S(2)}, u32[]{:S(2)}) collective-permute-start(bf16[96,2048]{1,0:T(8,128)(2,1)S(1)} %add_convert_fusion.4), channel_id=1, source_target_pairs={{0,4},{1,5},{2,6},{3,7},{4,0},{5,1},{6,2},{7,3},{8,12},{9,13},{10,... | collective-permute-start | bytes 1179656 | tf_op jit(solution)/shard_map/sum_z/ppermute | solution.py:24
  64.2 11.6 %all-to-all-start.5 = ((bf16[4,24,2048]{2,1,0:T(8,128)(2,1)}), bf16[4,24,2048]{2,1,0:T(8,128)(2,1)S(1)}, u32[]{:S(2)}, u32[]{:S(2)}) async-start(bf16[4,24,2048]{2,1,0:T(8,128)(2,1)} %bitcast.41), calls=%async_computation.5 | async-start | bytes 786432 | tf_op jit(solution)/shard_map/sum_x/all_to_all | solution.py:30
  88.7 40.0 %copy-start.13 = (bf16[4,24,2048]{2,1,0:T(8,128)(2,1)}, bf16[4,24,2048]{2,1,0:T(8,128)(2,1)S(1)}, u32[]{:S(2)}) copy-start(bf16[4,24,2048]{2,1,0:T(8,128)(2,1)S(1)} %all_to_all.40) | copy-start | bytes 1179652 | tf_op jit(solution)/shard_map/cond
  88.7 9.7 %collective-permute-start.11 = (bf16[96,2048]{1,0:T(8,128)(2,1)S(1)}, bf16[96,2048]{1,0:T(8,128)(2,1)S(1)}, u32[]{:S(2)}, u32[]{:S(2)}) collective-permute-start(bf16[96,2048]{1,0:T(8,128)(2,1)S(1)} %bitcast.118), channel_id=1, source_target_pairs={{0,4},{1,5},{2,6},{3,7},{4,0},{5,1},{6,2},{7,3},{8,12},{9,13},{10,... | collective-permute-start | bytes 1179656 | tf_op jit(solution)/shard_map/cond/branch_1_fun/gather_z/ppermute | solution.py:24
  91.2 13.5 %collective-permute-start.12 = (bf16[96,2048]{1,0:T(8,128)(2,1)S(1)}, bf16[96,2048]{1,0:T(8,128)(2,1)S(1)}, u32[]{:S(2)}, u32[]{:S(2)}) collective-permute-start(bf16[96,2048]{1,0:T(8,128)(2,1)S(1)} %bitcast.119), channel_id=1, source_target_pairs={{0,28},{1,29},{2,30},{3,31},{4,8},{5,9},{6,10},{7,11},{8,4},{9,5},... | collective-permute-start | bytes 1179656 | tf_op jit(solution)/shard_map/cond/branch_1_fun/gather_z/ppermute | solution.py:24
  98.4 30.3 %copy-start.18 = (bf16[96,2048]{1,0:T(8,128)(2,1)}, bf16[96,2048]{1,0:T(8,128)(2,1)S(1)}, u32[]{:S(2)}) copy-start(bf16[96,2048]{1,0:T(8,128)(2,1)S(1)} %collective-permute-done.11.refs_1_) | copy-start | bytes 1179652 | tf_op jit(solution)/shard_map/cond
  98.4 11.0 %collective-permute-start.14 = (bf16[96,2048]{1,0:T(8,128)(2,1)S(1)}, bf16[96,2048]{1,0:T(8,128)(2,1)}, u32[]{:S(2)}, u32[]{:S(2)}) collective-permute-start(bf16[96,2048]{1,0:T(8,128)(2,1)S(1)} %collective-permute-done.11.refs_1_), channel_id=1, source_target_pairs={{0,28},{1,29},{2,30},{3,31},{4,8},{5,9},{6,10},{7,11},{8,4},{9,5},... | collective-permute-start | bytes 1179656 | tf_op jit(solution)/shard_map/cond/branch_1_fun/gather_z/ppermute | solution.py:24
  104.7 24.0 %copy-start.23 = (bf16[96,2048]{1,0:T(8,128)(2,1)}, bf16[96,2048]{1,0:T(8,128)(2,1)S(1)}, u32[]{:S(2)}) copy-start(bf16[96,2048]{1,0:T(8,128)(2,1)S(1)} %collective-permute-done.12.refs_4_.refs_7_) | copy-start | bytes 1179652 | tf_op jit(solution)/shard_map/cond
  104.7 11.7 %collective-permute-start.13 = (bf16[96,2048]{1,0:T(8,128)(2,1)S(1)}, bf16[96,2048]{1,0:T(8,128)(2,1)}, u32[]{:S(2)}, u32[]{:S(2)}) collective-permute-start(bf16[96,2048]{1,0:T(8,128)(2,1)S(1)} %collective-permute-done.12.refs_4_.refs_7_), channel_id=1, source_target_pairs={{0,4},{1,5},{2,6},{3,7},{4,0},{5,1},{6,2},{7,3},{8,12},{9,13},{10,... | collective-permute-start | bytes 1179656 | tf_op jit(solution)/shard_map/cond/branch_1_fun/gather_z/ppermute | solution.py:24
  109.3 23.6 %collective-permute-start.15 = (bf16[96,2048]{1,0:T(8,128)(2,1)}, bf16[96,2048]{1,0:T(8,128)(2,1)S(1)}, u32[]{:S(2)}, u32[]{:S(2)}) collective-permute-start(bf16[96,2048]{1,0:T(8,128)(2,1)} %collective-permute-done.14.refs_3_.refs_6_), channel_id=1, source_target_pairs={{0,4},{1,5},{2,6},{3,7},{4,0},{5,1},{6,2},{7,3},{8,12},{9,13},{10,... | collective-permute-start | bytes 1179656 | tf_op jit(solution)/shard_map/cond/branch_1_fun/gather_z/ppermute | solution.py:24
  116.4 18.5 %collective-permute-start.17 = (bf16[96,2048]{1,0:T(8,128)(2,1)}, bf16[96,2048]{1,0:T(8,128)(2,1)S(1)}, u32[]{:S(2)}, u32[]{:S(2)}) collective-permute-start(bf16[96,2048]{1,0:T(8,128)(2,1)} %collective-permute-done.13.refs_2_), channel_id=1, source_target_pairs={{0,28},{1,29},{2,30},{3,31},{4,8},{5,9},{6,10},{7,11},{8,4},{9,5},... | collective-permute-start | bytes 1179656 | tf_op jit(solution)/shard_map/cond/branch_1_fun/gather_z/ppermute | solution.py:24
  121.9 28.5 %collective-permute-start.19 = (bf16[128,2048]{1,0:T(8,128)(2,1)S(1)}, bf16[128,2048]{1,0:T(8,128)(2,1)}, u32[]{:S(2)}, u32[]{:S(2)}) collective-permute-start(bf16[128,2048]{1,0:T(8,128)(2,1)S(1)} %get-tuple-element.77.refs_9_), channel_id=1, source_target_pairs={{0,64},{32,96},{64,128},{96,160},{128,192},{160,224},{192,256},{22... | collective-permute-start | bytes 1572872 | tf_op jit(solution)/shard_map/cond/branch_1_fun/early_partner/ppermute | solution.py:35
  133.0 17.4 %copy-start.3 = (bf16[96,2048]{1,0:T(8,128)(2,1)}, bf16[96,2048]{1,0:T(8,128)(2,1)S(1)}, u32[]{:S(2)}) copy-start(bf16[96,2048]{1,0:T(8,128)(2,1)S(1)} %collective-permute-done.15.refs_3_.refs_0_) | copy-start | bytes 1179652 | tf_op jit(solution)/shard_map/cond
  133.0 17.4 %collective-permute-start.16 = (bf16[96,1024]{1,0:T(8,128)(2,1)S(1)}, bf16[96,1024]{1,0:T(8,128)(2,1)S(1)}, u32[]{:S(2)}, u32[]{:S(2)}) collective-permute-start(bf16[96,1024]{1,0:T(8,128)(2,1)S(1)} %slice.102), channel_id=1, source_target_pairs={{0,28},{1,29},{2,30},{3,31},{4,8},{5,9},{6,10},{7,11},{8,4},{9,5},... | collective-permute-start | bytes 589832 | tf_op jit(solution)/shard_map/cond/branch_1_fun/gather_z/ppermute | solution.py:24
  134.9 15.4 %copy-start.8 = (bf16[96,2048]{1,0:T(8,128)(2,1)}, bf16[96,2048]{1,0:T(8,128)(2,1)S(1)}, u32[]{:S(2)}) copy-start(bf16[96,2048]{1,0:T(8,128)(2,1)S(1)} %collective-permute-done.17.refs_5_.refs_2_) | copy-start | bytes 1179652 | tf_op jit(solution)/shard_map/cond
  135.0 20.5 %collective-permute-start.18 = (bf16[96,1024]{1,0:T(8,128)(2,1)S(1)}, bf16[96,1024]{1,0:T(8,128)(2,1)S(1)}, u32[]{:S(2)}, u32[]{:S(2)}) collective-permute-start(bf16[96,1024]{1,0:T(8,128)(2,1)S(1)} %slice.103), channel_id=1, source_target_pairs={{0,4},{1,5},{2,6},{3,7},{4,0},{5,1},{6,2},{7,3},{8,12},{9,13},{10,... | collective-permute-start | bytes 589832 | tf_op jit(solution)/shard_map/cond/branch_1_fun/gather_z/ppermute | solution.py:24
  150.4 0.7 copy-start.38
  153.4 23.1 %copy-start.28 = (bf16[128,1024]{1,0:T(8,128)(2,1)S(1)}, bf16[128,1024]{1,0:T(8,128)(2,1)}, u32[]{:S(2)}) copy-start(bf16[128,1024]{1,0:T(8,128)(2,1)} %moment.12) | copy-start | bytes 786436 | tf_op jit(solution)/shard_map/cond
  153.4 20.3 %collective-permute-start.20 = (bf16[128,1024]{1,0:T(8,128)(2,1)}, bf16[128,1024]{1,0:T(8,128)(2,1)S(1)}, u32[]{:S(2)}, u32[]{:S(2)}) collective-permute-start(bf16[128,1024]{1,0:T(8,128)(2,1)} %moment.12), channel_id=1, source_target_pairs={{0,64},{32,96},{64,128},{96,160},{128,192},{160,224},{192,256},{22... | collective-permute-start | bytes 786440 | tf_op jit(solution)/shard_map/cond/branch_1_fun/partner/ppermute | solution.py:35
  155.4 0.7 copy-start.43
  158.4 18.0 %copy-start.33 = (bf16[128,1024]{1,0:T(8,128)(2,1)S(1)}, bf16[128,1024]{1,0:T(8,128)(2,1)}, u32[]{:S(2)}) copy-start(bf16[128,1024]{1,0:T(8,128)(2,1)} %moment.13) | copy-start | bytes 786436 | tf_op jit(solution)/shard_map/cond
  158.4 18.0 %collective-permute-start.21 = (bf16[128,1024]{1,0:T(8,128)(2,1)}, bf16[128,1024]{1,0:T(8,128)(2,1)S(1)}, u32[]{:S(2)}, u32[]{:S(2)}) collective-permute-start(bf16[128,1024]{1,0:T(8,128)(2,1)} %moment.13), channel_id=1, source_target_pairs={{0,64},{32,96},{64,128},{96,160},{128,192},{160,224},{192,256},{22... | collective-permute-start | bytes 786440 | tf_op jit(solution)/shard_map/cond/branch_1_fun/partner/ppermute | solution.py:35
  178.3 0.8 copy-start.47
  178.3 1.0 copy-start.48
  178.3 1.0 copy-start.49

commit v6 on v5

--- a/solution.py
+++ b/solution.py
@@ -11,6 +11,7 @@
 BETA_MOM = 0.9
 STEP_RATE = 0.1
 NX = 4
+SMALL = pltpu.CompilerParams(vmem_limit_bytes=16 << 20)
 SCALARS = pl.BlockSpec(memory_space=pltpu.SMEM)
 
 
@@ -48,7 +49,7 @@
 def times_rows(heads_ref, blocks, first, held):
     rows = blocks[0].shape[0]
     for j, block in enumerate(blocks):
-        held[j * rows : (j + 1) * rows, :] = block[...]
+        held[j * rows : (j + 1) * rows, :] = block
     count = len(blocks) * rows
     return lax.dot_general(
         heads_ref[first * rows : first * rows + count, :],
@@ -60,16 +61,24 @@
 
 def near_kernel(nz, heads_ref, *refs):
     blocks, out_ref, held, other = refs[:-3], refs[-3], refs[-2], refs[-1]
-    low = nz // 2 - 1
-    out_ref[...] = times_rows(heads_ref, blocks[:low], 0, held) + times_rows(
-        heads_ref, blocks[low:], nz // 2 + 2, other
-    )
-
-
-def moment_kernel(scaling, nz, heads_ref, *refs):
+    low, tile = nz // 2 - 1, held.shape[1]
+    for c in range(0, out_ref.shape[1], tile):
+        part = [block[:, c : c + tile] for block in blocks]
+        out_ref[:, c : c + tile] = times_rows(heads_ref, part[:low], 0, held) + times_rows(
+            heads_ref, part[low:], nz // 2 + 2, other
+        )
+
+
+def moment_kernel(scaling, nz, first, heads_ref, *refs):
     blocks, near_ref, mom_ref, out_ref, held = refs[:-4], refs[-4], refs[-3], refs[-2], refs[-1]
-    total = near_ref[...] + times_rows(heads_ref, blocks, nz // 2 - 1, held)
-    out_ref[...] = (BETA_MOM * mom_ref[...].astype(jnp.float32) + total * scaling).astype(jnp.bfloat16)
+    tile = held.shape[1]
+    for c in range(0, out_ref.shape[1], tile):
+        own, full = slice(c, c + tile), slice(first + c, first + c + tile)
+        part = [blocks[0][:, full], blocks[1][:, own], blocks[2][:, full]]
+        total = near_ref[:, full] + times_rows(heads_ref, part, nz // 2 - 1, held)
+        out_ref[:, own] = (BETA_MOM * mom_ref[:, full].astype(jnp.float32) + total * scaling).astype(
+            jnp.bfloat16
+        )
 
 
 def near_of(heads, blocks):
@@ -77,13 +86,11 @@
     deep = heads.shape[1]
     tile = min(512, width)
     near = [blocks[j] for j in range(nz) if abs(j - nz // 2) > 1]
-    column = lambda n: pl.BlockSpec((n, tile), lambda i: (0, i))
     return pl.pallas_call(
         partial(near_kernel, nz),
-        grid=(width // tile,),
         out_shape=jax.ShapeDtypeStruct((deep, width), jnp.float32),
-        in_specs=[pl.BlockSpec(heads.shape, lambda i: (0, 0))] + [column(rows)] * len(near),
-        out_specs=column(deep),
+        in_specs=vmem(1 + len(near)),
+        out_specs=vmem(1)[0],
         scratch_shapes=[
             pltpu.VMEM(((nz // 2 - 1) * rows, tile), jnp.bfloat16),
             pltpu.VMEM(((nz // 2 - 2) * rows, tile), jnp.bfloat16),
@@ -92,6 +99,7 @@
             flops=2 * deep * len(near) * rows * width, bytes_accessed=2 * len(near) * rows * width, transcendentals=0
         ),
         name="near",
+        compiler_params=SMALL,
     )(heads, *near)
 
 
@@ -99,23 +107,33 @@
     nz, (rows, width) = len(blocks), blocks[0].shape
     deep, cols = heads.shape[1], width // 2
     tile = min(512, cols)
-    first = part * cols // tile
-    column = lambda n: pl.BlockSpec((n, tile), lambda i: (0, first + i))
-    own = lambda n: pl.BlockSpec((n, tile), lambda i: (0, i))
     far = [blocks[nz // 2 - 1], blocks[nz // 2][part], blocks[nz // 2 + 1]]
     return pl.pallas_call(
-        partial(moment_kernel, scaling, nz),
-        grid=(cols // tile,),
+        partial(moment_kernel, scaling, nz, part * cols),
         out_shape=jax.ShapeDtypeStruct((deep, cols), jnp.bfloat16),
-        in_specs=[pl.BlockSpec(heads.shape, lambda i: (0, 0)), column(rows), own(rows), column(rows)]
-        + [column(deep)] * 2,
-        out_specs=own(deep),
+        in_specs=vmem(3 + len(far)),
+        out_specs=vmem(1)[0],
         scratch_shapes=[pltpu.VMEM((len(far) * rows, tile), jnp.bfloat16)],
         cost_estimate=pl.CostEstimate(
             flops=2 * deep * len(far) * rows * cols, bytes_accessed=8 * deep * cols, transcendentals=0
         ),
         name="moment",
+        compiler_params=SMALL,
     )(heads, *far, near, mom)
+
+
+def mix_kernel(*refs):
+    w_ref, partner_w_ref, moments, new_w_ref, new_m_ref = refs[0], refs[1], refs[2:-2], refs[-2], refs[-1]
+    wide = lambda x: x.astype(jnp.float32)
+    narrow = lambda x: x.astype(jnp.bfloat16)
+    half = moments[0].shape[1]
+    for c in range(2):
+        part = slice(c * half, (c + 1) * half)
+        moment, partner_m = wide(moments[c][...]), wide(moments[2 + c][...])
+        updated = narrow(wide(w_ref[:, part]) - STEP_RATE * moment)
+        partner_u = narrow(wide(partner_w_ref[:, part]) - STEP_RATE * partner_m)
+        new_w_ref[:, part] = narrow((wide(updated) + wide(partner_u)) * 0.5)
+        new_m_ref[:, part] = narrow((moment + partner_m) * 0.5)
 
 
 def back_kernel(scaling, nz, place_ref, *refs):
@@ -150,6 +168,7 @@
             in_specs=[SCALARS] + vmem(1),
             out_specs=vmem(1)[0],
             name="order",
+            compiler_params=SMALL,
         )(place, heads_in.reshape(size, rows, deep)).reshape(tokens, deep)
     first_row = own * rows
     own_seg = lax.dynamic_slice_in_dim(seg_rows, first_row, rows, 0)
@@ -196,25 +215,28 @@
         held = [block] + [None] * (nz - 1)
         even = odd = block
         for m in range(1, nz // 2):
+            if m == 2:
+                even, odd, partner_w = lax.optimization_barrier((even, odd, partner_w))
             even, odd = swap_z(odd, 0), swap_z(even, 1)
             held[m], held[-m] = even, odd
         near = near_of(heads, held)
         even = lax.optimization_barrier((near, even))[1]
         odd = lax.optimization_barrier((near, odd))[1]
         held[nz // 2] = (swap_z(even[:, :half], 1), swap_z(odd[:, half:], 0))
-    new_w, new_m = [], []
+    moments, partner_m = [], []
     for c in range(2):
-        part = slice(c * half, (c + 1) * half)
-        if c == 1:
-            moment_in, partner_w = lax.optimization_barrier((moment_in, partner_w))
-        moment = moment_of(heads, held, near, moment_in, scaling, c)
+        moments.append(moment_of(heads, held, near, moment_in, scaling, c))
         with jax.named_scope("partner"):
-            partner_m = pass_replica(moment, hop).astype(jnp.float32)
-        moment = moment.astype(jnp.float32)
-        updated = (weight[:, part].astype(jnp.float32) - STEP_RATE * moment).astype(jnp.bfloat16)
-        partner_u = (partner_w[:, part].astype(jnp.float32) - STEP_RATE * partner_m).astype(jnp.bfloat16)
-        new_w.append(((updated.astype(jnp.float32) + partner_u.astype(jnp.float32)) * 0.5).astype(jnp.bfloat16))
-        new_m.append(((moment + partner_m) * 0.5).astype(jnp.bfloat16))
+            partner_m.append(pass_replica(moments[c], hop))
+    with jax.named_scope("mix"):
+        new_w, new_m = pl.pallas_call(
+            mix_kernel,
+            out_shape=[jax.ShapeDtypeStruct(weight.shape, jnp.bfloat16)] * 2,
+            in_specs=vmem(6),
+            out_specs=vmem(2),
+            name="mix",
+            compiler_params=SMALL,
+        )(weight, partner_w, *moments, *partner_m)
     with jax.named_scope("back"):
         attn_grad = pl.pallas_call(
             partial(back_kernel, scaling, nz),
@@ -225,9 +247,9 @@
                 flops=2 * tokens * width * deep, bytes_accessed=2 * tokens * width, transcendentals=0
             ),
             name="back",
+            compiler_params=SMALL,
         )(place, *[h[0] if isinstance(h, tuple) else h for h in held], held[nz // 2][1], weight).reshape(tokens, deep)
-    join = lambda pieces: jnp.concatenate(pieces, axis=1)
-    return attn_grad, join(new_w), join(new_m)
+    return attn_grad, new_w, new_m
 
 
 def program(attn_out, proj, momentum, target, segment_ids, step):

time: 180 us -> 183 us (1.017)
  the two profiles are of different devices: /device:TPU:6 before, /device:TPU:14 now
where the time goes in v6:
time: 183 us; the launch traced here: 182 us
  starting transfers between devices  106 us (58%)
  waiting for transfers between devices  54.7 us (30%)
  loops' own time  5.65 us (3%)
  Pallas kernels  4.23 us (2%)
  matrix products  4.19 us (2%)
  other arithmetic  2.98 us (2%)
  local copies, waits for them, and re-layouts  2.55 us (1%)
    ppermute x16, starting transfers between devices, swap_z(): lax.ppermute(x, 'tensor', [(i, (i + step(i)) % size) for i in range(size)])  66.7 us
    ppermute x16, waiting for transfers between devices, swap_z(): lax.ppermute(x, 'tensor', [(i, (i + step(i)) % size) for i in range(size)])  30.7 us
    ppermute x3, starting transfers between devices, pass_replica(): lax.ppermute(x, 'replica', [(i, (i + by) % size) for i in range(size)])  26.9 us
    ppermute x3, waiting for transfers between devices, pass_replica(): lax.ppermute(x, 'replica', [(i, (i + by) % size) for i in range(size)])  18.4 us
    all_to_all x2, starting transfers between devices, exchange_x(): return lax.all_to_all(x, 'tensor', 0, 0, axis_index_groups=runs, tiled=True)  12.4 us
    all_to_all x2, waiting for transfers between devices, exchange_x(): return lax.all_to_all(x, 'tensor', 0, 0, axis_index_groups=runs, tiled=True)  5.68 us
    another operation x1, loops' own time, program(): lax.switch(step[0] % levels, branches, grad, heads, place, proj[0], momen...  5.65 us
    dot_general x8, matrix products, share(): jnp.dot(heads[j * chunk:(j + 1) * chunk], weight, preferred_element_type=...  4.19 us
  transfers between devices with their start and end apart: 21, of which 14 were waited for; matrix products, arithmetic and copies ran while one was open for 2% of the time, Pallas kernels for 1%

profile of v6, /device:TPU:14, one launch (start us, length us, event | category | flops | bytes accessed | tf_op | source)
XLA Modules:
  0.0 181.9 jit_solution(15766870992352922517)
XLA Ops:
  0.7 0.9 copy-done
  1.6 1.3 fusion
  3.0 17.3 %collective-permute-start.55 = (bf16[96,1024]{1,0:T(8,128)(2,1)S(1)}, bf16[96,1024]{1,0:T(8,128)(2,1)S(1)}, u32[]{:S(2)}, u32[]{:S(2)}) collective-permute-start(bf16[96,1024]{1,0:T(8,128)(2,1)S(1)} %get-tuple-element.131), channel_id=1, source_target_pairs={{0,28},{1,29},{2,30},{3,31},{4,8},{5,9},{6,10},{7,11},{8,4},{9,5},... | collective-permute-start | bytes 589832 | tf_op jit(solution)/shard_map/sum_z/ppermute | solution.py:25
  20.3 1.9 %collective-permute-start.59 = (bf16[96,1024]{1,0:T(8,128)(2,1)S(1)}, bf16[96,1024]{1,0:T(8,128)(2,1)S(1)}, u32[]{:S(2)}, u32[]{:S(2)}) collective-permute-start(bf16[96,1024]{1,0:T(8,128)(2,1)S(1)} %get-tuple-element.132), channel_id=1, source_target_pairs={{0,4},{1,5},{2,6},{3,7},{4,0},{5,1},{6,2},{7,3},{8,12},{9,13},{10,... | collective-permute-start | bytes 589832 | tf_op jit(solution)/shard_map/sum_z/ppermute | solution.py:25
  22.3 1.3 convolution_multiply_fusion.1
  23.6 0.3 convolution_multiply_fusion.2
  23.9 0.3 convolution_multiply_fusion.5
  24.1 4.5 %collective-permute-done.59 = bf16[96,1024]{1,0:T(8,128)(2,1)S(1)} collective-permute-done((bf16[96,1024]{1,0:T(8,128)(2,1)S(1)}, bf16[96,1024]{1,0:T(8,128)(2,1)S(1)}, u32[]{:S(2)}, u32[]{:S(2)}) %collective-permute-start.59) | collective-permute-done | bytes 196640 | tf_op jit(solution)/shard_map/sum_z/ppermute | solution.py:25
  28.6 0.3 add_convert_fusion.3
  28.9 2.2 %collective-permute-start.60 = (bf16[96,2048]{1,0:T(8,128)(2,1)S(1)}, bf16[96,2048]{1,0:T(8,128)(2,1)S(1)}, u32[]{:S(2)}, u32[]{:S(2)}) collective-permute-start(bf16[96,2048]{1,0:T(8,128)(2,1)S(1)} %add_convert_fusion.3), channel_id=1, source_target_pairs={{0,28},{1,29},{2,30},{3,31},{4,8},{5,9},{6,10},{7,11},{8,4},{9,5},... | collective-permute-start | bytes 1179656 | tf_op jit(solution)/shard_map/sum_z/ppermute | solution.py:25
  31.1 0.3 convolution_multiply_fusion.6
  31.3 0.0 collective-permute-done.55
  31.4 0.3 add_convert_fusion.6
  31.6 1.9 %collective-permute-start.56 = (bf16[96,2048]{1,0:T(8,128)(2,1)S(1)}, bf16[96,2048]{1,0:T(8,128)(2,1)S(1)}, u32[]{:S(2)}, u32[]{:S(2)}) collective-permute-start(bf16[96,2048]{1,0:T(8,128)(2,1)S(1)} %add_convert_fusion.6), channel_id=1, source_target_pairs={{0,4},{1,5},{2,6},{3,7},{4,0},{5,1},{6,2},{7,3},{8,12},{9,13},{10,... | collective-permute-start | bytes 1179656 | tf_op jit(solution)/shard_map/sum_z/ppermute | solution.py:25
  33.6 8.1 %collective-permute-done.60 = bf16[96,2048]{1,0:T(8,128)(2,1)S(1)} collective-permute-done((bf16[96,2048]{1,0:T(8,128)(2,1)S(1)}, bf16[96,2048]{1,0:T(8,128)(2,1)S(1)}, u32[]{:S(2)}, u32[]{:S(2)}) %collective-permute-start.60) | collective-permute-done | bytes 393248 | tf_op jit(solution)/shard_map/sum_z/ppermute | solution.py:25
  41.6 0.1 add_convert_fusion.2
  41.7 1.9 %collective-permute-start.61 = (bf16[96,2048]{1,0:T(8,128)(2,1)S(1)}, bf16[96,2048]{1,0:T(8,128)(2,1)S(1)}, u32[]{:S(2)}, u32[]{:S(2)}) collective-permute-start(bf16[96,2048]{1,0:T(8,128)(2,1)S(1)} %add_convert_fusion.2), channel_id=1, source_target_pairs={{0,4},{1,5},{2,6},{3,7},{4,0},{5,1},{6,2},{7,3},{8,12},{9,13},{10,... | collective-permute-start | bytes 1179656 | tf_op jit(solution)/shard_map/sum_z/ppermute | solution.py:25
  43.7 0.0 collective-permute-done.56
  43.7 0.1 add_convert_fusion.5
  43.7 5.0 %collective-permute-start.57 = (bf16[96,2048]{1,0:T(8,128)(2,1)S(1)}, bf16[96,2048]{1,0:T(8,128)(2,1)S(1)}, u32[]{:S(2)}, u32[]{:S(2)}) collective-permute-start(bf16[96,2048]{1,0:T(8,128)(2,1)S(1)} %add_convert_fusion.5), channel_id=1, source_target_pairs={{0,28},{1,29},{2,30},{3,31},{4,8},{5,9},{6,10},{7,11},{8,4},{9,5},... | collective-permute-start | bytes 1179656 | tf_op jit(solution)/shard_map/sum_z/ppermute | solution.py:25
  48.8 3.6 %collective-permute-done.61 = bf16[96,2048]{1,0:T(8,128)(2,1)S(1)} collective-permute-done((bf16[96,2048]{1,0:T(8,128)(2,1)S(1)}, bf16[96,2048]{1,0:T(8,128)(2,1)S(1)}, u32[]{:S(2)}, u32[]{:S(2)}) %collective-permute-start.61) | collective-permute-done | bytes 393248 | tf_op jit(solution)/shard_map/sum_z/ppermute | solution.py:25
  52.4 0.1 add_convert_fusion.1
  52.4 0.0 copy-start.4
  52.5 0.0 copy-start.2
  52.5 4.0 %collective-permute-start.62 = (bf16[96,2048]{1,0:T(8,128)(2,1)S(1)}, bf16[96,2048]{1,0:T(8,128)(2,1)S(1)}, u32[]{:S(2)}, u32[]{:S(2)}) collective-permute-start(bf16[96,2048]{1,0:T(8,128)(2,1)S(1)} %add_convert_fusion.1), channel_id=1, source_target_pairs={{0,28},{1,29},{2,30},{3,31},{4,8},{5,9},{6,10},{7,11},{8,4},{9,5},... | collective-permute-start | bytes 1179656 | tf_op jit(solution)/shard_map/sum_z/ppermute | solution.py:25
  56.4 0.1 add_convert_fusion.4
  56.5 2.5 %collective-permute-start.58 = (bf16[96,2048]{1,0:T(8,128)(2,1)S(1)}, bf16[96,2048]{1,0:T(8,128)(2,1)S(1)}, u32[]{:S(2)}, u32[]{:S(2)}) collective-permute-start(bf16[96,2048]{1,0:T(8,128)(2,1)S(1)} %add_convert_fusion.4), channel_id=1, source_target_pairs={{0,4},{1,5},{2,6},{3,7},{4,0},{5,1},{6,2},{7,3},{8,12},{9,13},{10,... | collective-permute-start | bytes 1179656 | tf_op jit(solution)/shard_map/sum_z/ppermute | solution.py:25
  59.1 0.3 convolution_multiply_fusion.7
  59.3 4.7 %collective-permute-done.62 = bf16[96,2048]{1,0:T(8,128)(2,1)S(1)} collective-permute-done((bf16[96,2048]{1,0:T(8,128)(2,1)S(1)}, bf16[96,2048]{1,0:T(8,128)(2,1)S(1)}, u32[]{:S(2)}, u32[]{:S(2)}) %collective-permute-start.62) | collective-permute-done | bytes 393248 | tf_op jit(solution)/shard_map/sum_z/ppermute | solution.py:25
  64.0 3.2 %collective-permute-done.58 = bf16[96,2048]{1,0:T(8,128)(2,1)S(1)} collective-permute-done((bf16[96,2048]{1,0:T(8,128)(2,1)S(1)}, bf16[96,2048]{1,0:T(8,128)(2,1)S(1)}, u32[]{:S(2)}, u32[]{:S(2)}) %collective-permute-start.58) | collective-permute-done | bytes 393248 | tf_op jit(solution)/shard_map/sum_z/ppermute | solution.py:25
  67.3 0.9 add_convert_fusion
  68.1 6.6 %all-to-all-start.5 = ((bf16[4,24,2048]{2,1,0:T(8,128)(2,1)}), bf16[4,24,2048]{2,1,0:T(8,128)(2,1)S(1)}, u32[]{:S(2)}, u32[]{:S(2)}) async-start(bf16[4,24,2048]{2,1,0:T(8,128)(2,1)} %bitcast.31), calls=%async_computation.5 | async-start | bytes 786432 | tf_op jit(solution)/shard_map/sum_x/all_to_all | solution.py:31
  75.4 0.1 dynamic-slice_bitcast_fusion
  75.5 0.2 convert_reduce_fusion.1
  75.7 5.7 %all-to-all-done.5 = bf16[4,24,2048]{2,1,0:T(8,128)(2,1)S(1)} async-done(((bf16[4,24,2048]{2,1,0:T(8,128)(2,1)}), bf16[4,24,2048]{2,1,0:T(8,128)(2,1)S(1)}, u32[]{:S(2)}, u32[]{:S(2)}) %all-to-all-start.5) | async-done | bytes 393248 | tf_op jit(solution)/shard_map/sum_x/all_to_all | solution.py:31
  81.4 1.6 fusion.2
  83.0 98.2 %conditional.1 = (bf16[128,2048]{1,0:T(8,128)(2,1)}, bf16[128,2048]{1,0:T(8,128)(2,1)}, bf16[1,768,128]{2,1,0:T(8,128)(2,1)S(1)}) conditional(s32[]{:T(128)} %clamp.3, (bf16[24,2048]{1,0:T(8,128)(2,1)S(1)}, bf16[128,2048]{1,0:T(8,128)(2,1)S(1)}, bf16[32,24,128]{2,1,0:T(8,128)(2,1)S(1)}, ...), branch_computations={%region_2.3_spmd, %region_3.4_spmd, %region_4.5_spmd, %region_5.6_... | conditional | flops 805306368 | bytes 24871408 | solution.py:259
  88.5 0.8 tile.14
  89.3 5.8 %all-to-all-start.4 = ((bf16[4,24,2048]{2,1,0:T(8,128)(2,1)}), bf16[4,24,2048]{2,1,0:T(8,128)(2,1)S(1)}, u32[]{:S(2)}, u32[]{:S(2)}) async-start(bf16[4,24,2048]{2,1,0:T(8,128)(2,1)} %tile.14), calls=%async_computation.4 | async-start | bytes 786432 | tf_op jit(solution)/shard_map/cond/branch_4_fun/gather_x/all_to_all | solution.py:31
  95.1 8.2 %collective-permute-start.46 = (bf16[128,2048]{1,0:T(8,128)(2,1)S(1)}, bf16[128,2048]{1,0:T(8,128)(2,1)S(1)}, u32[]{:S(2)}, u32[]{:S(2)}) collective-permute-start(bf16[128,2048]{1,0:T(8,128)(2,1)S(1)} %get-tuple-element.109.refs_0_.refs_9_), channel_id=1, source_target_pairs={{0,512},{32,544},{64,576},{96,608},{128,640},{160,672},{192,704},{... | collective-permute-start | bytes 1572872 | tf_op jit(solution)/shard_map/cond/branch_4_fun/early_partner/ppermute | solution.py:36
  103.3 2.1 %collective-permute-start.45 = (bf16[96,2048]{1,0:T(8,128)(2,1)S(1)}, bf16[96,2048]{1,0:T(8,128)(2,1)S(1)}, u32[]{:S(2)}, u32[]{:S(2)}) collective-permute-start(bf16[96,2048]{1,0:T(8,128)(2,1)S(1)} %bitcast.82), channel_id=1, source_target_pairs={{0,28},{1,29},{2,30},{3,31},{4,8},{5,9},{6,10},{7,11},{8,4},{9,5},... | collective-permute-start | bytes 1179656 | tf_op jit(solution)/shard_map/cond/branch_4_fun/gather_z/ppermute | solution.py:25
  105.3 1.9 %collective-permute-start.44 = (bf16[96,2048]{1,0:T(8,128)(2,1)S(1)}, bf16[96,2048]{1,0:T(8,128)(2,1)S(1)}, u32[]{:S(2)}, u32[]{:S(2)}) collective-permute-start(bf16[96,2048]{1,0:T(8,128)(2,1)S(1)} %bitcast.83), channel_id=1, source_target_pairs={{0,4},{1,5},{2,6},{3,7},{4,0},{5,1},{6,2},{7,3},{8,12},{9,13},{10,... | collective-permute-start | bytes 1179656 | tf_op jit(solution)/shard_map/cond/branch_4_fun/gather_z/ppermute | solution.py:25
  107.2 6.5 %collective-permute-done.46.refs_1_ = bf16[128,2048]{1,0:T(8,128)(2,1)S(1)} collective-permute-done((bf16[128,2048]{1,0:T(8,128)(2,1)S(1)}, bf16[128,2048]{1,0:T(8,128)(2,1)S(1)}, u32[]{:S(2)}, u32[]{:S(2)}) %collective-permute-start.46) | collective-permute-done | bytes 524320 | tf_op jit(solution)/shard_map/cond/branch_4_fun/early_partner/ppermute | solution.py:36
  113.8 0.4 collective-permute-done.45.refs_4_.refs_7_
  114.1 0.9 collective-permute-done.44.refs_1_
  115.0 5.0 %collective-permute-start.47 = (bf16[96,2048]{1,0:T(8,128)(2,1)S(1)}, bf16[96,2048]{1,0:T(8,128)(2,1)S(1)}, u32[]{:S(2)}, u32[]{:S(2)}) collective-permute-start(bf16[96,2048]{1,0:T(8,128)(2,1)S(1)} %collective-permute-done.44.refs_1_), channel_id=1, source_target_pairs={{0,28},{1,29},{2,30},{3,31},{4,8},{5,9},{6,10},{7,11},{8,4},{9,5},... | collective-permute-start | bytes 1179656 | tf_op jit(solution)/shard_map/cond/branch_4_fun/gather_z/ppermute | solution.py:25
  120.0 4.4 %collective-permute-start.49 = (bf16[96,2048]{1,0:T(8,128)(2,1)S(1)}, bf16[96,2048]{1,0:T(8,128)(2,1)S(1)}, u32[]{:S(2)}, u32[]{:S(2)}) collective-permute-start(bf16[96,2048]{1,0:T(8,128)(2,1)S(1)} %collective-permute-done.45.refs_4_.refs_7_), channel_id=1, source_target_pairs={{0,4},{1,5},{2,6},{3,7},{4,0},{5,1},{6,2},{7,3},{8,12},{9,13},{10,... | collective-permute-start | bytes 1179656 | tf_op jit(solution)/shard_map/cond/branch_4_fun/gather_z/ppermute | solution.py:25
  124.4 1.4 collective-permute-done.47.refs_3_.refs_6_
  125.9 4.3 %collective-permute-start.48 = (bf16[96,2048]{1,0:T(8,128)(2,1)S(1)}, bf16[96,2048]{1,0:T(8,128)(2,1)S(1)}, u32[]{:S(2)}, u32[]{:S(2)}) collective-permute-start(bf16[96,2048]{1,0:T(8,128)(2,1)S(1)} %collective-permute-done.47.refs_3_.refs_6_), channel_id=1, source_target_pairs={{0,4},{1,5},{2,6},{3,7},{4,0},{5,1},{6,2},{7,3},{8,12},{9,13},{10,... | collective-permute-start | bytes 1179656 | tf_op jit(solution)/shard_map/cond/branch_4_fun/gather_z/ppermute | solution.py:25
  130.1 1.5 collective-permute-done.49.refs_2_
  131.7 3.7 %collective-permute-start.51 = (bf16[96,2048]{1,0:T(8,128)(2,1)S(1)}, bf16[96,2048]{1,0:T(8,128)(2,1)S(1)}, u32[]{:S(2)}, u32[]{:S(2)}) collective-permute-start(bf16[96,2048]{1,0:T(8,128)(2,1)S(1)} %collective-permute-done.49.refs_2_), channel_id=1, source_target_pairs={{0,28},{1,29},{2,30},{3,31},{4,8},{5,9},{6,10},{7,11},{8,4},{9,5},... | collective-permute-start | bytes 1179656 | tf_op jit(solution)/shard_map/cond/branch_4_fun/gather_z/ppermute | solution.py:25
  135.4 0.6 near.9.refs_3_
  136.0 4.5 %collective-permute-start.50 = (bf16[96,1024]{1,0:T(8,128)(2,1)S(1)}, bf16[96,1024]{1,0:T(8,128)(2,1)S(1)}, u32[]{:S(2)}, u32[]{:S(2)}) collective-permute-start(bf16[96,1024]{1,0:T(8,128)(2,1)S(1)} %slice.64), channel_id=1, source_target_pairs={{0,28},{1,29},{2,30},{3,31},{4,8},{5,9},{6,10},{7,11},{8,4},{9,5},... | collective-permute-start | bytes 589832 | tf_op jit(solution)/shard_map/cond/branch_4_fun/gather_z/ppermute | solution.py:25
  140.5 2.4 %collective-permute-done.51.refs_2_.refs_5_ = bf16[96,2048]{1,0:T(8,128)(2,1)S(1)} collective-permute-done((bf16[96,2048]{1,0:T(8,128)(2,1)S(1)}, bf16[96,2048]{1,0:T(8,128)(2,1)S(1)}, u32[]{:S(2)}, u32[]{:S(2)}) %collective-permute-start.51) | collective-permute-done | bytes 393248 | tf_op jit(solution)/shard_map/cond/branch_4_fun/gather_z/ppermute | solution.py:25
  142.9 4.0 %collective-permute-start.52 = (bf16[96,1024]{1,0:T(8,128)(2,1)S(1)}, bf16[96,1024]{1,0:T(8,128)(2,1)S(1)}, u32[]{:S(2)}, u32[]{:S(2)}) collective-permute-start(bf16[96,1024]{1,0:T(8,128)(2,1)S(1)} %slice.65), channel_id=1, source_target_pairs={{0,4},{1,5},{2,6},{3,7},{4,0},{5,1},{6,2},{7,3},{8,12},{9,13},{10,... | collective-permute-start | bytes 589832 | tf_op jit(solution)/shard_map/cond/branch_4_fun/gather_z/ppermute | solution.py:25
  147.0 0.3 moment.18.refs_2_
  147.3 16.8 %collective-permute-start.53 = (bf16[128,1024]{1,0:T(8,128)(2,1)S(1)}, bf16[128,1024]{1,0:T(8,128)(2,1)S(1)}, u32[]{:S(2)}, u32[]{:S(2)}) collective-permute-start(bf16[128,1024]{1,0:T(8,128)(2,1)S(1)} %moment.18.refs_2_), channel_id=1, source_target_pairs={{0,512},{32,544},{64,576},{96,608},{128,640},{160,672},{192,704},{... | collective-permute-start | bytes 786440 | tf_op jit(solution)/shard_map/cond/branch_4_fun/partner/ppermute | solution.py:36
  164.1 0.3 moment.19.refs_3_
  164.5 1.9 %collective-permute-start.54 = (bf16[128,1024]{1,0:T(8,128)(2,1)S(1)}, bf16[128,1024]{1,0:T(8,128)(2,1)S(1)}, u32[]{:S(2)}, u32[]{:S(2)}) collective-permute-start(bf16[128,1024]{1,0:T(8,128)(2,1)S(1)} %moment.19.refs_3_), channel_id=1, source_target_pairs={{0,512},{32,544},{64,576},{96,608},{128,640},{160,672},{192,704},{... | collective-permute-start | bytes 786440 | tf_op jit(solution)/shard_map/cond/branch_4_fun/partner/ppermute | solution.py:36
  166.4 1.5 back.9
  167.8 9.0 %collective-permute-done.53.refs_4_ = bf16[128,1024]{1,0:T(8,128)(2,1)S(1)} collective-permute-done((bf16[128,1024]{1,0:T(8,128)(2,1)S(1)}, bf16[128,1024]{1,0:T(8,128)(2,1)S(1)}, u32[]{:S(2)}, u32[]{:S(2)}) %collective-permute-start.53) | collective-permute-done | bytes 262176 | tf_op jit(solution)/shard_map/cond/branch_4_fun/partner/ppermute | solution.py:36
  176.9 2.8 %collective-permute-done.54.refs_5_ = bf16[128,1024]{1,0:T(8,128)(2,1)S(1)} collective-permute-done((bf16[128,1024]{1,0:T(8,128)(2,1)S(1)}, bf16[128,1024]{1,0:T(8,128)(2,1)S(1)}, u32[]{:S(2)}, u32[]{:S(2)}) %collective-permute-start.54) | collective-permute-done | bytes 262176 | tf_op jit(solution)/shard_map/cond/branch_4_fun/partner/ppermute | solution.py:36
  179.7 1.5 mix.9
  181.2 0.7 copy-done.3
  (19 shorter events, 0.2 us)
Async XLA Ops:
  0.6 0.9 copy-start
  1.6 22.0 %copy-start.1 = (bf16[1,128,2048]{2,1,0:T(8,128)(2,1)S(1)}, bf16[1,128,2048]{2,1,0:T(8,128)(2,1)}, u32[]{:S(2)}) copy-start(bf16[1,128,2048]{2,1,0:T(8,128)(2,1)} %param.12) | copy-start | bytes 1572868
  3.0 28.3 %collective-permute-start.55 = (bf16[96,1024]{1,0:T(8,128)(2,1)S(1)}, bf16[96,1024]{1,0:T(8,128)(2,1)S(1)}, u32[]{:S(2)}, u32[]{:S(2)}) collective-permute-start(bf16[96,1024]{1,0:T(8,128)(2,1)S(1)} %get-tuple-element.131), channel_id=1, source_target_pairs={{0,28},{1,29},{2,30},{3,31},{4,8},{5,9},{6,10},{7,11},{8,4},{9,5},... | collective-permute-start | bytes 589832 | tf_op jit(solution)/shard_map/sum_z/ppermute | solution.py:25
  20.3 8.3 %collective-permute-start.59 = (bf16[96,1024]{1,0:T(8,128)(2,1)S(1)}, bf16[96,1024]{1,0:T(8,128)(2,1)S(1)}, u32[]{:S(2)}, u32[]{:S(2)}) collective-permute-start(bf16[96,1024]{1,0:T(8,128)(2,1)S(1)} %get-tuple-element.132), channel_id=1, source_target_pairs={{0,4},{1,5},{2,6},{3,7},{4,0},{5,1},{6,2},{7,3},{8,12},{9,13},{10,... | collective-permute-start | bytes 589832 | tf_op jit(solution)/shard_map/sum_z/ppermute | solution.py:25
  28.9 12.8 %collective-permute-start.60 = (bf16[96,2048]{1,0:T(8,128)(2,1)S(1)}, bf16[96,2048]{1,0:T(8,128)(2,1)S(1)}, u32[]{:S(2)}, u32[]{:S(2)}) collective-permute-start(bf16[96,2048]{1,0:T(8,128)(2,1)S(1)} %add_convert_fusion.3), channel_id=1, source_target_pairs={{0,28},{1,29},{2,30},{3,31},{4,8},{5,9},{6,10},{7,11},{8,4},{9,5},... | collective-permute-start | bytes 1179656 | tf_op jit(solution)/shard_map/sum_z/ppermute | solution.py:25
  31.6 12.0 %collective-permute-start.56 = (bf16[96,2048]{1,0:T(8,128)(2,1)S(1)}, bf16[96,2048]{1,0:T(8,128)(2,1)S(1)}, u32[]{:S(2)}, u32[]{:S(2)}) collective-permute-start(bf16[96,2048]{1,0:T(8,128)(2,1)S(1)} %add_convert_fusion.6), channel_id=1, source_target_pairs={{0,4},{1,5},{2,6},{3,7},{4,0},{5,1},{6,2},{7,3},{8,12},{9,13},{10,... | collective-permute-start | bytes 1179656 | tf_op jit(solution)/shard_map/sum_z/ppermute | solution.py:25
  41.7 10.6 %collective-permute-start.61 = (bf16[96,2048]{1,0:T(8,128)(2,1)S(1)}, bf16[96,2048]{1,0:T(8,128)(2,1)S(1)}, u32[]{:S(2)}, u32[]{:S(2)}) collective-permute-start(bf16[96,2048]{1,0:T(8,128)(2,1)S(1)} %add_convert_fusion.2), channel_id=1, source_target_pairs={{0,4},{1,5},{2,6},{3,7},{4,0},{5,1},{6,2},{7,3},{8,12},{9,13},{10,... | collective-permute-start | bytes 1179656 | tf_op jit(solution)/shard_map/sum_z/ppermute | solution.py:25
  43.7 12.7 %collective-permute-start.57 = (bf16[96,2048]{1,0:T(8,128)(2,1)S(1)}, bf16[96,2048]{1,0:T(8,128)(2,1)S(1)}, u32[]{:S(2)}, u32[]{:S(2)}) collective-permute-start(bf16[96,2048]{1,0:T(8,128)(2,1)S(1)} %add_convert_fusion.5), channel_id=1, source_target_pairs={{0,28},{1,29},{2,30},{3,31},{4,8},{5,9},{6,10},{7,11},{8,4},{9,5},... | collective-permute-start | bytes 1179656 | tf_op jit(solution)/shard_map/sum_z/ppermute | solution.py:25
  52.4 22.9 %copy-start.4 = (s32[1,768]{1,0:T(1,128)S(1)}, s32[1,768]{1,0:T(1,128)}, u32[]{:S(2)}) copy-start(s32[1,768]{1,0:T(1,128)} %param.15) | copy-start | bytes 9220
  52.5 30.5 %copy-start.2 = (bf16[1,128,2048]{2,1,0:T(8,128)(2,1)S(1)}, bf16[1,128,2048]{2,1,0:T(8,128)(2,1)}, u32[]{:S(2)}) copy-start(bf16[1,128,2048]{2,1,0:T(8,128)(2,1)} %param.13) | copy-start | bytes 1572868
  52.5 11.6 %collective-permute-start.62 = (bf16[96,2048]{1,0:T(8,128)(2,1)S(1)}, bf16[96,2048]{1,0:T(8,128)(2,1)S(1)}, u32[]{:S(2)}, u32[]{:S(2)}) collective-permute-start(bf16[96,2048]{1,0:T(8,128)(2,1)S(1)} %add_convert_fusion.1), channel_id=1, source_target_pairs={{0,28},{1,29},{2,30},{3,31},{4,8},{5,9},{6,10},{7,11},{8,4},{9,5},... | collective-permute-start | bytes 1179656 | tf_op jit(solution)/shard_map/sum_z/ppermute | solution.py:25
  56.5 10.7 %collective-permute-start.58 = (bf16[96,2048]{1,0:T(8,128)(2,1)S(1)}, bf16[96,2048]{1,0:T(8,128)(2,1)S(1)}, u32[]{:S(2)}, u32[]{:S(2)}) collective-permute-start(bf16[96,2048]{1,0:T(8,128)(2,1)S(1)} %add_convert_fusion.4), channel_id=1, source_target_pairs={{0,4},{1,5},{2,6},{3,7},{4,0},{5,1},{6,2},{7,3},{8,12},{9,13},{10,... | collective-permute-start | bytes 1179656 | tf_op jit(solution)/shard_map/sum_z/ppermute | solution.py:25
  68.1 13.3 %all-to-all-start.5 = ((bf16[4,24,2048]{2,1,0:T(8,128)(2,1)}), bf16[4,24,2048]{2,1,0:T(8,128)(2,1)S(1)}, u32[]{:S(2)}, u32[]{:S(2)}) async-start(bf16[4,24,2048]{2,1,0:T(8,128)(2,1)} %bitcast.31), calls=%async_computation.5 | async-start | bytes 786432 | tf_op jit(solution)/shard_map/sum_x/all_to_all | solution.py:31
  89.3 14.0 %all-to-all-start.4 = ((bf16[4,24,2048]{2,1,0:T(8,128)(2,1)}), bf16[4,24,2048]{2,1,0:T(8,128)(2,1)S(1)}, u32[]{:S(2)}, u32[]{:S(2)}) async-start(bf16[4,24,2048]{2,1,0:T(8,128)(2,1)} %tile.14), calls=%async_computation.4 | async-start | bytes 786432 | tf_op jit(solution)/shard_map/cond/branch_4_fun/gather_x/all_to_all | solution.py:31
  95.1 18.7 %collective-permute-start.46 = (bf16[128,2048]{1,0:T(8,128)(2,1)S(1)}, bf16[128,2048]{1,0:T(8,128)(2,1)S(1)}, u32[]{:S(2)}, u32[]{:S(2)}) collective-permute-start(bf16[128,2048]{1,0:T(8,128)(2,1)S(1)} %get-tuple-element.109.refs_0_.refs_9_), channel_id=1, source_target_pairs={{0,512},{32,544},{64,576},{96,608},{128,640},{160,672},{192,704},{... | collective-permute-start | bytes 1572872 | tf_op jit(solution)/shard_map/cond/branch_4_fun/early_partner/ppermute | solution.py:36
  103.3 10.9 %collective-permute-start.45 = (bf16[96,2048]{1,0:T(8,128)(2,1)S(1)}, bf16[96,2048]{1,0:T(8,128)(2,1)S(1)}, u32[]{:S(2)}, u32[]{:S(2)}) collective-permute-start(bf16[96,2048]{1,0:T(8,128)(2,1)S(1)} %bitcast.82), channel_id=1, source_target_pairs={{0,28},{1,29},{2,30},{3,31},{4,8},{5,9},{6,10},{7,11},{8,4},{9,5},... | collective-permute-start | bytes 1179656 | tf_op jit(solution)/shard_map/cond/branch_4_fun/gather_z/ppermute | solution.py:25
  105.3 9.7 %collective-permute-start.44 = (bf16[96,2048]{1,0:T(8,128)(2,1)S(1)}, bf16[96,2048]{1,0:T(8,128)(2,1)S(1)}, u32[]{:S(2)}, u32[]{:S(2)}) collective-permute-start(bf16[96,2048]{1,0:T(8,128)(2,1)S(1)} %bitcast.83), channel_id=1, source_target_pairs={{0,4},{1,5},{2,6},{3,7},{4,0},{5,1},{6,2},{7,3},{8,12},{9,13},{10,... | collective-permute-start | bytes 1179656 | tf_op jit(solution)/shard_map/cond/branch_4_fun/gather_z/ppermute | solution.py:25
  115.0 10.9 %collective-permute-start.47 = (bf16[96,2048]{1,0:T(8,128)(2,1)S(1)}, bf16[96,2048]{1,0:T(8,128)(2,1)S(1)}, u32[]{:S(2)}, u32[]{:S(2)}) collective-permute-start(bf16[96,2048]{1,0:T(8,128)(2,1)S(1)} %collective-permute-done.44.refs_1_), channel_id=1, source_target_pairs={{0,28},{1,29},{2,30},{3,31},{4,8},{5,9},{6,10},{7,11},{8,4},{9,5},... | collective-permute-start | bytes 1179656 | tf_op jit(solution)/shard_map/cond/branch_4_fun/gather_z/ppermute | solution.py:25
  120.0 11.7 %collective-permute-start.49 = (bf16[96,2048]{1,0:T(8,128)(2,1)S(1)}, bf16[96,2048]{1,0:T(8,128)(2,1)S(1)}, u32[]{:S(2)}, u32[]{:S(2)}) collective-permute-start(bf16[96,2048]{1,0:T(8,128)(2,1)S(1)} %collective-permute-done.45.refs_4_.refs_7_), channel_id=1, source_target_pairs={{0,4},{1,5},{2,6},{3,7},{4,0},{5,1},{6,2},{7,3},{8,12},{9,13},{10,... | collective-permute-start | bytes 1179656 | tf_op jit(solution)/shard_map/cond/branch_4_fun/gather_z/ppermute | solution.py:25
  125.9 10.2 %collective-permute-start.48 = (bf16[96,2048]{1,0:T(8,128)(2,1)S(1)}, bf16[96,2048]{1,0:T(8,128)(2,1)S(1)}, u32[]{:S(2)}, u32[]{:S(2)}) collective-permute-start(bf16[96,2048]{1,0:T(8,128)(2,1)S(1)} %collective-permute-done.47.refs_3_.refs_6_), channel_id=1, source_target_pairs={{0,4},{1,5},{2,6},{3,7},{4,0},{5,1},{6,2},{7,3},{8,12},{9,13},{10,... | collective-permute-start | bytes 1179656 | tf_op jit(solution)/shard_map/cond/branch_4_fun/gather_z/ppermute | solution.py:25
  131.7 11.3 %collective-permute-start.51 = (bf16[96,2048]{1,0:T(8,128)(2,1)S(1)}, bf16[96,2048]{1,0:T(8,128)(2,1)S(1)}, u32[]{:S(2)}, u32[]{:S(2)}) collective-permute-start(bf16[96,2048]{1,0:T(8,128)(2,1)S(1)} %collective-permute-done.49.refs_2_), channel_id=1, source_target_pairs={{0,28},{1,29},{2,30},{3,31},{4,8},{5,9},{6,10},{7,11},{8,4},{9,5},... | collective-permute-start | bytes 1179656 | tf_op jit(solution)/shard_map/cond/branch_4_fun/gather_z/ppermute | solution.py:25
  136.0 11.0 %collective-permute-start.50 = (bf16[96,1024]{1,0:T(8,128)(2,1)S(1)}, bf16[96,1024]{1,0:T(8,128)(2,1)S(1)}, u32[]{:S(2)}, u32[]{:S(2)}) collective-permute-start(bf16[96,1024]{1,0:T(8,128)(2,1)S(1)} %slice.64), channel_id=1, source_target_pairs={{0,28},{1,29},{2,30},{3,31},{4,8},{5,9},{6,10},{7,11},{8,4},{9,5},... | collective-permute-start | bytes 589832 | tf_op jit(solution)/shard_map/cond/branch_4_fun/gather_z/ppermute | solution.py:25
  142.9 21.2 %collective-permute-start.52 = (bf16[96,1024]{1,0:T(8,128)(2,1)S(1)}, bf16[96,1024]{1,0:T(8,128)(2,1)S(1)}, u32[]{:S(2)}, u32[]{:S(2)}) collective-permute-start(bf16[96,1024]{1,0:T(8,128)(2,1)S(1)} %slice.65), channel_id=1, source_target_pairs={{0,4},{1,5},{2,6},{3,7},{4,0},{5,1},{6,2},{7,3},{8,12},{9,13},{10,... | collective-permute-start | bytes 589832 | tf_op jit(solution)/shard_map/cond/branch_4_fun/gather_z/ppermute | solution.py:25
  147.3 29.5 %collective-permute-start.53 = (bf16[128,1024]{1,0:T(8,128)(2,1)S(1)}, bf16[128,1024]{1,0:T(8,128)(2,1)S(1)}, u32[]{:S(2)}, u32[]{:S(2)}) collective-permute-start(bf16[128,1024]{1,0:T(8,128)(2,1)S(1)} %moment.18.refs_2_), channel_id=1, source_target_pairs={{0,512},{32,544},{64,576},{96,608},{128,640},{160,672},{192,704},{... | collective-permute-start | bytes 786440 | tf_op jit(solution)/shard_map/cond/branch_4_fun/partner/ppermute | solution.py:36
  164.5 15.2 %collective-permute-start.54 = (bf16[128,1024]{1,0:T(8,128)(2,1)S(1)}, bf16[128,1024]{1,0:T(8,128)(2,1)S(1)}, u32[]{:S(2)}, u32[]{:S(2)}) collective-permute-start(bf16[128,1024]{1,0:T(8,128)(2,1)S(1)} %moment.19.refs_3_), channel_id=1, source_target_pairs={{0,512},{32,544},{64,576},{96,608},{128,640},{160,672},{192,704},{... | collective-permute-start | bytes 786440 | tf_op jit(solution)/shard_map/cond/branch_4_fun/partner/ppermute | solution.py:36
  181.2 0.7 copy-start.3

commit v7 on v6

--- a/solution.py
+++ b/solution.py
@@ -11,6 +11,7 @@
 BETA_MOM = 0.9
 STEP_RATE = 0.1
 NX = 4
+ROW = 4
 SMALL = pltpu.CompilerParams(vmem_limit_bytes=16 << 20)
 SCALARS = pl.BlockSpec(memory_space=pltpu.SMEM)
 
@@ -215,8 +216,10 @@
         held = [block] + [None] * (nz - 1)
         even = odd = block
         for m in range(1, nz // 2):
-            if m == 2:
-                even, odd, partner_w = lax.optimization_barrier((even, odd, partner_w))
+            if hop >= ROW and m == 2:
+                odd, partner_w = lax.optimization_barrier((odd, partner_w))
+            if hop < ROW and m == 3:
+                even, partner_w = lax.optimization_barrier((even, partner_w))
             even, odd = swap_z(odd, 0), swap_z(even, 1)
             held[m], held[-m] = even, odd
         near = near_of(heads, held)

time: 183 us -> 166 us (0.907)
  the two profiles are of different devices: /device:TPU:14 before, /device:TPU:66 now
where the time goes in v7:
time: 166 us
  waiting for transfers between devices  70.1 us (42%)
  starting transfers between devices  69.3 us (42%)
  blocking collectives  11.3 us (7%)
  Pallas kernels  4.24 us (3%)
  matrix products  4.19 us (3%)
  other arithmetic  2.98 us (2%)
  local copies, waits for them, and re-layouts  1.8 us (1%)
    ppermute x16, starting transfers between devices, swap_z(): lax.ppermute(x, 'tensor', [(i, (i + step(i)) % size) for i in range(size)])  56.8 us
    ppermute x16, waiting for transfers between devices, swap_z(): lax.ppermute(x, 'tensor', [(i, (i + step(i)) % size) for i in range(size)])  48.4 us
    ppermute x3, waiting for transfers between devices, pass_replica(): lax.ppermute(x, 'replica', [(i, (i + by) % size) for i in range(size)])  15.3 us
    all_to_all x1, blocking collectives, exchange_x(): return lax.all_to_all(x, 'tensor', 0, 0, axis_index_groups=runs, tiled=True)  11.3 us
    ppermute x3, starting transfers between devices, pass_replica(): lax.ppermute(x, 'replica', [(i, (i + by) % size) for i in range(size)])  7.38 us
    all_to_all x1, waiting for transfers between devices, exchange_x(): return lax.all_to_all(x, 'tensor', 0, 0, axis_index_groups=runs, tiled=True)  6.43 us
    all_to_all x1, starting transfers between devices, exchange_x(): return lax.all_to_all(x, 'tensor', 0, 0, axis_index_groups=runs, tiled=True)  5.14 us
    dot_general x8, matrix products, share(): jnp.dot(heads[j * chunk:(j + 1) * chunk], weight, preferred_element_type=...  4.19 us
  transfers between devices with their start and end apart: 20, of which 15 were waited for; matrix products, arithmetic and copies ran while one was open for 2% of the time, Pallas kernels for 2%

profile of v7, /device:TPU:66, one launch (start us, length us, event | category | flops | bytes accessed | tf_op | source)
XLA Modules:
  0.0 165.6 jit_solution(12141531219167776190)
XLA Ops:
  0.7 0.9 copy-done
  1.6 1.4 fusion
  3.0 17.3 %collective-permute-start.55 = (bf16[96,1024]{1,0:T(8,128)(2,1)S(1)}, bf16[96,1024]{1,0:T(8,128)(2,1)S(1)}, u32[]{:S(2)}, u32[]{:S(2)}) collective-permute-start(bf16[96,1024]{1,0:T(8,128)(2,1)S(1)} %get-tuple-element.126), channel_id=1, source_target_pairs={{0,28},{1,29},{2,30},{3,31},{4,8},{5,9},{6,10},{7,11},{8,4},{9,5},... | collective-permute-start | bytes 589832 | tf_op jit(solution)/shard_map/sum_z/ppermute | solution.py:26
  20.3 1.9 %collective-permute-start.59 = (bf16[96,1024]{1,0:T(8,128)(2,1)S(1)}, bf16[96,1024]{1,0:T(8,128)(2,1)S(1)}, u32[]{:S(2)}, u32[]{:S(2)}) collective-permute-start(bf16[96,1024]{1,0:T(8,128)(2,1)S(1)} %get-tuple-element.127), channel_id=1, source_target_pairs={{0,4},{1,5},{2,6},{3,7},{4,0},{5,1},{6,2},{7,3},{8,12},{9,13},{10,... | collective-permute-start | bytes 589832 | tf_op jit(solution)/shard_map/sum_z/ppermute | solution.py:26
  22.3 1.3 convolution_multiply_fusion.1
  23.6 0.3 convolution_multiply_fusion.2
  23.9 0.3 convolution_multiply_fusion.5
  24.1 4.5 %collective-permute-done.59 = bf16[96,1024]{1,0:T(8,128)(2,1)S(1)} collective-permute-done((bf16[96,1024]{1,0:T(8,128)(2,1)S(1)}, bf16[96,1024]{1,0:T(8,128)(2,1)S(1)}, u32[]{:S(2)}, u32[]{:S(2)}) %collective-permute-start.59) | collective-permute-done | bytes 196640 | tf_op jit(solution)/shard_map/sum_z/ppermute | solution.py:26
  28.6 0.3 add_convert_fusion.3
  28.9 2.2 %collective-permute-start.60 = (bf16[96,2048]{1,0:T(8,128)(2,1)S(1)}, bf16[96,2048]{1,0:T(8,128)(2,1)S(1)}, u32[]{:S(2)}, u32[]{:S(2)}) collective-permute-start(bf16[96,2048]{1,0:T(8,128)(2,1)S(1)} %add_convert_fusion.3), channel_id=1, source_target_pairs={{0,28},{1,29},{2,30},{3,31},{4,8},{5,9},{6,10},{7,11},{8,4},{9,5},... | collective-permute-start | bytes 1179656 | tf_op jit(solution)/shard_map/sum_z/ppermute | solution.py:26
  31.1 0.3 convolution_multiply_fusion.6
  31.3 0.0 collective-permute-done.55
  31.4 0.3 add_convert_fusion.6
  31.6 1.9 %collective-permute-start.56 = (bf16[96,2048]{1,0:T(8,128)(2,1)S(1)}, bf16[96,2048]{1,0:T(8,128)(2,1)S(1)}, u32[]{:S(2)}, u32[]{:S(2)}) collective-permute-start(bf16[96,2048]{1,0:T(8,128)(2,1)S(1)} %add_convert_fusion.6), channel_id=1, source_target_pairs={{0,4},{1,5},{2,6},{3,7},{4,0},{5,1},{6,2},{7,3},{8,12},{9,13},{10,... | collective-permute-start | bytes 1179656 | tf_op jit(solution)/shard_map/sum_z/ppermute | solution.py:26
  33.6 8.1 %collective-permute-done.60 = bf16[96,2048]{1,0:T(8,128)(2,1)S(1)} collective-permute-done((bf16[96,2048]{1,0:T(8,128)(2,1)S(1)}, bf16[96,2048]{1,0:T(8,128)(2,1)S(1)}, u32[]{:S(2)}, u32[]{:S(2)}) %collective-permute-start.60) | collective-permute-done | bytes 393248 | tf_op jit(solution)/shard_map/sum_z/ppermute | solution.py:26
  41.6 0.1 add_convert_fusion.2
  41.7 1.9 %collective-permute-start.61 = (bf16[96,2048]{1,0:T(8,128)(2,1)S(1)}, bf16[96,2048]{1,0:T(8,128)(2,1)S(1)}, u32[]{:S(2)}, u32[]{:S(2)}) collective-permute-start(bf16[96,2048]{1,0:T(8,128)(2,1)S(1)} %add_convert_fusion.2), channel_id=1, source_target_pairs={{0,4},{1,5},{2,6},{3,7},{4,0},{5,1},{6,2},{7,3},{8,12},{9,13},{10,... | collective-permute-start | bytes 1179656 | tf_op jit(solution)/shard_map/sum_z/ppermute | solution.py:26
  43.7 0.1 add_convert_fusion.5
  43.7 5.0 %collective-permute-start.57 = (bf16[96,2048]{1,0:T(8,128)(2,1)S(1)}, bf16[96,2048]{1,0:T(8,128)(2,1)S(1)}, u32[]{:S(2)}, u32[]{:S(2)}) collective-permute-start(bf16[96,2048]{1,0:T(8,128)(2,1)S(1)} %add_convert_fusion.5), channel_id=1, source_target_pairs={{0,28},{1,29},{2,30},{3,31},{4,8},{5,9},{6,10},{7,11},{8,4},{9,5},... | collective-permute-start | bytes 1179656 | tf_op jit(solution)/shard_map/sum_z/ppermute | solution.py:26
  48.8 3.6 %collective-permute-done.61 = bf16[96,2048]{1,0:T(8,128)(2,1)S(1)} collective-permute-done((bf16[96,2048]{1,0:T(8,128)(2,1)S(1)}, bf16[96,2048]{1,0:T(8,128)(2,1)S(1)}, u32[]{:S(2)}, u32[]{:S(2)}) %collective-permute-start.61) | collective-permute-done | bytes 393248 | tf_op jit(solution)/shard_map/sum_z/ppermute | solution.py:26
  52.4 0.1 add_convert_fusion.1
  52.4 0.0 copy-start.4
  52.5 0.0 copy-start.2
  52.5 4.0 %collective-permute-start.62 = (bf16[96,2048]{1,0:T(8,128)(2,1)S(1)}, bf16[96,2048]{1,0:T(8,128)(2,1)S(1)}, u32[]{:S(2)}, u32[]{:S(2)}) collective-permute-start(bf16[96,2048]{1,0:T(8,128)(2,1)S(1)} %add_convert_fusion.1), channel_id=1, source_target_pairs={{0,28},{1,29},{2,30},{3,31},{4,8},{5,9},{6,10},{7,11},{8,4},{9,5},... | collective-permute-start | bytes 1179656 | tf_op jit(solution)/shard_map/sum_z/ppermute | solution.py:26
  56.4 0.0 collective-permute-done.57
  56.4 0.1 add_convert_fusion.4
  56.5 2.5 %collective-permute-start.58 = (bf16[96,2048]{1,0:T(8,128)(2,1)S(1)}, bf16[96,2048]{1,0:T(8,128)(2,1)S(1)}, u32[]{:S(2)}, u32[]{:S(2)}) collective-permute-start(bf16[96,2048]{1,0:T(8,128)(2,1)S(1)} %add_convert_fusion.4), channel_id=1, source_target_pairs={{0,4},{1,5},{2,6},{3,7},{4,0},{5,1},{6,2},{7,3},{8,12},{9,13},{10,... | collective-permute-start | bytes 1179656 | tf_op jit(solution)/shard_map/sum_z/ppermute | solution.py:26
  59.1 0.3 convolution_multiply_fusion.7
  59.3 4.7 %collective-permute-done.62 = bf16[96,2048]{1,0:T(8,128)(2,1)S(1)} collective-permute-done((bf16[96,2048]{1,0:T(8,128)(2,1)S(1)}, bf16[96,2048]{1,0:T(8,128)(2,1)S(1)}, u32[]{:S(2)}, u32[]{:S(2)}) %collective-permute-start.62) | collective-permute-done | bytes 393248 | tf_op jit(solution)/shard_map/sum_z/ppermute | solution.py:26
  64.0 3.2 %collective-permute-done.58 = bf16[96,2048]{1,0:T(8,128)(2,1)S(1)} collective-permute-done((bf16[96,2048]{1,0:T(8,128)(2,1)S(1)}, bf16[96,2048]{1,0:T(8,128)(2,1)S(1)}, u32[]{:S(2)}, u32[]{:S(2)}) %collective-permute-start.58) | collective-permute-done | bytes 393248 | tf_op jit(solution)/shard_map/sum_z/ppermute | solution.py:26
  67.3 0.9 add_convert_fusion
  68.1 5.1 %all-to-all-start.5 = ((bf16[4,24,2048]{2,1,0:T(8,128)(2,1)}), bf16[4,24,2048]{2,1,0:T(8,128)(2,1)S(1)}, u32[]{:S(2)}, u32[]{:S(2)}) async-start(bf16[4,24,2048]{2,1,0:T(8,128)(2,1)} %bitcast.31), calls=%async_computation.5 | async-start | bytes 786432 | tf_op jit(solution)/shard_map/sum_x/all_to_all | solution.py:32
  74.0 0.1 dynamic-slice_bitcast_fusion
  74.1 0.2 convert_reduce_fusion.1
  74.3 6.4 %all-to-all-done.5 = bf16[4,24,2048]{2,1,0:T(8,128)(2,1)S(1)} async-done(((bf16[4,24,2048]{2,1,0:T(8,128)(2,1)}), bf16[4,24,2048]{2,1,0:T(8,128)(2,1)S(1)}, u32[]{:S(2)}, u32[]{:S(2)}) %all-to-all-start.5) | async-done | bytes 393248 | tf_op jit(solution)/shard_map/sum_x/all_to_all | solution.py:32
  80.7 1.6 fusion.2
  82.3 82.7 %conditional.1 = (bf16[128,2048]{1,0:T(8,128)(2,1)}, bf16[128,2048]{1,0:T(8,128)(2,1)}, bf16[1,768,128]{2,1,0:T(8,128)(2,1)S(1)}) conditional(s32[]{:T(128)} %clamp.3, (bf16[24,2048]{1,0:T(8,128)(2,1)S(1)}, bf16[128,2048]{1,0:T(8,128)(2,1)S(1)}, bf16[32,24,128]{2,1,0:T(8,128)(2,1)S(1)}, ...), branch_computations={%region_2.3_spmd, %region_3.4_spmd, %region_4.5_spmd, %region_5.6_... | conditional | flops 805306368 | bytes 24871408 | solution.py:262
  82.3 11.3 %all_to_all.39 = bf16[4,24,2048]{2,1,0:T(8,128)(2,1)S(1)} all-to-all(bf16[4,24,2048]{2,1,0:T(8,128)(2,1)S(1)} %tile.10), channel_id=1, replica_groups={{0,1,2,3},{4,5,6,7},{8,9,10,11},{12,13,14,15},{16,17,18,19},{20,21,22,2..., dimensions={0} | all-to-all | bytes 786432 | tf_op jit(solution)/shard_map/cond/branch_0_fun/gather_x/all_to_all | solution.py:32
  93.6 2.2 %collective-permute-start.3 = (bf16[96,2048]{1,0:T(8,128)(2,1)S(1)}, bf16[96,2048]{1,0:T(8,128)(2,1)S(1)}, u32[]{:S(2)}, u32[]{:S(2)}) collective-permute-start(bf16[96,2048]{1,0:T(8,128)(2,1)S(1)} %bitcast.78), channel_id=1, source_target_pairs={{0,4},{1,5},{2,6},{3,7},{4,0},{5,1},{6,2},{7,3},{8,12},{9,13},{10,... | collective-permute-start | bytes 1179656 | tf_op jit(solution)/shard_map/cond/branch_0_fun/gather_z/ppermute | solution.py:26
  95.8 2.5 %collective-permute-start = (bf16[96,2048]{1,0:T(8,128)(2,1)S(1)}, bf16[96,2048]{1,0:T(8,128)(2,1)S(1)}, u32[]{:S(2)}, u32[]{:S(2)}) collective-permute-start(bf16[96,2048]{1,0:T(8,128)(2,1)S(1)} %bitcast.79), channel_id=1, source_target_pairs={{0,28},{1,29},{2,30},{3,31},{4,8},{5,9},{6,10},{7,11},{8,4},{9,5},... | collective-permute-start | bytes 1179656 | tf_op jit(solution)/shard_map/cond/branch_0_fun/gather_z/ppermute | solution.py:26
  98.3 1.9 %collective-permute-start.2 = (bf16[128,2048]{1,0:T(8,128)(2,1)S(1)}, bf16[128,2048]{1,0:T(8,128)(2,1)S(1)}, u32[]{:S(2)}, u32[]{:S(2)}) collective-permute-start(bf16[128,2048]{1,0:T(8,128)(2,1)S(1)} %get-tuple-element.61.refs_0_.refs_9_), channel_id=1, source_target_pairs={{0,32},{32,64},{64,96},{96,128},{128,160},{160,192},{192,224},{224... | collective-permute-start | bytes 1572872 | tf_op jit(solution)/shard_map/cond/branch_0_fun/early_partner/ppermute | solution.py:37
  100.2 3.0 %collective-permute-done.3.refs_1_ = bf16[96,2048]{1,0:T(8,128)(2,1)S(1)} collective-permute-done((bf16[96,2048]{1,0:T(8,128)(2,1)S(1)}, bf16[96,2048]{1,0:T(8,128)(2,1)S(1)}, u32[]{:S(2)}, u32[]{:S(2)}) %collective-permute-start.3) | collective-permute-done | bytes 393248 | tf_op jit(solution)/shard_map/cond/branch_0_fun/gather_z/ppermute | solution.py:26
  103.3 2.2 %collective-permute-start.4 = (bf16[96,2048]{1,0:T(8,128)(2,1)S(1)}, bf16[96,2048]{1,0:T(8,128)(2,1)S(1)}, u32[]{:S(2)}, u32[]{:S(2)}) collective-permute-start(bf16[96,2048]{1,0:T(8,128)(2,1)S(1)} %collective-permute-done.3.refs_1_), channel_id=1, source_target_pairs={{0,28},{1,29},{2,30},{3,31},{4,8},{5,9},{6,10},{7,11},{8,4},{9,5},... | collective-permute-start | bytes 1179656 | tf_op jit(solution)/shard_map/cond/branch_0_fun/gather_z/ppermute | solution.py:26
  105.5 1.2 collective-permute-done.refs_4_.refs_7_
  106.7 2.4 %collective-permute-start.1 = (bf16[96,2048]{1,0:T(8,128)(2,1)S(1)}, bf16[96,2048]{1,0:T(8,128)(2,1)S(1)}, u32[]{:S(2)}, u32[]{:S(2)}) collective-permute-start(bf16[96,2048]{1,0:T(8,128)(2,1)S(1)} %collective-permute-done.refs_4_.refs_7_), channel_id=1, source_target_pairs={{0,4},{1,5},{2,6},{3,7},{4,0},{5,1},{6,2},{7,3},{8,12},{9,13},{10,... | collective-permute-start | bytes 1179656 | tf_op jit(solution)/shard_map/cond/branch_0_fun/gather_z/ppermute | solution.py:26
  109.1 8.9 %collective-permute-done.4.refs_3_.refs_6_ = bf16[96,2048]{1,0:T(8,128)(2,1)S(1)} collective-permute-done((bf16[96,2048]{1,0:T(8,128)(2,1)S(1)}, bf16[96,2048]{1,0:T(8,128)(2,1)S(1)}, u32[]{:S(2)}, u32[]{:S(2)}) %collective-permute-start.4) | collective-permute-done | bytes 393248 | tf_op jit(solution)/shard_map/cond/branch_0_fun/gather_z/ppermute | solution.py:26
  118.0 1.9 %collective-permute-start.5 = (bf16[96,2048]{1,0:T(8,128)(2,1)S(1)}, bf16[96,2048]{1,0:T(8,128)(2,1)S(1)}, u32[]{:S(2)}, u32[]{:S(2)}) collective-permute-start(bf16[96,2048]{1,0:T(8,128)(2,1)S(1)} %collective-permute-done.4.refs_3_.refs_6_), channel_id=1, source_target_pairs={{0,4},{1,5},{2,6},{3,7},{4,0},{5,1},{6,2},{7,3},{8,12},{9,13},{10,... | collective-permute-start | bytes 1179656 | tf_op jit(solution)/shard_map/cond/branch_0_fun/gather_z/ppermute | solution.py:26
  119.9 0.5 collective-permute-done.2.refs_1_
  120.4 4.6 %collective-permute-start.7 = (bf16[96,2048]{1,0:T(8,128)(2,1)S(1)}, bf16[96,2048]{1,0:T(8,128)(2,1)S(1)}, u32[]{:S(2)}, u32[]{:S(2)}) collective-permute-start(bf16[96,2048]{1,0:T(8,128)(2,1)S(1)} %collective-permute-done.1.refs_2_), channel_id=1, source_target_pairs={{0,28},{1,29},{2,30},{3,31},{4,8},{5,9},{6,10},{7,11},{8,4},{9,5},... | collective-permute-start | bytes 1179656 | tf_op jit(solution)/shard_map/cond/branch_0_fun/gather_z/ppermute | solution.py:26
  125.0 0.6 near.5.refs_3_
  125.6 5.8 %collective-permute-done.5.refs_0_.refs_3_ = bf16[96,2048]{1,0:T(8,128)(2,1)S(1)} collective-permute-done((bf16[96,2048]{1,0:T(8,128)(2,1)S(1)}, bf16[96,2048]{1,0:T(8,128)(2,1)S(1)}, u32[]{:S(2)}, u32[]{:S(2)}) %collective-permute-start.5) | collective-permute-done | bytes 393248 | tf_op jit(solution)/shard_map/cond/branch_0_fun/gather_z/ppermute | solution.py:26
  131.4 1.9 %collective-permute-start.6 = (bf16[96,1024]{1,0:T(8,128)(2,1)S(1)}, bf16[96,1024]{1,0:T(8,128)(2,1)S(1)}, u32[]{:S(2)}, u32[]{:S(2)}) collective-permute-start(bf16[96,1024]{1,0:T(8,128)(2,1)S(1)} %slice.56), channel_id=1, source_target_pairs={{0,28},{1,29},{2,30},{3,31},{4,8},{5,9},{6,10},{7,11},{8,4},{9,5},... | collective-permute-start | bytes 589832 | tf_op jit(solution)/shard_map/cond/branch_0_fun/gather_z/ppermute | solution.py:26
  133.3 1.3 collective-permute-done.7.refs_2_.refs_5_
  134.7 2.3 %collective-permute-start.8 = (bf16[96,1024]{1,0:T(8,128)(2,1)S(1)}, bf16[96,1024]{1,0:T(8,128)(2,1)S(1)}, u32[]{:S(2)}, u32[]{:S(2)}) collective-permute-start(bf16[96,1024]{1,0:T(8,128)(2,1)S(1)} %slice.57), channel_id=1, source_target_pairs={{0,4},{1,5},{2,6},{3,7},{4,0},{5,1},{6,2},{7,3},{8,12},{9,13},{10,... | collective-permute-start | bytes 589832 | tf_op jit(solution)/shard_map/cond/branch_0_fun/gather_z/ppermute | solution.py:26
  137.0 4.0 %collective-permute-done.6.refs_1_.refs_4_ = bf16[96,1024]{1,0:T(8,128)(2,1)S(1)} collective-permute-done((bf16[96,1024]{1,0:T(8,128)(2,1)S(1)}, bf16[96,1024]{1,0:T(8,128)(2,1)S(1)}, u32[]{:S(2)}, u32[]{:S(2)}) %collective-permute-start.6) | collective-permute-done | bytes 196640 | tf_op jit(solution)/shard_map/cond/branch_0_fun/gather_z/ppermute | solution.py:26
  141.0 0.3 moment.10.refs_2_
  141.3 1.9 %collective-permute-start.9 = (bf16[128,1024]{1,0:T(8,128)(2,1)S(1)}, bf16[128,1024]{1,0:T(8,128)(2,1)S(1)}, u32[]{:S(2)}, u32[]{:S(2)}) collective-permute-start(bf16[128,1024]{1,0:T(8,128)(2,1)S(1)} %moment.10.refs_2_), channel_id=1, source_target_pairs={{0,32},{32,64},{64,96},{96,128},{128,160},{160,192},{192,224},{224... | collective-permute-start | bytes 786440 | tf_op jit(solution)/shard_map/cond/branch_0_fun/partner/ppermute | solution.py:37
  143.2 0.3 moment.11.refs_3_
  143.6 3.5 %collective-permute-start.10 = (bf16[128,1024]{1,0:T(8,128)(2,1)S(1)}, bf16[128,1024]{1,0:T(8,128)(2,1)S(1)}, u32[]{:S(2)}, u32[]{:S(2)}) collective-permute-start(bf16[128,1024]{1,0:T(8,128)(2,1)S(1)} %moment.11.refs_3_), channel_id=1, source_target_pairs={{0,32},{32,64},{64,96},{96,128},{128,160},{160,192},{192,224},{224... | collective-permute-start | bytes 786440 | tf_op jit(solution)/shard_map/cond/branch_0_fun/partner/ppermute | solution.py:37
  147.1 1.5 back.5
  148.6 12.0 %collective-permute-done.9.refs_4_ = bf16[128,1024]{1,0:T(8,128)(2,1)S(1)} collective-permute-done((bf16[128,1024]{1,0:T(8,128)(2,1)S(1)}, bf16[128,1024]{1,0:T(8,128)(2,1)S(1)}, u32[]{:S(2)}, u32[]{:S(2)}) %collective-permute-start.9) | collective-permute-done | bytes 262176 | tf_op jit(solution)/shard_map/cond/branch_0_fun/partner/ppermute | solution.py:37
  160.6 2.8 %collective-permute-done.10.refs_5_ = bf16[128,1024]{1,0:T(8,128)(2,1)S(1)} collective-permute-done((bf16[128,1024]{1,0:T(8,128)(2,1)S(1)}, bf16[128,1024]{1,0:T(8,128)(2,1)S(1)}, u32[]{:S(2)}, u32[]{:S(2)}) %collective-permute-start.10) | collective-permute-done | bytes 262176 | tf_op jit(solution)/shard_map/cond/branch_0_fun/partner/ppermute | solution.py:37
  163.4 1.5 mix.5
  164.9 0.7 copy-done.3
  (18 shorter events, 0.2 us)
Async XLA Ops:
  0.6 0.9 copy-start
  1.6 22.0 %copy-start.1 = (bf16[1,128,2048]{2,1,0:T(8,128)(2,1)S(1)}, bf16[1,128,2048]{2,1,0:T(8,128)(2,1)}, u32[]{:S(2)}) copy-start(bf16[1,128,2048]{2,1,0:T(8,128)(2,1)} %param.12) | copy-start | bytes 1572868
  3.0 28.3 %collective-permute-start.55 = (bf16[96,1024]{1,0:T(8,128)(2,1)S(1)}, bf16[96,1024]{1,0:T(8,128)(2,1)S(1)}, u32[]{:S(2)}, u32[]{:S(2)}) collective-permute-start(bf16[96,1024]{1,0:T(8,128)(2,1)S(1)} %get-tuple-element.126), channel_id=1, source_target_pairs={{0,28},{1,29},{2,30},{3,31},{4,8},{5,9},{6,10},{7,11},{8,4},{9,5},... | collective-permute-start | bytes 589832 | tf_op jit(solution)/shard_map/sum_z/ppermute | solution.py:26
  20.3 8.3 %collective-permute-start.59 = (bf16[96,1024]{1,0:T(8,128)(2,1)S(1)}, bf16[96,1024]{1,0:T(8,128)(2,1)S(1)}, u32[]{:S(2)}, u32[]{:S(2)}) collective-permute-start(bf16[96,1024]{1,0:T(8,128)(2,1)S(1)} %get-tuple-element.127), channel_id=1, source_target_pairs={{0,4},{1,5},{2,6},{3,7},{4,0},{5,1},{6,2},{7,3},{8,12},{9,13},{10,... | collective-permute-start | bytes 589832 | tf_op jit(solution)/shard_map/sum_z/ppermute | solution.py:26
  28.9 12.8 %collective-permute-start.60 = (bf16[96,2048]{1,0:T(8,128)(2,1)S(1)}, bf16[96,2048]{1,0:T(8,128)(2,1)S(1)}, u32[]{:S(2)}, u32[]{:S(2)}) collective-permute-start(bf16[96,2048]{1,0:T(8,128)(2,1)S(1)} %add_convert_fusion.3), channel_id=1, source_target_pairs={{0,28},{1,29},{2,30},{3,31},{4,8},{5,9},{6,10},{7,11},{8,4},{9,5},... | collective-permute-start | bytes 1179656 | tf_op jit(solution)/shard_map/sum_z/ppermute | solution.py:26
  31.6 12.0 %collective-permute-start.56 = (bf16[96,2048]{1,0:T(8,128)(2,1)S(1)}, bf16[96,2048]{1,0:T(8,128)(2,1)S(1)}, u32[]{:S(2)}, u32[]{:S(2)}) collective-permute-start(bf16[96,2048]{1,0:T(8,128)(2,1)S(1)} %add_convert_fusion.6), channel_id=1, source_target_pairs={{0,4},{1,5},{2,6},{3,7},{4,0},{5,1},{6,2},{7,3},{8,12},{9,13},{10,... | collective-permute-start | bytes 1179656 | tf_op jit(solution)/shard_map/sum_z/ppermute | solution.py:26
  41.7 10.6 %collective-permute-start.61 = (bf16[96,2048]{1,0:T(8,128)(2,1)S(1)}, bf16[96,2048]{1,0:T(8,128)(2,1)S(1)}, u32[]{:S(2)}, u32[]{:S(2)}) collective-permute-start(bf16[96,2048]{1,0:T(8,128)(2,1)S(1)} %add_convert_fusion.2), channel_id=1, source_target_pairs={{0,4},{1,5},{2,6},{3,7},{4,0},{5,1},{6,2},{7,3},{8,12},{9,13},{10,... | collective-permute-start | bytes 1179656 | tf_op jit(solution)/shard_map/sum_z/ppermute | solution.py:26
  43.7 12.7 %collective-permute-start.57 = (bf16[96,2048]{1,0:T(8,128)(2,1)S(1)}, bf16[96,2048]{1,0:T(8,128)(2,1)S(1)}, u32[]{:S(2)}, u32[]{:S(2)}) collective-permute-start(bf16[96,2048]{1,0:T(8,128)(2,1)S(1)} %add_convert_fusion.5), channel_id=1, source_target_pairs={{0,28},{1,29},{2,30},{3,31},{4,8},{5,9},{6,10},{7,11},{8,4},{9,5},... | collective-permute-start | bytes 1179656 | tf_op jit(solution)/shard_map/sum_z/ppermute | solution.py:26
  52.4 21.5 %copy-start.4 = (s32[1,768]{1,0:T(1,128)S(1)}, s32[1,768]{1,0:T(1,128)}, u32[]{:S(2)}) copy-start(s32[1,768]{1,0:T(1,128)} %param.15) | copy-start | bytes 9220
  52.5 29.8 %copy-start.2 = (bf16[1,128,2048]{2,1,0:T(8,128)(2,1)S(1)}, bf16[1,128,2048]{2,1,0:T(8,128)(2,1)}, u32[]{:S(2)}) copy-start(bf16[1,128,2048]{2,1,0:T(8,128)(2,1)} %param.13) | copy-start | bytes 1572868
  52.5 11.6 %collective-permute-start.62 = (bf16[96,2048]{1,0:T(8,128)(2,1)S(1)}, bf16[96,2048]{1,0:T(8,128)(2,1)S(1)}, u32[]{:S(2)}, u32[]{:S(2)}) collective-permute-start(bf16[96,2048]{1,0:T(8,128)(2,1)S(1)} %add_convert_fusion.1), channel_id=1, source_target_pairs={{0,28},{1,29},{2,30},{3,31},{4,8},{5,9},{6,10},{7,11},{8,4},{9,5},... | collective-permute-start | bytes 1179656 | tf_op jit(solution)/shard_map/sum_z/ppermute | solution.py:26
  56.5 10.7 %collective-permute-start.58 = (bf16[96,2048]{1,0:T(8,128)(2,1)S(1)}, bf16[96,2048]{1,0:T(8,128)(2,1)S(1)}, u32[]{:S(2)}, u32[]{:S(2)}) collective-permute-start(bf16[96,2048]{1,0:T(8,128)(2,1)S(1)} %add_convert_fusion.4), channel_id=1, source_target_pairs={{0,4},{1,5},{2,6},{3,7},{4,0},{5,1},{6,2},{7,3},{8,12},{9,13},{10,... | collective-permute-start | bytes 1179656 | tf_op jit(solution)/shard_map/sum_z/ppermute | solution.py:26
  68.1 12.6 %all-to-all-start.5 = ((bf16[4,24,2048]{2,1,0:T(8,128)(2,1)}), bf16[4,24,2048]{2,1,0:T(8,128)(2,1)S(1)}, u32[]{:S(2)}, u32[]{:S(2)}) async-start(bf16[4,24,2048]{2,1,0:T(8,128)(2,1)} %bitcast.31), calls=%async_computation.5 | async-start | bytes 786432 | tf_op jit(solution)/shard_map/sum_x/all_to_all | solution.py:32
  93.6 9.7 %collective-permute-start.3 = (bf16[96,2048]{1,0:T(8,128)(2,1)S(1)}, bf16[96,2048]{1,0:T(8,128)(2,1)S(1)}, u32[]{:S(2)}, u32[]{:S(2)}) collective-permute-start(bf16[96,2048]{1,0:T(8,128)(2,1)S(1)} %bitcast.78), channel_id=1, source_target_pairs={{0,4},{1,5},{2,6},{3,7},{4,0},{5,1},{6,2},{7,3},{8,12},{9,13},{10,... | collective-permute-start | bytes 1179656 | tf_op jit(solution)/shard_map/cond/branch_0_fun/gather_z/ppermute | solution.py:26
  95.8 10.9 %collective-permute-start = (bf16[96,2048]{1,0:T(8,128)(2,1)S(1)}, bf16[96,2048]{1,0:T(8,128)(2,1)S(1)}, u32[]{:S(2)}, u32[]{:S(2)}) collective-permute-start(bf16[96,2048]{1,0:T(8,128)(2,1)S(1)} %bitcast.79), channel_id=1, source_target_pairs={{0,28},{1,29},{2,30},{3,31},{4,8},{5,9},{6,10},{7,11},{8,4},{9,5},... | collective-permute-start | bytes 1179656 | tf_op jit(solution)/shard_map/cond/branch_0_fun/gather_z/ppermute | solution.py:26
  98.3 22.1 %collective-permute-start.2 = (bf16[128,2048]{1,0:T(8,128)(2,1)S(1)}, bf16[128,2048]{1,0:T(8,128)(2,1)S(1)}, u32[]{:S(2)}, u32[]{:S(2)}) collective-permute-start(bf16[128,2048]{1,0:T(8,128)(2,1)S(1)} %get-tuple-element.61.refs_0_.refs_9_), channel_id=1, source_target_pairs={{0,32},{32,64},{64,96},{96,128},{128,160},{160,192},{192,224},{224... | collective-permute-start | bytes 1572872 | tf_op jit(solution)/shard_map/cond/branch_0_fun/early_partner/ppermute | solution.py:37
  103.3 14.8 %collective-permute-start.4 = (bf16[96,2048]{1,0:T(8,128)(2,1)S(1)}, bf16[96,2048]{1,0:T(8,128)(2,1)S(1)}, u32[]{:S(2)}, u32[]{:S(2)}) collective-permute-start(bf16[96,2048]{1,0:T(8,128)(2,1)S(1)} %collective-permute-done.3.refs_1_), channel_id=1, source_target_pairs={{0,28},{1,29},{2,30},{3,31},{4,8},{5,9},{6,10},{7,11},{8,4},{9,5},... | collective-permute-start | bytes 1179656 | tf_op jit(solution)/shard_map/cond/branch_0_fun/gather_z/ppermute | solution.py:26
  106.7 13.7 %collective-permute-start.1 = (bf16[96,2048]{1,0:T(8,128)(2,1)S(1)}, bf16[96,2048]{1,0:T(8,128)(2,1)S(1)}, u32[]{:S(2)}, u32[]{:S(2)}) collective-permute-start(bf16[96,2048]{1,0:T(8,128)(2,1)S(1)} %collective-permute-done.refs_4_.refs_7_), channel_id=1, source_target_pairs={{0,4},{1,5},{2,6},{3,7},{4,0},{5,1},{6,2},{7,3},{8,12},{9,13},{10,... | collective-permute-start | bytes 1179656 | tf_op jit(solution)/shard_map/cond/branch_0_fun/gather_z/ppermute | solution.py:26
  118.0 13.3 %collective-permute-start.5 = (bf16[96,2048]{1,0:T(8,128)(2,1)S(1)}, bf16[96,2048]{1,0:T(8,128)(2,1)S(1)}, u32[]{:S(2)}, u32[]{:S(2)}) collective-permute-start(bf16[96,2048]{1,0:T(8,128)(2,1)S(1)} %collective-permute-done.4.refs_3_.refs_6_), channel_id=1, source_target_pairs={{0,4},{1,5},{2,6},{3,7},{4,0},{5,1},{6,2},{7,3},{8,12},{9,13},{10,... | collective-permute-start | bytes 1179656 | tf_op jit(solution)/shard_map/cond/branch_0_fun/gather_z/ppermute | solution.py:26
  120.4 14.2 %collective-permute-start.7 = (bf16[96,2048]{1,0:T(8,128)(2,1)S(1)}, bf16[96,2048]{1,0:T(8,128)(2,1)S(1)}, u32[]{:S(2)}, u32[]{:S(2)}) collective-permute-start(bf16[96,2048]{1,0:T(8,128)(2,1)S(1)} %collective-permute-done.1.refs_2_), channel_id=1, source_target_pairs={{0,28},{1,29},{2,30},{3,31},{4,8},{5,9},{6,10},{7,11},{8,4},{9,5},... | collective-permute-start | bytes 1179656 | tf_op jit(solution)/shard_map/cond/branch_0_fun/gather_z/ppermute | solution.py:26
  131.4 9.6 %collective-permute-start.6 = (bf16[96,1024]{1,0:T(8,128)(2,1)S(1)}, bf16[96,1024]{1,0:T(8,128)(2,1)S(1)}, u32[]{:S(2)}, u32[]{:S(2)}) collective-permute-start(bf16[96,1024]{1,0:T(8,128)(2,1)S(1)} %slice.56), channel_id=1, source_target_pairs={{0,28},{1,29},{2,30},{3,31},{4,8},{5,9},{6,10},{7,11},{8,4},{9,5},... | collective-permute-start | bytes 589832 | tf_op jit(solution)/shard_map/cond/branch_0_fun/gather_z/ppermute | solution.py:26
  134.7 8.6 %collective-permute-start.8 = (bf16[96,1024]{1,0:T(8,128)(2,1)S(1)}, bf16[96,1024]{1,0:T(8,128)(2,1)S(1)}, u32[]{:S(2)}, u32[]{:S(2)}) collective-permute-start(bf16[96,1024]{1,0:T(8,128)(2,1)S(1)} %slice.57), channel_id=1, source_target_pairs={{0,4},{1,5},{2,6},{3,7},{4,0},{5,1},{6,2},{7,3},{8,12},{9,13},{10,... | collective-permute-start | bytes 589832 | tf_op jit(solution)/shard_map/cond/branch_0_fun/gather_z/ppermute | solution.py:26
  141.3 19.3 %collective-permute-start.9 = (bf16[128,1024]{1,0:T(8,128)(2,1)S(1)}, bf16[128,1024]{1,0:T(8,128)(2,1)S(1)}, u32[]{:S(2)}, u32[]{:S(2)}) collective-permute-start(bf16[128,1024]{1,0:T(8,128)(2,1)S(1)} %moment.10.refs_2_), channel_id=1, source_target_pairs={{0,32},{32,64},{64,96},{96,128},{128,160},{160,192},{192,224},{224... | collective-permute-start | bytes 786440 | tf_op jit(solution)/shard_map/cond/branch_0_fun/partner/ppermute | solution.py:37
  143.6 19.9 %collective-permute-start.10 = (bf16[128,1024]{1,0:T(8,128)(2,1)S(1)}, bf16[128,1024]{1,0:T(8,128)(2,1)S(1)}, u32[]{:S(2)}, u32[]{:S(2)}) collective-permute-start(bf16[128,1024]{1,0:T(8,128)(2,1)S(1)} %moment.11.refs_3_), channel_id=1, source_target_pairs={{0,32},{32,64},{64,96},{96,128},{128,160},{160,192},{192,224},{224... | collective-permute-start | bytes 786440 | tf_op jit(solution)/shard_map/cond/branch_0_fun/partner/ppermute | solution.py:37
  164.9 0.7 copy-start.3
